TPU v7x, 32 devices: a whole 2x2x4 slice. The times are simulated.
32 devices in a mesh: win: 8 (over z, x), fsdp: 4 (over y, core).
Axes of the slice: x: 2, y: 2, z: 4, core: 2. Of those that a mesh axis runs over, the one named last changes fastest.
Arguments:
- tokens: bfloat16 [4, 56, 14, 1344], P('fsdp', 'win'), may hold values from -6 to 6
- cotangent: bfloat16 [4, 56, 14, 1344], P('fsdp', 'win'), may hold values from -6 to 6
- crop_ids: int32 [4, 56], P('fsdp'), may hold values from 0 to 1, never falling along the last dimension, each value on 1 to 35 neighbouring positions
- params: float32 [2, 124928], P(None, 'fsdp'), may hold values from -5 to 5
- first_moment: float32 [2, 124928], P(None, 'fsdp'), may hold values from -1 to 1
- second_moment: float32 [2, 124928], P(None, 'fsdp'), may hold values from 0 to 1
Outputs:
- block_out: bfloat16 [4, 56, 14, 1344], P('fsdp', 'win')
- input_grad: bfloat16 [4, 56, 14, 1344], P('fsdp', 'win')
- grad_norm: float32 [], replicated
- new_params: float32 [2, 124928], P(None, 'fsdp')
- new_first: float32 [2, 124928], P(None, 'fsdp')
- new_second: float32 [2, 124928], P(None, 'fsdp')
- params_copy: bfloat16 [2, 124928], P(None, 'fsdp')
Inputs may be any that keep to these rules, and one draw needn't show every extreme that they name: `crop_ids`: each row numbers 2 crops along the first dimension: 0 at the start, never falling, rising by one at each crop's end, each crop 1 to 35 slices long.
All inputs are finite; a program needn't handle non-finite values.
Results may differ from a plain program's by a relative error of at most 0.019.
Values may be sent and summed in bfloat16 or wider, within the bound.
A program may use at most 256 MiB of HBM per device.

v0:
```python
import math

import jax
import jax.numpy as jnp
from jax import lax
from jax.sharding import PartitionSpec as P

C = 96
HEADS = 6
HEAD = 16
HID = 384
WS = 7
SHIFT = 3
TABLE = 2197
SY = 14
SZ = 14
BPAD = 124928
STEP = 5


EPS_NORM = 1e-05
CLIP_LIMIT = 1.0
LEARN_RATE = 0.4
BETA_FIRST = 0.9
BETA_SECOND = 0.999
WEIGHT_DECAY = 0.05
EPS_ADAM = 1e-08
MASK_FILL = -1e30


def shifted_2(shard, axis, by):
    size = lax.axis_size(axis)
    return lax.ppermute(shard, axis, [(i, (i + by) % size) for i in range(size)])


def piece_sizes():
    return [C * 3 * C, C * C, C * HID, HID * C, TABLE * HEADS, C, C, C, C, C, C, C, HID, C]


def split_block(flat_row):
    shapes = [
        (C, 3 * C),
        (C, C),
        (C, HID),
        (HID, C),
        (TABLE, HEADS),
        (C,),
        (C,),
        (C,),
        (C,),
        (C,),
        (C,),
        (C,),
        (HID,),
        (C,),
    ]
    pieces = []
    offset = 0
    for extent, shape_one in zip(piece_sizes(), shapes):
        pieces.append(flat_row[offset : offset + extent].reshape(shape_one))
        offset = offset + extent
    return pieces


def pack_block(grads_list):
    flat_row = jnp.concatenate([member.reshape(-1) for member in grads_list])
    return jnp.pad(flat_row, (0, BPAD - flat_row.shape[0]))


def relative_index():
    spots_all = jnp.arange(WS**3)
    coord_a = spots_all // (WS * WS)
    coord_b = spots_all // WS % WS
    coord_c = spots_all % WS
    table_span = 2 * WS - 1

    def differ(coord_one):
        return coord_one[:, None] - coord_one[None, :] + WS - 1

    return (differ(coord_a) * table_span + differ(coord_b)) * table_span + differ(coord_c)


def region_labels(extent):
    spots_all = jnp.arange(extent)
    return (spots_all >= extent - WS).astype(jnp.int32) + (spots_all >= extent - SHIFT).astype(
        jnp.int32
    )


def to_windows(values):
    extent_x, extent_y, extent_z = values.shape[:3]
    trailing = values.shape[3:]
    blocked = values.reshape(
        (extent_x // WS, WS, extent_y // WS, WS, extent_z // WS, WS) + trailing
    )
    axes_order = (0, 2, 4, 1, 3, 5) + tuple(range(6, 6 + len(trailing)))
    return blocked.transpose(axes_order).reshape((-1, WS**3) + trailing)


def from_windows(windows, extent_x, extent_y, extent_z):
    trailing = windows.shape[2:]
    blocked = windows.reshape(
        (extent_x // WS, extent_y // WS, extent_z // WS, WS, WS, WS) + trailing
    )
    axes_order = (0, 3, 1, 4, 2, 5) + tuple(range(6, 6 + len(trailing)))
    return blocked.transpose(axes_order).reshape((extent_x, extent_y, extent_z) + trailing)


def layer_norm(values, gain_row, bias_row):
    centered = values - jnp.mean(values, axis=-1, keepdims=True)
    variance = jnp.mean(centered * centered, axis=-1, keepdims=True)
    return centered * lax.rsqrt(variance + EPS_NORM) * gain_row + bias_row


def gelu_exact(values):
    return jax.nn.gelu(values, approximate=False)


def gather_block(shard_row):
    whole = lax.all_gather(shard_row.astype(jnp.bfloat16), "fsdp", axis=0, tiled=True)
    return split_block(whole)


def masked_scores(queries, key_rows, block_labels, table_bias):
    scores = (
        HEAD ** (-0.5)
        * jnp.einsum("wqhd,wkhd->whqk", queries, key_rows, preferred_element_type=jnp.float32)
        + table_bias[None]
    )
    allowed = (block_labels[:, :, None] == block_labels[:, None, :])[:, None]
    return jnp.where(allowed, scores, MASK_FILL)


def attention_forward(qkv_wins, label_wins, table_bias):
    window_count = qkv_wins.shape[0]
    group_size = math.gcd(window_count, 2)
    stacked = qkv_wins.reshape(window_count // group_size, group_size, WS**3, 3, HEADS, HEAD)
    label_stack = label_wins.reshape(window_count // group_size, group_size, WS**3)

    def one_group(inputs):
        block_qkv, block_labels = inputs
        queries = block_qkv[:, :, 0]
        key_rows = block_qkv[:, :, 1]
        value_rows = block_qkv[:, :, 2]
        masked = masked_scores(queries, key_rows, block_labels, table_bias)
        highest = jnp.max(masked, axis=-1, keepdims=True)
        log_total = highest + jnp.log(jnp.sum(jnp.exp(masked - highest), axis=-1, keepdims=True))
        soft_weights = jnp.exp(masked - log_total).astype(jnp.bfloat16)
        attended = jnp.einsum(
            "whqk,wkhd->wqhd", soft_weights, value_rows, preferred_element_type=jnp.float32
        )
        return (attended.astype(jnp.bfloat16), log_total[..., 0])

    attended, log_totals = lax.map(one_group, (stacked, label_stack))
    return (attended.reshape(window_count, WS**3, C), log_totals)


def attention_backward(qkv_wins, label_wins, table_bias, log_totals, d_attended):
    window_count = qkv_wins.shape[0]
    group_size = math.gcd(window_count, 2)
    stacked = qkv_wins.reshape(window_count // group_size, group_size, WS**3, 3, HEADS, HEAD)
    label_stack = label_wins.reshape(window_count // group_size, group_size, WS**3)
    grad_stack = d_attended.reshape(window_count // group_size, group_size, WS**3, HEADS, HEAD)

    def one_group(table_total, inputs):
        block_qkv, block_labels, block_log, block_grad = inputs
        queries = block_qkv[:, :, 0]
        key_rows = block_qkv[:, :, 1]
        value_rows = block_qkv[:, :, 2]
        masked = masked_scores(queries, key_rows, block_labels, table_bias)
        soft_exact = jnp.exp(masked - block_log[..., None])
        d_soft = jnp.einsum(
            "wqhd,wkhd->whqk", block_grad, value_rows, preferred_element_type=jnp.float32
        )
        inner_sum = jnp.sum(d_soft * soft_exact, axis=-1, keepdims=True)
        d_scores = (soft_exact * (d_soft - inner_sum)).astype(jnp.bfloat16)
        d_values = jnp.einsum(
            "whqk,wqhd->wkhd",
            soft_exact.astype(jnp.bfloat16),
            block_grad,
            preferred_element_type=jnp.float32,
        )
        d_queries = HEAD ** (-0.5) * jnp.einsum(
            "whqk,wkhd->wqhd", d_scores, key_rows, preferred_element_type=jnp.float32
        )
        d_keys = HEAD ** (-0.5) * jnp.einsum(
            "whqk,wqhd->wkhd", d_scores, queries, preferred_element_type=jnp.float32
        )
        d_triple = jnp.stack([d_queries, d_keys, d_values], axis=2).astype(jnp.bfloat16)
        return (table_total + jnp.sum(d_scores.astype(jnp.float32), axis=0), d_triple)

    start_table = jnp.zeros((HEADS, WS**3, WS**3), jnp.float32)
    d_table_full, d_qkv = lax.scan(
        one_group, start_table, (stacked, label_stack, log_totals, grad_stack)
    )
    return (d_qkv.reshape(window_count, WS**3, 3 * C), d_table_full)


def block_forward(cell_values, labels, weights, rel_index, shifted):
    (
        w_qkv,
        w_proj,
        w_one,
        w_two,
        bias_table,
        gain_one,
        bias_one,
        bias_query,
        bias_value,
        bias_proj,
        gain_two,
        bias_two,
        bias_hidden,
        bias_out,
    ) = weights
    extent_x = cell_values.shape[0]
    normed, norm_one_pull = jax.vjp(
        layer_norm, cell_values, gain_one.astype(jnp.float32), bias_one.astype(jnp.float32)
    )
    normed = normed.astype(jnp.bfloat16)
    if shifted:
        halo_slab = shifted_2(normed[:SHIFT], "win", -1)
        region = jnp.concatenate([normed[SHIFT:], halo_slab], axis=0)
        region = jnp.roll(region, (-SHIFT, -SHIFT), axis=(1, 2))
    else:
        region = normed
    windows = to_windows(region)
    label_wins = to_windows(labels)
    bias_all = jnp.concatenate([bias_query, jnp.zeros_like(bias_query), bias_value]).astype(
        jnp.float32
    )
    qkv_flat = jnp.dot(windows.reshape(-1, C), w_qkv, preferred_element_type=jnp.float32) + bias_all
    qkv_wins = qkv_flat.astype(jnp.bfloat16).reshape(-1, WS**3, 3 * C)
    table_bias = jnp.take(bias_table, rel_index, axis=0).astype(jnp.float32)
    table_bias = table_bias.reshape(WS**3, WS**3, HEADS).transpose(2, 0, 1)
    attended_wins, log_totals = attention_forward(qkv_wins, label_wins, table_bias)
    attended = from_windows(attended_wins, extent_x, SY, SZ)
    if shifted:
        attended = jnp.roll(attended, (SHIFT, SHIFT), axis=(1, 2))
    branch = jnp.dot(
        attended.reshape(-1, C), w_proj, preferred_element_type=jnp.float32
    ) + bias_proj.astype(jnp.float32)
    branch = branch.astype(jnp.bfloat16).reshape(extent_x, SY, SZ, C)
    if shifted:
        incoming = shifted_2(branch[extent_x - SHIFT :], "win", 1)
        branch = jnp.concatenate([incoming, branch[: extent_x - SHIFT]], axis=0)
    middle = cell_values + branch.astype(jnp.float32)
    normed_two, norm_two_pull = jax.vjp(
        layer_norm, middle, gain_two.astype(jnp.float32), bias_two.astype(jnp.float32)
    )
    normed_two = normed_two.astype(jnp.bfloat16).reshape(-1, C)
    hidden = jnp.dot(normed_two, w_one, preferred_element_type=jnp.float32) + bias_hidden.astype(
        jnp.float32
    )
    active, gelu_pull = jax.vjp(gelu_exact, hidden)
    active = active.astype(jnp.bfloat16)
    result = jnp.dot(active, w_two, preferred_element_type=jnp.float32) + bias_out.astype(
        jnp.float32
    )
    output = middle + result.reshape(extent_x, SY, SZ, C)
    kept = (
        norm_one_pull,
        windows,
        label_wins,
        qkv_wins,
        table_bias,
        log_totals,
        attended,
        norm_two_pull,
        normed_two,
        gelu_pull,
        active,
    )
    return (output, kept)


def block_backward(d_output, kept, weights, rel_index, shifted):
    (
        w_qkv,
        w_proj,
        w_one,
        w_two,
        bias_table,
        gain_one,
        bias_one,
        bias_query,
        bias_value,
        bias_proj,
        gain_two,
        bias_two,
        bias_hidden,
        bias_out,
    ) = weights
    (
        norm_one_pull,
        windows,
        label_wins,
        qkv_wins,
        table_bias,
        log_totals,
        attended,
        norm_two_pull,
        normed_two,
        gelu_pull,
        active,
    ) = kept
    extent_x = d_output.shape[0]
    d_result = d_output.reshape(-1, C).astype(jnp.bfloat16)
    grad_bias_out = jnp.sum(d_result.astype(jnp.float32), axis=0)
    grad_w_two = jnp.dot(active.T, d_result, preferred_element_type=jnp.float32)
    d_active = jnp.dot(d_result, w_two.T, preferred_element_type=jnp.float32)
    d_hidden = gelu_pull(d_active)[0].astype(jnp.bfloat16)
    grad_bias_hidden = jnp.sum(d_hidden.astype(jnp.float32), axis=0)
    grad_w_one = jnp.dot(normed_two.T, d_hidden, preferred_element_type=jnp.float32)
    d_normed_two = jnp.dot(d_hidden, w_one.T, preferred_element_type=jnp.float32)
    d_middle_norm, grad_gain_two, grad_bias_two = norm_two_pull(
        d_normed_two.reshape(extent_x, SY, SZ, C)
    )
    d_middle = d_output + d_middle_norm
    d_branch = d_middle.astype(jnp.bfloat16)
    if shifted:
        returned = shifted_2(d_branch[:SHIFT], "win", -1)
        d_branch = jnp.concatenate([d_branch[SHIFT:], returned], axis=0)
    d_branch_flat = d_branch.reshape(-1, C)
    grad_bias_proj = jnp.sum(d_branch_flat.astype(jnp.float32), axis=0)
    grad_w_proj = jnp.dot(
        attended.reshape(-1, C).T, d_branch_flat, preferred_element_type=jnp.float32
    )
    d_attended = jnp.dot(d_branch_flat, w_proj.T, preferred_element_type=jnp.float32)
    d_attended = d_attended.astype(jnp.bfloat16).reshape(extent_x, SY, SZ, C)
    if shifted:
        d_attended = jnp.roll(d_attended, (-SHIFT, -SHIFT), axis=(1, 2))
    d_qkv, d_table_full = attention_backward(
        qkv_wins, label_wins, table_bias, log_totals, to_windows(d_attended)
    )
    d_qkv_flat = d_qkv.reshape(-1, 3 * C)
    grad_w_qkv = jnp.dot(windows.reshape(-1, C).T, d_qkv_flat, preferred_element_type=jnp.float32)
    column_sums = jnp.sum(d_qkv_flat.astype(jnp.float32), axis=0)
    grad_bias_query = column_sums[:C]
    grad_bias_value = column_sums[2 * C :]
    grad_table = jax.ops.segment_sum(
        d_table_full.transpose(1, 2, 0).reshape(-1, HEADS), rel_index, num_segments=TABLE
    )
    d_region = jnp.dot(d_qkv_flat, w_qkv.T, preferred_element_type=jnp.float32)
    d_region = from_windows(d_region.reshape(-1, WS**3, C), extent_x, SY, SZ)
    if shifted:
        d_region = jnp.roll(d_region, (SHIFT, SHIFT), axis=(1, 2)).astype(jnp.bfloat16)
        sent_back = shifted_2(d_region[extent_x - SHIFT :], "win", 1)
        d_normed = jnp.concatenate([sent_back, d_region[: extent_x - SHIFT]], axis=0).astype(
            jnp.float32
        )
    else:
        d_normed = d_region
    d_cells_norm, grad_gain_one, grad_bias_one = norm_one_pull(d_normed)
    d_cells = d_middle + d_cells_norm
    grads_list = [
        grad_w_qkv,
        grad_w_proj,
        grad_w_one,
        grad_w_two,
        grad_table,
        grad_gain_one,
        grad_bias_one,
        grad_bias_query,
        grad_bias_value,
        grad_bias_proj,
        grad_gain_two,
        grad_bias_two,
        grad_bias_hidden,
        grad_bias_out,
    ]
    return (d_cells, grads_list)


def reduce_block(flat_grad):
    summed = lax.psum(flat_grad.astype(jnp.bfloat16), "win")
    return lax.psum_scatter(summed, "fsdp", scatter_dimension=0, tiled=True).astype(jnp.float32)


def per_device(tokens, cotangent, crop_ids, params, first_moment, second_moment):
    extent_x = tokens.shape[1]
    position = lax.axis_index("win")
    total_x = extent_x * lax.axis_size("win")
    cell_values = tokens[0].astype(jnp.float32).reshape(extent_x, SY, SZ, C)
    crop_row = crop_ids[0]
    spots_x = jnp.arange(extent_x)
    crops_plain = jnp.take(crop_row, position * extent_x + spots_x)
    crops_shift = jnp.take(crop_row, (position * extent_x + SHIFT + spots_x) % total_x)
    labels_plain = jnp.broadcast_to(9 * crops_plain[:, None, None], (extent_x, SY, SZ))
    labels_shift = (
        9 * crops_shift[:, None, None]
        + 3 * region_labels(SY)[None, :, None]
        + region_labels(SZ)[None, None, :]
    )
    rel_index = relative_index().reshape(-1)
    first_weights = gather_block(params[0])
    first_out, first_kept = block_forward(
        cell_values, labels_plain, first_weights, rel_index, False
    )
    second_weights = gather_block(params[1])
    second_out, second_kept = block_forward(
        first_out, labels_shift, second_weights, rel_index, True
    )
    d_final = cotangent[0].astype(jnp.float32).reshape(extent_x, SY, SZ, C)
    d_first, second_grads = block_backward(d_final, second_kept, second_weights, rel_index, True)
    d_input, first_grads = block_backward(d_first, first_kept, first_weights, rel_index, False)
    shard_first = reduce_block(pack_block(first_grads))
    shard_second = reduce_block(pack_block(second_grads))
    shards = jnp.stack([shard_first, shard_second])
    grad_norm = jnp.sqrt(lax.psum(jnp.sum(shards * shards), "fsdp"))
    clipped = shards * jnp.minimum(1.0, CLIP_LIMIT / (grad_norm + 1e-06))
    new_first = BETA_FIRST * first_moment + (1.0 - BETA_FIRST) * clipped
    new_second = BETA_SECOND * second_moment + (1.0 - BETA_SECOND) * clipped * clipped
    first_hat = new_first / (1.0 - BETA_FIRST**STEP)
    second_hat = new_second / (1.0 - BETA_SECOND**STEP)
    new_params = params - LEARN_RATE * (
        first_hat / (jnp.sqrt(second_hat) + EPS_ADAM) + WEIGHT_DECAY * params
    )
    block_out = second_out.reshape(1, extent_x, SY, SZ * C).astype(jnp.bfloat16)
    input_grad = d_input.reshape(1, extent_x, SY, SZ * C).astype(jnp.bfloat16)
    return (
        block_out,
        input_grad,
        grad_norm,
        new_params,
        new_first,
        new_second,
        new_params.astype(jnp.bfloat16),
    )


def solution(mesh):
    return jax.shard_map(
        per_device,
        mesh=mesh,
        in_specs=(
            P("fsdp", "win", None, None),
            P("fsdp", "win", None, None),
            P("fsdp", None),
            P(None, "fsdp"),
            P(None, "fsdp"),
            P(None, "fsdp"),
        ),
        out_specs=(
            P("fsdp", "win", None, None),
            P("fsdp", "win", None, None),
            P(),
            P(None, "fsdp"),
            P(None, "fsdp"),
            P(None, "fsdp"),
            P(None, "fsdp"),
        ),
        check_vma=False,
    )
```

profile of v0, /device:TPU:0, one launch (start us, length us, event | category | flops | bytes accessed | tf_op | source)
XLA Modules:
  0.0 2822.0 jit_solution(974413595007390664)
XLA Ops:
  8.5 8.5 all-gather
  19.8 7.1 all-gather.1
  45.5 3.2 reshape_reshape.51
  49.9 408.3 %gather_fusion.1 = bf16[117649,6]{1,0:T(8,128)(2,1)} fusion(bf16[2197,6]{1,0:T(8,128)(2,1)S(1)} %reshape.1054, s32[117760]{0:T(1024)S(1)} %pad_clamp_fusion), kind=kCustom, calls=%fused_computation.1.clone | custom fusion | bytes 3294172 | tf_op jit(solution)/shard_map/jit(_take)/gather | solution.py:234
  458.2 22.4 copy.318
  480.6 408.3 %gather_fusion.3 = bf16[117649,6]{1,0:T(8,128)(2,1)} fusion(bf16[2197,6]{1,0:T(8,128)(2,1)S(1)} %reshape.1063, s32[117760]{0:T(1024)S(1)} %pad_clamp_fusion), kind=kCustom, calls=%fused_computation.3.clone | custom fusion | bytes 3294172 | tf_op jit(solution)/shard_map/jit(_take)/gather | solution.py:234
  889.0 22.3 copy.330
  911.3 5.3 select_convert_fusion
  916.6 6.5 reshape.1105
  923.1 3.2 copy.320
  926.4 13.3 while.50
  940.3 3.9 copy.321
  944.2 4.0 reshape_reshape.52
  953.7 6.9 multiply_convert_fusion.3
  969.4 4.5 collective-permute-start
  990.5 6.4 reshape.1106
  996.9 3.3 copy.332
  1007.7 3.9 reshape_reshape.55
  1014.4 14.5 while.51
  1028.9 3.8 copy.333
  1032.7 4.0 reshape_reshape.57
  1068.9 6.9 multiply_convert_fusion.2
  1094.2 3.0 multiply_reduce_fusion.2
  1101.2 4.7 collective-permute-start.2
  1122.3 3.2 reshape_reshape.58
  1125.6 3.1 copy.347
  1129.7 45.7 %while.52 = (s32[]{:T(128)}, f32[6,343,343]{1,2,0:T(8,128)}, bf16[2,2,343,3,6,16]{2,5,4,1,3,0:T(8,128)(2,1)}, s32[2,2,343]{2,1,0:T(2,128)S(1)}, bf16[2,2,343,3,6...) while((s32[]{:T(128)}, f32[6,343,343]{1,2,0:T(8,128)}, ...), condition=%wide.region_21.24_spmd.clone, body=%wide.region_18.23_spmd.clone.sunk | while | flops 245279312 | bytes 80215808 | solution.py:193
  1134.0 4.0 multiply_reduce_fusion.16
  1138.0 7.3 convert_reduce_fusion.4
  1145.3 4.0 select_add_fusion.4
  1156.4 4.0 multiply_reduce_fusion.16
  1160.4 7.3 convert_reduce_fusion.4
  1167.7 5.0 select_add_fusion.4
  1175.4 3.1 copy.370
  1178.5 6.6 copy.388
  1185.1 9.5 reshape.1229
  1198.4 2.9 copy.372
  1204.0 5.6 reshape.1151
  1211.6 27.7 copy.373
  1239.3 625.6 %scatter_custom_fusion.1 = f32[2197,6]{1,0:T(8,128)S(1)} fusion(s32[117649]{0:T(1024)} %copy-done.37, f32[117649,6]{1,0:T(8,128)} %copy.373, f32[]{:T(128)} %constant.157.clone.1), kind=kCustom, calls=%fused_computation.198 | custom fusion | flops 705894 | bytes 53240 | tf_op jit(solution)/shard_map/scatter-add | solution.py:341
  1879.0 4.0 fusion.142
  1885.4 3.9 fusion.160
  1895.9 3.1 reshape_reshape.60
  1899.0 3.3 copy.358
  1903.4 46.0 %while.53 = (s32[]{:T(128)}, f32[6,343,343]{1,2,0:T(8,128)}, bf16[2,2,343,3,6,16]{2,5,4,1,3,0:T(8,128)(2,1)}, s32[2,2,343]{2,1,0:T(2,128)S(1)}, bf16[2,2,343,3,6...) while((s32[]{:T(128)}, f32[6,343,343]{1,2,0:T(8,128)}, ...), condition=%wide.region_29.32_spmd.clone, body=%wide.region_26.31_spmd.clone.sunk | while | flops 245279312 | bytes 80215808 | solution.py:193
  1907.9 4.0 multiply_reduce_fusion.17
  1911.9 7.3 convert_reduce_fusion.5
  1919.2 4.0 select_add_fusion.5
  1930.3 4.0 multiply_reduce_fusion.17
  1934.3 7.3 convert_reduce_fusion.5
  1941.6 5.0 select_add_fusion.5
  1949.4 3.0 copy.366
  1952.3 7.9 copy.389
  1962.6 2.9 copy.368
  1968.1 5.6 reshape.1143
  1975.6 10.3 reshape.1232
  1993.5 27.7 copy.369
  2021.2 625.7 %scatter_custom_fusion = f32[2197,6]{1,0:T(8,128)S(1)} fusion(s32[117649]{0:T(1024)} %copy-done.37, f32[117649,6]{1,0:T(8,128)} %copy.369, f32[]{:T(128)} %constant.157.clone.1), kind=kCustom, calls=%fused_computation.200 | custom fusion | flops 705894 | bytes 53240 | tf_op jit(solution)/shard_map/scatter-add | solution.py:341
  2651.6 19.9 concatenate.115
  2673.2 17.4 concatenate.116
  2695.8 30.8 %all-reduce.11.cloned.1.call-done = (bf16[124928]{0:T(1024)(128)(2,1)}, bf16[124928]{0:T(1024)(128)(2,1)}) async-done(((bf16[124928]{0:T(1024)(128)(2,1)}, bf16[124928]{0:T(1024)(128)(2,1)}), (bf16[124928]{0:T(1024)(128)(2,1)}, bf16[124928]{0:T(1024)(128)(2,1)})) %all-reduce.11.cloned.1.call-update) | async-done | bytes 499728
  2733.9 67.2 %all-reduce.9.cloned.1.call-done = (bf16[31232]{0:T(1024)(128)(2,1)}, bf16[31232]{0:T(1024)(128)(2,1)}) async-done(((bf16[31232]{0:T(1024)(128)(2,1)}, bf16[31232]{0:T(1024)(128)(2,1)}), (bf16[31232]{0:T(1024)(128)(2,1)}, bf16[31232]{0:T(1024)(128)(2,1)})) %all-reduce.9.cloned.1.call-update) | async-done | bytes 124944 | tf_op jit(solution)/shard_map/psum | solution.py:376
  2803.9 6.3 psum.23
  2810.9 2.9 fusion.139
  (627 shorter events, 259.4 us)
Async XLA Ops:
  7.2 26.4 copy-start
  7.2 2719.4 %all-reduce.11.cloned.1.call-start = ((), (), s32[]{:S(2)}) async-start(), calls=%async_computation.1 | async-start | bytes 999424
  18.4 24.3 copy-start.123
  18.9 18.2 copy-start.95
  19.0 10.5 copy-start.32
  19.8 16.7 copy-start.75
  31.3 6.0 copy-start.8
  32.2 9.7 copy-start.87
  32.8 9.9 copy-start.22
  42.1 6.7 copy-start.66
  889.0 22.3 copy-start.96
  939.7 8.5 copy-start.2
  950.0 10.7 copy-start.34
  952.8 12.6 copy-start.18
  952.8 7.9 copy-start.69
  952.9 7.7 copy-start.119
  953.5 7.2 copy-start.88
  953.5 7.2 copy-start.91
  953.7 7.1 copy-start.121
  953.7 7.0 copy-start.97
  953.7 7.0 copy-start.137
  962.0 5.9 copy-start.16
  965.4 11.7 copy-start.54
  967.9 15.4 copy-start.64
  969.4 30.8 %collective-permute-start = (bf16[3,14,14,96]{3,2,1,0:T(8,128)(2,1)}, bf16[3,14,14,96]{3,2,1,0:T(8,128)(2,1)}, u32[]{:S(2)}, u32[]{:S(2)}) collective-permute-start(bf16[3,14,14,96]{3,2,1,0:T(8,128)(2,1)} %slice.385), channel_id=1, source_target_pairs={{0,28},{4,0},{8,4},{12,8},{16,12},{20,16},{24,20},{28,24},{1,29},{... | collective-permute-start | bytes 338696 | tf_op jit(solution)/shard_map/ppermute | solution.py:33
  981.0 6.0 copy-start.57
  1005.3 8.4 copy-start.46
  1036.9 9.5 copy-start.142
  1036.9 10.7 copy-start.50
  1046.0 10.5 collective-permute-start.1
  1060.7 8.2 copy-start.129
  1060.7 8.2 copy-start.136
  1068.9 6.9 copy-start.99
  1079.5 7.9 copy-start.135
  1087.4 6.7 copy-start.51
  1087.4 6.7 copy-start.104
  1087.4 6.7 copy-start.105
  1099.4 8.3 copy-start.33
  1101.2 12.5 collective-permute-start.2
  1167.7 5.0 copy-start.4
  1185.1 9.5 copy-start.102
  1204.0 5.6 copy-start.42
  1204.0 6.3 copy-start.47
  1211.5 657.3 %collective-permute-start.3 = (bf16[3,14,14,96]{3,2,1,0:T(8,128)(2,1)S(1)}, bf16[3,14,14,96]{3,2,1,0:T(8,128)(2,1)S(1)}, u32[]{:S(2)}, u32[]{:S(2)}) collective-permute-start(bf16[3,14,14,96]{3,2,1,0:T(8,128)(2,1)S(1)} %pad_maximum_fusion.8), channel_id=1, source_target_pairs={{0,4},{4,8},{8,12},{12,16},{16,20},{20,24},{24,28},{28,0},{1,5},{5... | collective-permute-start | bytes 338696 | tf_op jit(solution)/shard_map/ppermute | solution.py:33
  1870.6 8.4 copy-start.21
  1870.6 8.4 copy-start.25
  1870.6 8.4 copy-start.27
  1870.6 8.4 copy-start.82
  1941.6 5.0 copy-start.5
  1952.3 7.9 copy-start.100
  1952.3 8.6 copy-start.103
  1952.3 10.2 copy-start.6
  1968.1 5.6 copy-start.43
  1968.1 6.3 copy-start.45
  1975.6 10.3 copy-start.101
  2021.2 629.1 %copy-start.61 = (bf16[3,14,14,96]{3,2,1,0:T(8,128)(2,1)S(1)}, bf16[3,14,14,96]{3,2,1,0:T(8,128)(2,1)}, u32[]{:S(2)}) copy-start(bf16[3,14,14,96]{3,2,1,0:T(8,128)(2,1)} %copy-done.60) | copy-start | bytes 338692
  2021.2 652.0 %copy-start.113 = (bf16[13182]{0:T(1024)(128)(2,1)S(1)}, bf16[13182]{0:T(1024)(128)(2,1)}, u32[]{:S(2)}) copy-start(bf16[13182]{0:T(1024)(128)(2,1)} %reshape.1090) | copy-start | bytes 79096
  2021.2 652.0 %copy-start.116 = (bf16[9216]{0:T(1024)(128)(2,1)S(1)}, bf16[9216]{0:T(1024)(128)(2,1)}, u32[]{:S(2)}) copy-start(bf16[9216]{0:T(1024)(128)(2,1)} %reshape.1086) | copy-start | bytes 55300
  2021.2 652.0 %copy-start.132 = (bf16[96]{0:T(256)(128)(2,1)S(1)}, bf16[96]{0:T(256)(128)(2,1)}, u32[]{:S(2)}) copy-start(bf16[96]{0:T(256)(128)(2,1)} %get-tuple-element.397) | copy-start | bytes 580
  2650.3 79.5 %copy-start.29 = (f32[7,14,14,96]{3,2,1,0:T(8,128)S(1)}, f32[7,14,14,96]{3,2,1,0:T(8,128)}, u32[]{:S(2)}) copy-start(f32[7,14,14,96]{3,2,1,0:T(8,128)} %get-tuple-element.481) | copy-start | bytes 1580548
  2650.3 79.5 %copy-start.31 = (f32[7,14,14,96]{3,2,1,0:T(8,128)S(1)}, f32[7,14,14,96]{3,2,1,0:T(8,128)}, u32[]{:S(2)}) copy-start(f32[7,14,14,96]{3,2,1,0:T(8,128)} %copy-done.30) | copy-start | bytes 1580548
  2650.3 79.5 %copy-start.84 = (f32[7,14,14]{2,1,0:T(8,128)S(1)}, f32[7,14,14]{2,1,0:T(8,128)}, u32[]{:S(2)}) copy-start(f32[7,14,14]{2,1,0:T(8,128)} %copy-done.83) | copy-start | bytes 16468
  2692.3 108.8 %all-reduce.9.cloned.1.call-start = ((), (), s32[]{:S(2)}) async-start(), calls=%async_computation | async-start | bytes 253952 | tf_op jit(solution)/shard_map/psum | solution.py:376
  2729.8 84.0 %copy-start.1 = (s32[1,56]{1,0:T(1,128)S(1)}, s32[1,56]{1,0:T(1,128)}, u32[]{:S(2)}) copy-start(s32[1,56]{1,0:T(1,128)} %param.20) | copy-start | bytes 676
  (93 other events, 202.5 us)
Sparse Core Ops, SparseCore 0:
  2692.4 34.1 all-reduce.10
  2730.7 70.3 all-reduce.8
where the time goes:
time: 2840 us; the launch traced here: 2820 us
  other arithmetic  1370 us (48%)
  local copies, waits for them, and re-layouts  1200 us (42%)
  waiting for transfers between devices  98 us (3%)
  matrix products  95.9 us (3%)
    scatter-add x2, other arithmetic, block_backward(): jax.ops.segment_sum(d_table_full.transpose(1, 2, 0).reshape(-1, HEADS), r...  1250 us
    gather x4, local copies, waits for them, and re-layouts, block_forward(): table_bias = jnp.take(bias_table, rel_index, axis=0).astype(jnp.float32)  861 us
    psum x1, waiting for transfers between devices, reduce_block(): summed = lax.psum(flat_grad.astype(jnp.bfloat16), 'win')  67.2 us
    reshape x4, local copies, waits for them, and re-layouts, block_backward(): d_table_full.transpose(1, 2, 0).reshape(-1, HEADS)  66.7 us
  transfers between devices with their start and end apart: 6, of which 2 were waited for; matrix products, arithmetic and copies ran while one was open for 25% of the time, Pallas kernels for 0%

commit v1 on v0

--- a/solution.py
+++ b/solution.py
@@ -78,6 +78,22 @@
         return coord_one[:, None] - coord_one[None, :] + WS - 1
 
     return (differ(coord_a) * table_span + differ(coord_b)) * table_span + differ(coord_c)
+
+
+def expand_table(bias_table):
+    span = 2 * WS - 1
+    cube = bias_table.T.reshape(HEADS, span, span, span)
+    cube = jnp.stack([cube[:, :, :, WS - 1 - k : 2 * WS - 1 - k] for k in range(WS)], axis=1)
+    cube = jnp.stack([cube[:, :, :, WS - 1 - k : 2 * WS - 1 - k] for k in range(WS)], axis=1)
+    cube = jnp.stack([cube[:, :, :, WS - 1 - k : 2 * WS - 1 - k] for k in range(WS)], axis=1)
+    return cube.reshape(HEADS, WS**3, WS**3).transpose(0, 2, 1)
+
+
+def collapse_table(d_full):
+    pull = jax.linear_transpose(
+        expand_table, jax.ShapeDtypeStruct((TABLE, HEADS), jnp.float32)
+    )
+    return pull(d_full)[0]
 
 
 def region_labels(extent):
@@ -231,8 +247,7 @@
     )
     qkv_flat = jnp.dot(windows.reshape(-1, C), w_qkv, preferred_element_type=jnp.float32) + bias_all
     qkv_wins = qkv_flat.astype(jnp.bfloat16).reshape(-1, WS**3, 3 * C)
-    table_bias = jnp.take(bias_table, rel_index, axis=0).astype(jnp.float32)
-    table_bias = table_bias.reshape(WS**3, WS**3, HEADS).transpose(2, 0, 1)
+    table_bias = expand_table(bias_table.astype(jnp.float32))
     attended_wins, log_totals = attention_forward(qkv_wins, label_wins, table_bias)
     attended = from_windows(attended_wins, extent_x, SY, SZ)
     if shifted:
@@ -338,9 +353,7 @@
     column_sums = jnp.sum(d_qkv_flat.astype(jnp.float32), axis=0)
     grad_bias_query = column_sums[:C]
     grad_bias_value = column_sums[2 * C :]
-    grad_table = jax.ops.segment_sum(
-        d_table_full.transpose(1, 2, 0).reshape(-1, HEADS), rel_index, num_segments=TABLE
-    )
+    grad_table = collapse_table(d_table_full)
     d_region = jnp.dot(d_qkv_flat, w_qkv.T, preferred_element_type=jnp.float32)
     d_region = from_windows(d_region.reshape(-1, WS**3, C), extent_x, SY, SZ)
     if shifted:

time: 2840 us -> 987 us (0.35)
  other arithmetic: 1370 us -> 177 us
  local copies, waits for them, and re-layouts: 1200 us -> 539 us
    scatter-add x2 -> x0, other arithmetic: 1250 us -> none  [block_backward(): jax.ops.segment_sum(d_table_full.transpose(1, 2, 0).reshape(-1, HEADS), r...]
    gather x4 -> x0, local copies, waits for them, and re-layouts: 861 us -> none  [block_forward(): table_bias = jnp.take(bias_table, rel_index, axis=0).astype(jnp.float32)]
    another operation x12 -> x24, local copies, waits for them, and re-layouts: 38 us -> 143 us  [the longest x12 102 us: expand_table(): jnp.stack([cube[:, :, :, WS - 1 - k:2 * WS - 1 - k] for k in range(WS)],...]
    reshape x4 -> x14, local copies, waits for them, and re-layouts: 66.7 us -> 159 us  [the longest x6 155 us: expand_table(): return cube.reshape(HEADS, WS ** 3, WS ** 3).transpose(0, 2, 1)]
    add_any x0 -> x4, other arithmetic: none -> 58.7 us  [expand_table(): cube[:, :, :, WS - 1 - k:2 * WS - 1 - k]]
    unnamed x278 -> x312, local copies, waits for them, and re-layouts: 17.3 us -> 65.6 us
  transfers between devices with their start and end apart: 6 -> 6, of which waited for: 2 -> 3; matrix products, arithmetic and copies ran while one was open for 25% -> 25% of each run, Pallas kernels for 0% -> 0%
where the time goes in v1:
time: 987 us; the launch traced here: 977 us
  local copies, waits for them, and re-layouts  539 us (55%)
  other arithmetic  177 us (18%)
  matrix products  109 us (11%)
  waiting for transfers between devices  104 us (11%)
  blocking collectives  22.7 us (2%)
  between operations  18.9 us (2%)
    reshape x6, local copies, waits for them, and re-layouts, expand_table(): return cube.reshape(HEADS, WS ** 3, WS ** 3).transpose(0, 2, 1)  155 us
    another operation x12, local copies, waits for them, and re-layouts, expand_table(): jnp.stack([cube[:, :, :, WS - 1 - k:2 * WS - 1 - k] for k in range(WS)],...  102 us
    psum x1, waiting for transfers between devices, reduce_block(): summed = lax.psum(flat_grad.astype(jnp.bfloat16), 'win')  67.7 us
    unnamed x312, local copies, waits for them, and re-layouts  65.6 us
    add_any x4, other arithmetic, expand_table(): cube[:, :, :, WS - 1 - k:2 * WS - 1 - k]  58.7 us
    another operation x12, local copies, waits for them, and re-layouts  41.5 us
    unnamed x3, waiting for transfers between devices  34 us
    reduce_sum x4, other arithmetic, one_group(): jnp.sum(d_scores.astype(jnp.float32), axis=0)  30.1 us
  transfers between devices with their start and end apart: 6, of which 3 were waited for; matrix products, arithmetic and copies ran while one was open for 25% of the time, Pallas kernels for 0%

profile of v1, /device:TPU:0, one launch (start us, length us, event | category | flops | bytes accessed | tf_op | source)
XLA Modules:
  0.0 977.4 jit_solution(12601309097481381476)
XLA Ops:
  8.5 8.5 all-gather
  26.8 7.9 all-gather.1
  39.4 3.8 fusion.69
  43.2 3.8 fusion.68
  47.0 3.8 fusion.67
  50.9 3.8 fusion.66
  54.7 3.8 fusion.65
  58.5 3.8 fusion.64
  62.3 3.8 fusion.63
  66.1 35.4 %reshape.1024 = f32[6,343,343]{2,0,1:T(8,128)} reshape(f32[6,7,7,7,7,7,7]{6,5,4,0,3,2,1:T(8,128)} %fusion.63) | data formatting | bytes 5647152 | tf_op jit(solution)/shard_map/reshape | solution.py:89
  114.7 3.8 reshape_reshape.51
  124.9 14.9 %while.50 = (s32[]{:T(128)}, bf16[2,2,343,6,16]{2,4,3,1,0:T(8,128)(2,1)}, f32[2,2,6,343]{3,2,1,0:T(8,128)}, bf16[2,2,343,3,6,16]{2,5,4,1,3,0:T(8,128)(2,1)}, s32...) while((s32[]{:T(128)}, bf16[2,2,343,6,16]{2,4,3,1,0:T(8,128)(2,1)}, ...), condition=%wide.region_5.7_spmd, body=%wide.region_2.6_spmd.sunk | while | flops 110416504 | bytes 31729696 | solution.py:170
  139.8 4.9 copy.415
  144.7 4.2 reshape_reshape.52
  160.3 6.6 multiply_convert_fusion.3
  175.0 4.5 collective-permute-start
  200.1 3.8 fusion.62
  203.9 3.8 fusion.61
  207.7 3.8 fusion.60
  211.5 3.8 fusion.59
  215.4 3.8 fusion.58
  219.2 3.8 fusion.57
  223.0 3.8 fusion.56
  226.8 35.2 %reshape.1025 = f32[6,343,343]{2,0,1:T(8,128)} reshape(f32[6,7,7,7,7,7,7]{6,5,4,0,3,2,1:T(8,128)} %fusion.56) | data formatting | bytes 5647152 | tf_op jit(solution)/shard_map/reshape | solution.py:89
  278.3 3.8 reshape_reshape.55
  285.7 16.3 %while.51 = (s32[]{:T(128)}, bf16[2,2,343,6,16]{2,4,3,1,0:T(8,128)(2,1)}, f32[2,2,6,343]{3,2,1,0:T(8,128)}, bf16[2,2,343,3,6,16]{2,5,4,1,3,0:T(8,128)(2,1)}, s32...) while((s32[]{:T(128)}, bf16[2,2,343,6,16]{2,4,3,1,0:T(8,128)(2,1)}, ...), condition=%wide.region_13.15_spmd, body=%wide.region_10.14_spmd.sunk | while | flops 110416504 | bytes 31729696 | solution.py:170
  302.0 4.7 copy.427
  306.7 4.2 reshape_reshape.57
  334.8 7.0 multiply_convert_fusion.2
  391.1 50.0 %while.52 = (s32[]{:T(128)}, f32[6,343,343]{1,2,0:T(8,128)}, bf16[2,2,343,3,6,16]{2,5,4,1,3,0:T(8,128)(2,1)}, s32[2,2,343]{2,1,0:T(2,128)S(1)}, bf16[2,2,343,3,6...) while((s32[]{:T(128)}, f32[6,343,343]{1,2,0:T(8,128)}, ...), condition=%wide.region_21.23_spmd.clone, body=%wide.region_18.22_spmd.clone.sunk | while | flops 245279312 | bytes 79869072 | solution.py:209
  394.5 4.0 multiply_reduce_fusion.16
  398.5 7.5 convert_reduce_fusion.4
  411.8 3.8 select_add_fusion.4
  419.0 4.0 multiply_reduce_fusion.16
  423.0 7.5 convert_reduce_fusion.4
  436.3 4.8 select_add_fusion.4
  441.1 7.8 copy.520
  448.9 9.6 reshape.1027
  462.3 39.3 %reshape.918 = f32[6,7,7,7,7,7,7]{6,5,4,3,2,1,0:T(8,128)} reshape(f32[6,343,343]{2,1,0:T(8,128)S(1)} %bitcast.730) | data formatting | bytes 5647152 | tf_op jit(solution)/shard_map/transpose()/reshape | solution.py:89
  501.6 36.0 %slice_bitcast_fusion.34 = (f32[6,7,7,7,7,7]{5,4,3,2,1,0:T(8,128)S(1)}, f32[6,7,7,7,7,7]{5,4,3,2,1,0:T(8,128)}, f32[6,7,7,7,7,7]{5,4,3,2,1,0:T(8,128)}, f32[6,7,...) fusion(f32[6,7,7,7,7,7,7]{6,5,4,3,2,1,0:T(8,128)} %reshape.918), kind=kLoop, calls=%fused_computation.110 | loop fusion | bytes 5647152 | tf_op jit(solution)/shard_map/transpose()/unstack | solution.py:88
  537.7 22.6 %pad_add_fusion = f32[6,7,7,13,7,7]{5,4,3,2,1,0:T(8,128)} fusion(f32[6,7,7,7,7,7]{5,4,3,2,1,0:T(8,128)} %get-tuple-element.493, f32[6,7,7,7,7,7]{5,4,3,2,1,0:T(8,128)} %get-tuple-element.494, f32[6,7,7,7,7,7]{5,4,3,2,1,0:T(8,128)} %get-tuple-element.489, f32[6,7,7,7,7,7]{5,4,3,2,1,0:T(8,128)} %get-tuple-element.490, ...), kind=kLoop, calls=%fused_computation.102 | loop fusion | flops 1123668 | bytes 3572688 | tf_op jit(solution)/shard_map/transpose()/add_any | solution.py:88
  560.3 10.5 %slice_bitcast_fusion.62 = (f32[6,7,13,7,7]{4,3,2,1,0:T(8,128)S(1)}, f32[6,7,13,7,7]{4,3,2,1,0:T(8,128)}, f32[6,7,13,7,7]{4,3,2,1,0:T(8,128)}, f32[6,7,13,7,7]{4...) fusion(f32[6,7,7,13,7,7]{5,4,3,2,1,0:T(8,128)} %pad_add_fusion), kind=kLoop, calls=%fused_computation.173 | loop fusion | bytes 1498224 | tf_op jit(solution)/shard_map/transpose()/unstack | solution.py:87
  570.7 6.8 pad_add_fusion.2
  602.5 3.4 fusion.175
  608.3 4.0 fusion.193
  629.1 50.1 %while.53 = (s32[]{:T(128)}, f32[6,343,343]{1,2,0:T(8,128)}, bf16[2,2,343,3,6,16]{2,5,4,1,3,0:T(8,128)(2,1)}, s32[2,2,343]{2,1,0:T(2,128)S(1)}, bf16[2,2,343,3,6...) while((s32[]{:T(128)}, f32[6,343,343]{1,2,0:T(8,128)}, ...), condition=%wide.region_29.31_spmd.clone, body=%wide.region_26.30_spmd.clone.sunk | while | flops 245279312 | bytes 79869072 | solution.py:209
  632.4 4.0 multiply_reduce_fusion.17
  636.4 7.5 convert_reduce_fusion.5
  649.8 3.9 select_add_fusion.5
  657.0 4.0 multiply_reduce_fusion.17
  661.0 7.5 convert_reduce_fusion.5
  674.4 4.8 select_add_fusion.5
  679.2 7.9 copy.521
  690.1 39.7 %reshape.911 = f32[6,7,7,7,7,7,7]{6,5,4,3,2,1,0:T(8,128)} reshape(f32[6,343,343]{2,1,0:T(8,128)S(1)} %bitcast.729) | data formatting | bytes 5647152 | tf_op jit(solution)/shard_map/transpose()/reshape | solution.py:89
  729.8 36.0 %slice_bitcast_fusion.41 = (f32[6,7,7,7,7,7]{5,4,3,2,1,0:T(8,128)S(1)}, f32[6,7,7,7,7,7]{5,4,3,2,1,0:T(8,128)}, f32[6,7,7,7,7,7]{5,4,3,2,1,0:T(8,128)}, f32[6,7,...) fusion(f32[6,7,7,7,7,7,7]{6,5,4,3,2,1,0:T(8,128)} %reshape.911), kind=kLoop, calls=%fused_computation.117 | loop fusion | bytes 5647152 | tf_op jit(solution)/shard_map/transpose()/unstack | solution.py:88
  765.8 22.6 %pad_add_fusion.1 = f32[6,7,7,13,7,7]{5,4,3,2,1,0:T(8,128)} fusion(f32[6,7,7,7,7,7]{5,4,3,2,1,0:T(8,128)} %get-tuple-element.486, f32[6,7,7,7,7,7]{5,4,3,2,1,0:T(8,128)} %get-tuple-element.487, f32[6,7,7,7,7,7]{5,4,3,2,1,0:T(8,128)} %get-tuple-element.482, f32[6,7,7,7,7,7]{5,4,3,2,1,0:T(8,128)} %get-tuple-element.483, ...), kind=kLoop, calls=%fused_computation.103 | loop fusion | flops 1123668 | bytes 3572688 | tf_op jit(solution)/shard_map/transpose()/add_any | solution.py:88
  788.4 10.5 %slice_bitcast_fusion.69 = (f32[6,7,13,7,7]{4,3,2,1,0:T(8,128)S(1)}, f32[6,7,13,7,7]{4,3,2,1,0:T(8,128)}, f32[6,7,13,7,7]{4,3,2,1,0:T(8,128)}, f32[6,7,13,7,7]{4...) fusion(f32[6,7,7,13,7,7]{5,4,3,2,1,0:T(8,128)} %pad_add_fusion.1), kind=kLoop, calls=%fused_computation.180 | loop fusion | bytes 1498224 | tf_op jit(solution)/shard_map/transpose()/unstack | solution.py:87
  798.9 6.7 pad_add_fusion.3
  810.3 10.3 %reshape.1030 = bf16[2,2,7,7,7,288]{5,4,3,2,1,0:T(8,128)(2,1)} reshape(bf16[2,2,343,3,6,16]{5,4,3,2,1,0:T(8,128)(2,1)} %copy.521) | data formatting | bytes 1580544 | tf_op jit(solution)/shard_map/reshape.359
  833.5 8.1 concatenate.115
  843.5 4.6 concatenate.116
  849.2 34.0 %all-reduce.53.cloned.1.call-done = (bf16[124928]{0:T(1024)(128)(2,1)}, bf16[124928]{0:T(1024)(128)(2,1)}) async-done(((bf16[124928]{0:T(1024)(128)(2,1)}, bf16[124928]{0:T(1024)(128)(2,1)}), (bf16[124928]{0:T(1024)(128)(2,1)}, bf16[124928]{0:T(1024)(128)(2,1)})) %all-reduce.53.cloned.1.call-update) | async-done | bytes 499728
  890.0 67.7 %all-reduce.51.cloned.1.call-done = (bf16[31232]{0:T(1024)(128)(2,1)}, bf16[31232]{0:T(1024)(128)(2,1)}) async-done(((bf16[31232]{0:T(1024)(128)(2,1)}, bf16[31232]{0:T(1024)(128)(2,1)}), (bf16[31232]{0:T(1024)(128)(2,1)}, bf16[31232]{0:T(1024)(128)(2,1)})) %all-reduce.51.cloned.1.call-update) | async-done | bytes 124944 | tf_op jit(solution)/shard_map/psum | solution.py:389
  960.4 6.3 psum.23
  (691 shorter events, 316.0 us)
Async XLA Ops:
  7.2 114.2 %copy-start = (s32[1,56]{1,0:T(1,128)S(1)}, s32[1,56]{1,0:T(1,128)}, u32[]{:S(2)}) copy-start(s32[1,56]{1,0:T(1,128)} %param.18) | copy-start | bytes 676
  7.2 13.1 %copy-start.34 = (bf16[1,7,14,1344]{3,2,1,0:T(8,128)(2,1)S(1)}, bf16[1,7,14,1344]{3,2,1,0:T(8,128)(2,1)}, u32[]{:S(2)}) copy-start(bf16[1,7,14,1344]{3,2,1,0:T(8,128)(2,1)} %param.16) | copy-start | bytes 790276
  7.2 876.0 %all-reduce.53.cloned.1.call-start = ((), (), s32[]{:S(2)}) async-start(), calls=%async_computation.1 | async-start | bytes 999424
  17.8 86.8 %copy-start.123 = (f32[96]{0:T(128)}, f32[96]{0:T(128)S(1)}, u32[]{:S(2)}) copy-start(f32[96]{0:T(128)S(1)} %get-tuple-element.538) | copy-start | bytes 1156
  19.2 16.5 %copy-start.8 = (f32[7,14,14,96]{3,2,1,0:T(8,128)}, f32[7,14,14,96]{3,2,1,0:T(8,128)S(1)}, u32[]{:S(2)}) copy-start(f32[7,14,14,96]{3,2,1,0:T(8,128)S(1)} %reshape.922) | copy-start | bytes 1580548
  20.1 84.3 %copy-start.85 = (f32[7,14,14]{2,1,0:T(8,128)}, f32[7,14,14]{2,1,0:T(8,128)S(1)}, u32[]{:S(2)}) copy-start(f32[7,14,14]{2,1,0:T(8,128)S(1)} %multiply_reduce_fusion.9) | copy-start | bytes 16468
  108.8 16.1 %copy-start.43 = (bf16[1372,96]{1,0:T(8,128)(2,1)}, bf16[1372,96]{1,0:T(8,128)(2,1)S(1)}, u32[]{:S(2)}) copy-start(bf16[1372,96]{1,0:T(8,128)(2,1)S(1)} %reshape_reshape.50) | copy-start | bytes 790276
  139.8 9.9 %copy-start.2 = (f32[6,343,343]{1,2,0:T(8,128)}, f32[6,343,343]{1,2,0:T(8,128)S(1)}, u32[]{:S(2)}) copy-start(f32[6,343,343]{1,2,0:T(8,128)S(1)} %get-tuple-element.884) | copy-start | bytes 8470732
  139.8 9.9 %copy-start.107 = (s32[2,2,343]{2,1,0:T(2,128)}, s32[2,2,343]{2,1,0:T(2,128)S(1)}, u32[]{:S(2)}) copy-start(s32[2,2,343]{2,1,0:T(2,128)S(1)} %get-tuple-element.894) | copy-start | bytes 16468
  139.8 11.0 %copy-start.118 = (bf16[9216]{0:T(1024)(128)(2,1)S(1)}, bf16[9216]{0:T(1024)(128)(2,1)}, u32[]{:S(2)}) copy-start(bf16[9216]{0:T(1024)(128)(2,1)} %slice_reduce_fusion.7) | copy-start | bytes 55300
  154.3 12.7 %copy-start.36 = (f32[1372,96]{0,1:T(8,128)}, f32[1372,96]{0,1:T(8,128)S(1)}, u32[]{:S(2)}) copy-start(f32[1372,96]{0,1:T(8,128)S(1)} %get-tuple-element.555) | copy-start | bytes 1580548
  158.3 13.5 %copy-start.20 = (f32[7,14,14,96]{3,2,1,0:T(8,128)}, f32[7,14,14,96]{3,2,1,0:T(8,128)S(1)}, u32[]{:S(2)}) copy-start(f32[7,14,14,96]{3,2,1,0:T(8,128)S(1)} %get-tuple-element.472) | copy-start | bytes 1580548
  158.3 8.6 copy-start.64
  158.5 8.5 copy-start.119
  159.0 7.9 copy-start.87
  170.9 19.1 %copy-start.83 = (f32[7,14,14]{2,1,0:T(8,128)}, f32[7,14,14]{2,1,0:T(8,128)S(1)}, u32[]{:S(2)}) copy-start(f32[7,14,14]{2,1,0:T(8,128)S(1)} %div.119) | copy-start | bytes 16468
  171.7 18.3 %copy-start.91 = (f32[7,14,14]{2,1,0:T(8,128)}, f32[7,14,14]{2,1,0:T(8,128)S(1)}, u32[]{:S(2)}) copy-start(f32[7,14,14]{2,1,0:T(8,128)S(1)} %add.540) | copy-start | bytes 16468
  171.8 9.9 %copy-start.77 = (f32[7,14,14]{2,1,0:T(8,128)}, f32[7,14,14]{2,1,0:T(8,128)S(1)}, u32[]{:S(2)}) copy-start(f32[7,14,14]{2,1,0:T(8,128)S(1)} %rsqrt.58) | copy-start | bytes 16468
  171.8 20.5 %copy-start.93 = (bf16[27648]{0:T(1024)(128)(2,1)S(1)}, bf16[27648]{0:T(1024)(128)(2,1)}, u32[]{:S(2)}) copy-start(bf16[27648]{0:T(1024)(128)(2,1)} %slice_reduce_fusion.5) | copy-start | bytes 165892
  175.0 95.9 %collective-permute-start = (bf16[3,14,14,96]{3,2,1,0:T(8,128)(2,1)}, bf16[3,14,14,96]{3,2,1,0:T(8,128)(2,1)}, u32[]{:S(2)}, u32[]{:S(2)}) collective-permute-start(bf16[3,14,14,96]{3,2,1,0:T(8,128)(2,1)} %slice.570), channel_id=1, source_target_pairs={{0,28},{4,0},{8,4},{12,8},{16,12},{20,16},{24,20},{28,24},{1,29},{... | collective-permute-start | bytes 338696 | tf_op jit(solution)/shard_map/ppermute | solution.py:33
  276.0 9.7 copy-start.45
  315.3 9.4 collective-permute-start.1
  321.9 12.9 %copy-start.128 = (f32[96]{0:T(128)S(1)}, f32[96]{0:T(128)}, u32[]{:S(2)}) copy-start(f32[96]{0:T(128)} %get-tuple-element.525) | copy-start | bytes 1156
  321.9 12.9 %copy-start.135 = (f32[96]{0:T(128)S(1)}, f32[96]{0:T(128)}, u32[]{:S(2)}) copy-start(f32[96]{0:T(128)} %get-tuple-element.524) | copy-start | bytes 1156
  356.5 11.4 %copy-start.35 = (bf16[1,7,14,1344]{3,2,1,0:T(8,128)(2,1)S(1)}, bf16[1,7,14,1344]{3,2,1,0:T(8,128)(2,1)}, u32[]{:S(2)}) copy-start(bf16[1,7,14,1344]{3,2,1,0:T(8,128)(2,1)} %param.16) | copy-start | bytes 790276
  357.2 18.1 %collective-permute-start.2 = (bf16[3,14,14,96]{3,2,1,0:T(8,128)(2,1)}, bf16[3,14,14,96]{3,2,1,0:T(8,128)(2,1)}, u32[]{:S(2)}, u32[]{:S(2)}) collective-permute-start(bf16[3,14,14,96]{3,2,1,0:T(8,128)(2,1)} %slice.614), channel_id=1, source_target_pairs={{0,28},{4,0},{8,4},{12,8},{16,12},{20,16},{24,20},{28,24},{1,29},{... | collective-permute-start | bytes 338696 | tf_op jit(solution)/shard_map/ppermute | solution.py:33
  448.9 9.7 copy-start.99
  462.3 128.9 %collective-permute-start.3 = (bf16[3,14,14,96]{3,2,1,0:T(8,128)(2,1)}, bf16[3,14,14,96]{3,2,1,0:T(8,128)(2,1)}, u32[]{:S(2)}, u32[]{:S(2)}) collective-permute-start(bf16[3,14,14,96]{3,2,1,0:T(8,128)(2,1)} %pad_maximum_fusion.8), channel_id=1, source_target_pairs={{0,4},{4,8},{8,12},{12,16},{16,20},{20,24},{24,28},{28,0},{1,5},{5... | collective-permute-start | bytes 338696 | tf_op jit(solution)/shard_map/ppermute | solution.py:33
  579.3 8.0 copy-start.14
  581.2 8.6 copy-start.146
  581.3 9.2 copy-start.41
  586.5 11.1 %copy-start.19 = (f32[1372,96]{0,1:T(8,128)S(1)}, f32[1372,96]{0,1:T(8,128)}, u32[]{:S(2)}) copy-start(f32[1372,96]{0,1:T(8,128)} %copy-done.18) | copy-start | bytes 1580548
  586.5 11.0 %copy-start.111 = (f32[1372]{0:T(1024)S(1)}, f32[1372]{0:T(1024)}, u32[]{:S(2)}) copy-start(f32[1372]{0:T(1024)} %copy-done.110) | copy-start | bytes 16468
  586.5 11.0 %copy-start.126 = (f32[96]{0:T(128)S(1)}, f32[96]{0:T(128)}, u32[]{:S(2)}) copy-start(f32[96]{0:T(128)} %get-tuple-element.530) | copy-start | bytes 1156
  587.5 12.0 %copy-start.115 = (f32[1372]{0:T(1024)S(1)}, f32[1372]{0:T(1024)}, u32[]{:S(2)}) copy-start(f32[1372]{0:T(1024)} %copy-done.114) | copy-start | bytes 16468
  587.5 12.0 %copy-start.92 = (f32[7,14,14]{2,1,0:T(8,128)S(1)}, f32[7,14,14]{2,1,0:T(8,128)}, u32[]{:S(2)}) copy-start(f32[7,14,14]{2,1,0:T(8,128)} %copy-done.91) | copy-start | bytes 16468
  591.2 11.3 %copy-start.23 = (f32[7,14,14,96]{3,2,1,0:T(8,128)S(1)}, f32[7,14,14,96]{3,2,1,0:T(8,128)}, u32[]{:S(2)}) copy-start(f32[7,14,14,96]{3,2,1,0:T(8,128)} %get-tuple-element.466) | copy-start | bytes 1580548
  591.2 11.3 %copy-start.26 = (f32[7,14,14,96]{3,2,1,0:T(8,128)S(1)}, f32[7,14,14,96]{3,2,1,0:T(8,128)}, u32[]{:S(2)}) copy-start(f32[7,14,14,96]{3,2,1,0:T(8,128)} %reshape.931) | copy-start | bytes 1580548
  591.2 11.3 %copy-start.28 = (f32[7,14,14,96]{3,2,1,0:T(8,128)S(1)}, f32[7,14,14,96]{3,2,1,0:T(8,128)}, u32[]{:S(2)}) copy-start(f32[7,14,14,96]{3,2,1,0:T(8,128)} %copy-done.27) | copy-start | bytes 1580548
  591.2 11.3 %copy-start.78 = (f32[7,14,14]{2,1,0:T(8,128)S(1)}, f32[7,14,14]{2,1,0:T(8,128)}, u32[]{:S(2)}) copy-start(f32[7,14,14]{2,1,0:T(8,128)} %copy-done.77) | copy-start | bytes 16468
  591.2 11.3 %copy-start.82 = (f32[7,14,14]{2,1,0:T(8,128)S(1)}, f32[7,14,14]{2,1,0:T(8,128)}, u32[]{:S(2)}) copy-start(f32[7,14,14]{2,1,0:T(8,128)} %copy-done.81) | copy-start | bytes 16468
  591.2 11.3 %copy-start.84 = (f32[7,14,14]{2,1,0:T(8,128)S(1)}, f32[7,14,14]{2,1,0:T(8,128)}, u32[]{:S(2)}) copy-start(f32[7,14,14]{2,1,0:T(8,128)} %copy-done.83) | copy-start | bytes 16468
  679.2 10.9 %copy-start.6 = (f32[6,343,343]{1,2,0:T(8,128)S(1)}, f32[6,343,343]{1,2,0:T(8,128)}, u32[]{:S(2)}) copy-start(f32[6,343,343]{1,2,0:T(8,128)} %get-tuple-element.166) | copy-start | bytes 8470732
  810.3 10.3 %copy-start.98 = (bf16[96,288,1,1,1,1]{1,0,2,3,4,5:T(8,128)(2,1)S(1)}, bf16[96,288,1,1,1,1]{1,0,2,3,4,5:T(8,128)(2,1)}, u32[]{:S(2)}) copy-start(bf16[96,288,1,1,1,1]{1,0,2,3,4,5:T(8,128)(2,1)} %reshape.1022) | copy-start | bytes 165892
  823.4 7.9 copy-start.44
  825.0 8.2 copy-start.17
  825.2 18.2 %copy-start.101 = (bf16[36864]{0:T(1024)(128)(2,1)S(1)}, bf16[36864]{0:T(1024)(128)(2,1)}, u32[]{:S(2)}) copy-start(bf16[36864]{0:T(1024)(128)(2,1)} %reshape.916) | copy-start | bytes 221188
  825.2 18.2 %copy-start.112 = (bf16[13182]{0:T(1024)(128)(2,1)S(1)}, bf16[13182]{0:T(1024)(128)(2,1)}, u32[]{:S(2)}) copy-start(bf16[13182]{0:T(1024)(128)(2,1)} %reshape.920) | copy-start | bytes 79096
  825.2 18.2 %copy-start.116 = (bf16[9216]{0:T(1024)(128)(2,1)S(1)}, bf16[9216]{0:T(1024)(128)(2,1)}, u32[]{:S(2)}) copy-start(bf16[9216]{0:T(1024)(128)(2,1)} %reshape.915) | copy-start | bytes 55300
  827.9 15.5 %copy-start.145 = (bf16[96]{0:T(256)(128)(2,1)S(1)}, bf16[96]{0:T(256)(128)(2,1)}, u32[]{:S(2)}) copy-start(bf16[96]{0:T(256)(128)(2,1)} %get-tuple-element.455) | copy-start | bytes 580
  827.9 15.5 %copy-start.102 = (bf16[36864]{0:T(1024)(128)(2,1)S(1)}, bf16[36864]{0:T(1024)(128)(2,1)}, u32[]{:S(2)}) copy-start(bf16[36864]{0:T(1024)(128)(2,1)} %reshape.917) | copy-start | bytes 221188
  827.9 15.6 %copy-start.131 = (bf16[96]{0:T(256)(128)(2,1)S(1)}, bf16[96]{0:T(256)(128)(2,1)}, u32[]{:S(2)}) copy-start(bf16[96]{0:T(256)(128)(2,1)} %get-tuple-element.368) | copy-start | bytes 580
  827.9 15.6 %copy-start.138 = (bf16[96]{0:T(256)(128)(2,1)S(1)}, bf16[96]{0:T(256)(128)(2,1)}, u32[]{:S(2)}) copy-start(bf16[96]{0:T(256)(128)(2,1)} %reduce.25) | copy-start | bytes 580
  827.9 15.6 %copy-start.141 = (bf16[96]{0:T(256)(128)(2,1)S(1)}, bf16[96]{0:T(256)(128)(2,1)}, u32[]{:S(2)}) copy-start(bf16[96]{0:T(256)(128)(2,1)} %slice.477) | copy-start | bytes 580
  827.9 15.6 %copy-start.142 = (bf16[96]{0:T(256)(128)(2,1)S(1)}, bf16[96]{0:T(256)(128)(2,1)}, u32[]{:S(2)}) copy-start(bf16[96]{0:T(256)(128)(2,1)} %slice.479) | copy-start | bytes 580
  827.9 15.6 %copy-start.144 = (bf16[384]{0:T(512)(128)(2,1)S(1)}, bf16[384]{0:T(512)(128)(2,1)}, u32[]{:S(2)}) copy-start(bf16[384]{0:T(512)(128)(2,1)} %get-tuple-element.562) | copy-start | bytes 2308
  831.3 17.9 %copy-start.86 = (f32[7,14,14]{2,1,0:T(8,128)S(1)}, f32[7,14,14]{2,1,0:T(8,128)}, u32[]{:S(2)}) copy-start(f32[7,14,14]{2,1,0:T(8,128)} %copy-done.85) | copy-start | bytes 16468
  831.3 55.1 %copy-start.31 = (f32[7,14,14,96]{3,2,1,0:T(8,128)S(1)}, f32[7,14,14,96]{3,2,1,0:T(8,128)}, u32[]{:S(2)}) copy-start(f32[7,14,14,96]{3,2,1,0:T(8,128)} %get-tuple-element.452) | copy-start | bytes 1580548
  831.3 55.1 %copy-start.80 = (f32[7,14,14]{2,1,0:T(8,128)S(1)}, f32[7,14,14]{2,1,0:T(8,128)}, u32[]{:S(2)}) copy-start(f32[7,14,14]{2,1,0:T(8,128)} %copy-done.79) | copy-start | bytes 16468
  848.9 108.8 %all-reduce.51.cloned.1.call-start = ((), (), s32[]{:S(2)}) async-start(), calls=%async_computation | async-start | bytes 253952 | tf_op jit(solution)/shard_map/psum | solution.py:389
  848.9 118.5 %copy-start.63 = (f32[2,31232]{1,0:T(2,128)S(1)}, f32[2,31232]{1,0:T(2,128)}, u32[]{:S(2)}) copy-start(f32[2,31232]{1,0:T(2,128)} %param.19) | copy-start | bytes 749572
  848.9 118.5 %copy-start.103 = (f32[2,31232]{1,0:T(2,128)S(1)}, f32[2,31232]{1,0:T(2,128)}, u32[]{:S(2)}) copy-start(f32[2,31232]{1,0:T(2,128)} %param.20) | copy-start | bytes 749572
  849.0 118.5 %copy-start.104 = (f32[2,31232]{1,0:T(2,128)S(1)}, f32[2,31232]{1,0:T(2,128)}, u32[]{:S(2)}) copy-start(f32[2,31232]{1,0:T(2,128)} %param.21) | copy-start | bytes 749572
  886.3 82.9 %copy-start.1 = (s32[1,56]{1,0:T(1,128)S(1)}, s32[1,56]{1,0:T(1,128)}, u32[]{:S(2)}) copy-start(s32[1,56]{1,0:T(1,128)} %param.18) | copy-start | bytes 676
  (104 other events, 377.2 us)
Sparse Core Ops, SparseCore 0:
  849.0 34.1 all-reduce.52
  887.2 70.3 all-reduce.50

commit v2 on v0

v2 whole, which is shorter than its diff:
```python
import functools

import jax
import jax.numpy as jnp
import numpy as np
from jax import lax
from jax.experimental import pallas as pl
from jax.experimental.pallas import tpu as pltpu
from jax.sharding import PartitionSpec as P

C = 96
HEADS = 6
HEAD = 16
HID = 384
WS = 7
SHIFT = 3
SY = 14
SZ = 14
BPAD = 124928
STEP = 5
EPS_NORM = 1e-05
CLIP_LIMIT = 1.0
LEARN_RATE = 0.4
BETA_FIRST = 0.9
BETA_SECOND = 0.999
WEIGHT_DECAY = 0.05
EPS_ADAM = 1e-08
BIG = 1e30
LOG2E = 1.4426950408889634
LN2 = 0.6931471805599453

CELLS = WS**3
KROW = 352
QLANE = 384
FLAT = BPAD // 128
ROW_PROJ = 216
ROW_ONE = 288
ROW_TWO = 576
ROW_TABLE = 864
ROW_TAIL = 966
V_GAIN1, V_BIAS1, V_BQ, V_BV, V_BPROJ, V_GAIN2, V_BIAS2, V_BHID, V_BOUT = (
    0, 96, 192, 288, 384, 480, 576, 672, 1056,
)

F32 = jnp.float32
BF16 = jnp.bfloat16


def nn(a, b):
    return lax.dot_general(a, b, (((1,), (0,)), ((), ())), preferred_element_type=F32)


def nt(a, b):
    return lax.dot_general(a, b, (((1,), (1,)), ((), ())), preferred_element_type=F32)


def iota(shape, dim):
    return lax.broadcasted_iota(jnp.int32, shape, dim)


def roll(x, by):
    by = by % 128
    return x if by == 0 else pltpu.roll(x, by, 1)


def skew(x, by):
    while by > 0:
        some = min(1 << (by.bit_length() - 1), 16)
        x = pltpu.roll(x, 0, 1, stride=some, stride_axis=0)
        by -= some
    return x


def constant_tables():
    t = np.arange(QLANE)
    live = t < CELLS
    z, x, y = t // 49, t % 49 // 7, t % 7
    ints = np.full((8, QLANE), -1, np.int32)
    for s in range(2):
        for wy in range(2):
            cell_y = (y + 7 * wy + SHIFT * s) % SY
            ints[2 * s + wy] = np.where(live, z * 128 + x * 16 + cell_y, -1)
    ints[4] = np.where(live, z * 128 + t % 49, -1)
    ints[5] = np.where(live, x, -1)
    lane = np.arange(128)
    ints[6, :128] = np.where(lane < 49, 13 * (lane // 7) + lane % 7, -1000)
    marks = np.zeros((64, QLANE), np.float32)
    for i in range(7):
        marks[i] = live & (x == i)
        marks[7 + i] = live & (y == i)
        marks[14 + i] = live & (z == i)
        marks[32 + 7 + i] = live & ((i >= 4) != (y >= 4))
        marks[32 + 14 + i] = live & ((i >= 4) != (z >= 4))
    return jnp.asarray(ints), jnp.asarray(marks, BF16)


def unit_copy(pieces, units):
    out = None
    for at, unit in enumerate(units):
        if unit is None:
            continue
        i, g = unit
        moved = roll(pieces[i], 32 * (at - g))
        group = iota(moved.shape, 1) // 32
        base = jnp.zeros_like(moved) if out is None else out
        out = jnp.where(group == at, moved, base)
    return out


def read_matrix(flat, base, rows, width, store):
    units = width // 32
    if units % 4 == 0:
        step = units // 4
        for o in range(step):
            store(0, 1, o, flat[pl.ds(base + o, rows, stride=step), :])
        return
    groups = rows // 4
    loaded = [flat[pl.ds(base + o, groups, stride=units), :] for o in range(units)]
    for j in range(4):
        for p in range(units // 3):
            first = units * j + 3 * p
            store(j, 4, p, unit_copy(loaded, [divmod(first + s, 4) for s in range(3)] + [None]))


def write_matrix(flat, base, rows, width, load):
    units = width // 32
    if units % 4 == 0:
        step = units // 4
        for o in range(step):
            flat[pl.ds(base + o, rows, stride=step), :] = load(0, 1, o)
        return
    groups = rows // 4
    parts = units // 3
    loaded = [load(j, 4, p) for j in range(4) for p in range(parts)]
    for o in range(units):
        flat[pl.ds(base + o, groups, stride=units), :] = unit_copy(
            loaded, [divmod(4 * o + g, 3) for g in range(4)]
        )


def build_selectors(ints, select, place, spread):
    for s in range(2):
        for wy in range(2):
            need = ints[2 * s + wy : 2 * s + wy + 1, :]
            for r in range(7):
                row = iota((128, QLANE), 0) + 128 * r
                select[s, 128 * r : 128 * r + 128, QLANE * wy : QLANE * wy + QLANE] = jnp.where(
                    row == need, 1.0, 0.0
                ).astype(BF16)
    need = ints[4:5, :]
    for r in range(7):
        row = iota((128, QLANE), 0) + 128 * r
        place[128 * r : 128 * r + 128, :] = jnp.where(row == need, 1.0, 0.0).astype(BF16)
    gap = iota((176, 128), 0) - ints[6:7, :128]
    for k in range(49):
        hit = gap == 84 - 13 * (k // 7) - k % 7
        spread[:, 128 * k : 128 * k + 128] = jnp.where(hit, 1.0, 0.0).astype(BF16)


def table_pick(second):
    row = iota((176, 104), 0)
    col = iota((176, 104), 1) - second
    at = 128 * col
    start = 78 * row
    hit = (start >= at) & (start < at + 128) & (row < 169)
    return jnp.where(hit, 1.0, 0.0).astype(BF16)


def table_start():
    row = iota((176, 128), 0)
    return jnp.bitwise_and(78 * row, 127)


def build_table(flat, spread, place, tiles, table):
    rows = flat[ROW_TABLE : ROW_TABLE + 104, :].astype(BF16)
    first = skew(nn(table_pick(0), rows), 50)
    second = skew(nn(table_pick(1), rows), 50)
    lane = iota((176, 128), 1)
    mixed = jnp.where(lane + table_start() < 128, first, second)
    mixed = jnp.where((lane < 78) & (iota((176, 128), 0) < 169), mixed, 0.0)
    turned = jnp.concatenate([mixed, jnp.zeros((80, 128), F32)], axis=0).T
    cube = turned[:80, :176].astype(BF16)
    for k in range(49):
        tiles[pl.ds(k, 80, stride=56), :] = nn(cube, spread[:, 128 * k : 128 * k + 128])
    for ck in range(7):
        lhs = jnp.concatenate(
            [tiles[336 * (cq - ck + 6) : 336 * (cq - ck + 7), :].astype(BF16) for cq in range(7)],
            axis=1,
        )
        block = nn(lhs, place[...]) * LOG2E
        for h in range(HEADS):
            table[h, 49 * ck : 49 * ck + 49, :] = block[56 * h : 56 * h + 49, :]
    for h in range(HEADS):
        table[h, CELLS:KROW, :] = jnp.full((KROW - CELLS, QLANE), -BIG, F32)


def collapse_table(total, spread, place, tiles, flat):
    tiles[...] = jnp.zeros(tiles.shape, F32)
    for ck in range(7):
        lhs = jnp.concatenate(
            [total[h, 49 * ck : 49 * ck + 56, :] for h in range(HEADS)], axis=0
        ).astype(BF16)
        for cq in range(7):
            dc = cq - ck + 6
            tiles[336 * dc : 336 * dc + 336, :] += nt(lhs, place[128 * cq : 128 * cq + 128, :])
    cube = jnp.zeros((80, 176), F32)
    for k in range(49):
        cube += nt(
            tiles[pl.ds(k, 80, stride=56), :].astype(BF16), spread[:, 128 * k : 128 * k + 128]
        )
    wide = jnp.concatenate([cube, jnp.zeros((80, 80), F32)], axis=1)
    wide = jnp.concatenate([wide, jnp.zeros((48, 256), F32)], axis=0)
    mixed = wide.T[:176, :]
    mixed = skew(mixed, 78)
    fits = iota((176, 128), 1) >= table_start()
    lane = iota((176, 128), 1)
    length = jnp.bitwise_and(lane - table_start(), 127)
    live = (length < 78) & (iota((176, 128), 0) < 169)
    head = jnp.where(fits & live, mixed, 0.0).astype(BF16)
    rest = jnp.where(jnp.logical_not(fits) & live, mixed, 0.0).astype(BF16)

    def tn(a, b):
        return lax.dot_general(a, b, (((0,), (0,)), ((), ())), preferred_element_type=F32)

    return tn(table_pick(0), head) + tn(table_pick(1), rest)


def tail_vector(tail, start, width):
    o, at = divmod(start, 128)
    lane = iota((1, 128), 1)
    out = roll(tail[o : o + 1, :], -at)
    if at + width > 128:
        out = jnp.where(lane < 128 - at, out, roll(tail[o + 1 : o + 2, :], -at))
    return jnp.where(lane < width, out, 0.0)


def prepare(flat, W, wide, spread, place, tiles):
    rows = flat[ROW_TAIL : ROW_TAIL + 16, :]
    lane = iota((9, 128), 1)
    tail = jnp.where(lane < 2, roll(rows[:9], 2), roll(rows[1:10], 2))
    turned = jnp.concatenate([tail, jnp.zeros((119, 128), F32)], axis=0).T
    for o in range(9):
        W["cols"][128 * o : 128 * o + 128, :] = jnp.broadcast_to(turned[:, o : o + 1], (128, 128))

    def into(j, step, p, value):
        wide[p, pl.ds(j, value.shape[0], stride=step), :] = value

    def finish(p, bias):
        wide[p, 96:97, :] = bias
        wide[p, 97:128, :] = jnp.zeros((31, 128), F32)

    read_matrix(flat, 0, C, 3 * C, into)
    finish(0, tail_vector(tail, V_BQ, C))
    finish(1, jnp.zeros((1, 128), F32))
    finish(2, tail_vector(tail, V_BV, C))
    W["q_n"][...] = wide[0, 0:96, :].astype(BF16)
    for p in range(1, 3):
        W["kv_n"][:, 128 * p - 128 : 128 * p] = wide[p, 0:96, :].astype(BF16)
    for p in range(3):
        W["qkv_t"][96 * p : 96 * p + 96, :] = wide[p, 0:128, :].T[:96].astype(BF16)

    read_matrix(flat, ROW_PROJ, C, C, into)
    finish(0, tail_vector(tail, V_BPROJ, C))
    W["proj_n"][...] = wide[0, 0:96, :].astype(BF16)
    W["proj_t"][...] = wide[0, 0:128, :].T[:96].astype(BF16)

    read_matrix(flat, ROW_ONE, C, HID, into)
    for p in range(3):
        finish(p, tail_vector(tail, V_BHID + 128 * p, 128))
        W["one_n"][:, 128 * p : 128 * p + 128] = wide[p, 0:96, :].astype(BF16)
        W["one_t"][128 * p : 128 * p + 128, :] = wide[p, 0:128, :].T.astype(BF16)

    read_matrix(flat, ROW_TWO, HID, C, into)
    W["two_n"][...] = wide[0].astype(BF16)
    for p in range(3):
        W["two_t"][:, 128 * p : 128 * p + 128] = wide[0, 128 * p : 128 * p + 128, :].T[:96].astype(
            BF16
        )
    build_table(flat, spread, place, tiles, W["table"])


WEIGHT_SHAPES = dict(
    cols=((1152, 128), F32),
    q_n=((96, 128), BF16),
    kv_n=((96, 256), BF16),
    qkv_t=((288, 128), BF16),
    proj_n=((96, 128), BF16),
    proj_t=((96, 128), BF16),
    one_n=((96, 384), BF16),
    one_t=((384, 128), BF16),
    two_n=((384, 128), BF16),
    two_t=((96, 384), BF16),
    table=((HEADS, KROW, QLANE), F32),
)


SAVED_SHAPES = dict(
    normed=((128, QLANE), BF16),
    hat=((96, QLANE), F32),
    scale=((8, QLANE), F32),
    qkv=((288, QLANE), BF16),
    probs=((HEADS, KROW, QLANE), BF16),
    inverse=((8, QLANE), F32),
    attended=((128, QLANE), BF16),
    hat_two=((96, QLANE), F32),
    scale_two=((8, QLANE), F32),
    normed_two=((128, QLANE), BF16),
    slope=((HID, QLANE), BF16),
    active=((HID, QLANE), BF16),
)

GRAD_SHAPES = dict(
    q=((112, 128), F32),
    kv=((2, 112, 128), F32),
    proj=((112, 128), F32),
    one=((112, 384), F32),
    two=((400, 128), F32),
    gain1=((96, 128), F32),
    bias1=((96, 128), F32),
    gain2=((96, 128), F32),
    bias2=((96, 128), F32),
    total=((HEADS, KROW, QLANE), F32),
)


def column(W, start, rows=96):
    part = W["cols"][start : start + rows, :]
    return jnp.concatenate([part, part, part], axis=1)


def extended(rows):
    width = rows.shape[1]
    return jnp.concatenate([rows, jnp.ones((16, width), BF16), jnp.zeros((16, width), BF16)], axis=0)


def standardize(x):
    centered = x - jnp.mean(x, axis=0, keepdims=True)
    variance = jnp.mean(centered * centered, axis=0, keepdims=True)
    scale = lax.rsqrt(variance + EPS_NORM)
    return centered * scale, scale


def at_head(h, rows, tail):
    width = rows.shape[1]
    parts = []
    if h > 0:
        parts.append(jnp.zeros((16 * h, width), BF16))
    parts.append(rows)
    if h < HEADS - 1:
        parts.append(jnp.zeros((16 * (HEADS - 1 - h), width), BF16))
    return jnp.concatenate(parts + [tail], axis=0)


def scaled_queries(qkv):
    return (qkv[0:96].astype(F32) * (HEAD**-0.5 * LOG2E)).astype(BF16)


def window_forward(x, W, S, s, marks, barred):
    hat, scale = standardize(x)
    S["hat"][s] = hat
    S["scale"][s, 0:1] = scale
    normed = extended((hat * column(W, V_GAIN1) + column(W, V_BIAS1)).astype(BF16))
    S["normed"][s] = normed
    qkv = nn(W["qkv_t"][...], normed).astype(BF16)
    S["qkv"][s] = qkv
    queries = scaled_queries(qkv)
    keys = jnp.concatenate([qkv[96:192], marks[0:32, :]], axis=0).T[:KROW]
    ones = jnp.ones((16, KROW), BF16)
    parts = []
    for h in range(HEADS):
        scores = nn(keys, at_head(h, queries[16 * h : 16 * h + 16], barred)) + W["table"][h]
        highest = jnp.max(scores, axis=0, keepdims=True)
        probs = jnp.exp2(scores - highest).astype(BF16)
        S["probs"][s, h] = probs
        values = jnp.concatenate([qkv[192 + 16 * h : 208 + 16 * h, :KROW], ones], axis=0)
        mixed = nn(values, probs)
        inverse = 1.0 / mixed[16:17]
        S["inverse"][s, h : h + 1] = inverse
        parts.append((mixed[:16] * inverse).astype(BF16))
    attended = extended(jnp.concatenate(parts, axis=0))
    S["attended"][s] = attended
    branch = nn(W["proj_t"][...], attended).astype(BF16)
    middle = x + branch.astype(F32)
    hat, scale = standardize(middle)
    S["hat_two"][s] = hat
    S["scale_two"][s, 0:1] = scale
    normed_two = extended((hat * column(W, V_GAIN2) + column(W, V_BIAS2)).astype(BF16))
    S["normed_two"][s] = normed_two
    hidden = nn(W["one_t"][...], normed_two)
    share = 0.5 + 0.5 * lax.erf(hidden * (0.5**0.5))
    active = (hidden * share).astype(BF16)
    S["active"][s] = active
    slope = share + hidden * jnp.exp2(hidden * hidden * (-0.5 * LOG2E)) * 0.3989422804014327
    S["slope"][s] = slope.astype(BF16)
    return middle + nn(W["two_t"][...], active) + column(W, V_BOUT)


def fold(x):
    return x[:, 0:128] + x[:, 128:256] + x[:, 256:384]


def norm_backward(grad, hat, scale, gain):
    scaled = grad * gain
    mean_one = jnp.mean(scaled, axis=0, keepdims=True)
    mean_two = jnp.mean(scaled * hat, axis=0, keepdims=True)
    return scale * (scaled - mean_one - hat * mean_two)


def window_backward(grad, W, S, s, G, marks, barred):
    result = extended(grad.astype(BF16))
    active = S["active"][s]
    G["two"][...] += nt(jnp.concatenate([active, jnp.ones((16, QLANE), BF16)], axis=0), result)
    hidden = (nn(W["two_n"][...], result) * S["slope"][s].astype(F32)).astype(BF16)
    G["one"][...] += nt(S["normed_two"][s, 0:112], hidden)
    d_normed = nn(W["one_n"][...], hidden)
    hat = S["hat_two"][s]
    G["gain2"][...] += fold(d_normed * hat)
    G["bias2"][...] += fold(d_normed)
    d_middle = grad + norm_backward(d_normed, hat, S["scale_two"][s, 0:1], column(W, V_GAIN2))
    d_branch = extended(d_middle.astype(BF16))
    attended = S["attended"][s]
    G["proj"][...] += nt(attended[0:112], d_branch)
    d_attended = nn(W["proj_n"][...], d_branch).astype(BF16).astype(F32)
    product = d_attended * attended[0:96].astype(F32)
    qkv = S["qkv"][s]
    queries = scaled_queries(qkv)
    values = extended(qkv[192:288]).T[:KROW]
    d_keys = jnp.zeros((KROW, 128), F32)
    d_values = jnp.zeros((KROW, 128), F32)
    parts = []
    for h in range(HEADS):
        inverse = S["inverse"][s, h : h + 1]
        inner = jnp.sum(product[16 * h : 16 * h + 16], axis=0, keepdims=True) * inverse
        high = inner.astype(BF16)
        low = (inner - high.astype(F32)).astype(BF16)
        row = iota((32, QLANE), 0)
        less = jnp.where(row == 0, -high.astype(F32), jnp.where(row == 1, -low.astype(F32), 0.0))
        d_out = at_head(
            h, (d_attended[16 * h : 16 * h + 16] * inverse).astype(BF16), less.astype(BF16)
        )
        probs = S["probs"][s, h]
        d_scores = probs * nn(values, d_out).astype(BF16)
        G["total"][h] += d_scores.astype(F32)
        d_values += nt(probs, d_out)
        d_keys += nt(d_scores, at_head(h, queries[16 * h : 16 * h + 16], jnp.zeros_like(barred)))
        parts.append(nn(qkv[96 + 16 * h : 112 + 16 * h, :KROW], d_scores))
    d_queries = (jnp.concatenate(parts, axis=0) * HEAD**-0.5).astype(BF16)
    live = iota((KROW, 128), 1) < 96
    d_pair = jnp.concatenate(
        [jnp.where(live, d_keys * LN2, 0.0), jnp.where(live, d_values, 0.0)], axis=1
    ).astype(BF16)
    normed = S["normed"][s, 0:112]
    G["q"][:, 0:96] += nt(normed, d_queries)
    both = nn(normed[:, :KROW], d_pair)
    for p in range(2):
        G["kv"][p] += both[:, 128 * p : 128 * p + 128]
    d_pair = jnp.concatenate([d_pair, jnp.zeros((QLANE - KROW, 256), BF16)], axis=0)
    d_normed = nn(W["q_n"][:, 0:96], d_queries) + nt(W["kv_n"][...], d_pair)
    hat = S["hat"][s]
    G["gain1"][...] += fold(d_normed * hat)
    G["bias1"][...] += fold(d_normed)
    return d_middle + norm_backward(d_normed, hat, S["scale"][s, 0:1], column(W, V_GAIN1))


def finish_gradients(G, flat, wide, spread, place, tiles):
    def qkv_rows(j, step, p):
        if p == 0:
            return G["q"][pl.ds(j, 24, stride=4), :]
        return G["kv"][p - 1, pl.ds(j, 24, stride=4), :]

    write_matrix(flat, 0, C, 3 * C, qkv_rows)
    write_matrix(flat, ROW_PROJ, C, C, lambda j, step, p: G["proj"][pl.ds(j, 24, stride=4), :])
    write_matrix(
        flat, ROW_ONE, C, HID, lambda j, step, p: G["one"][0:96, 128 * p : 128 * p + 128]
    )
    write_matrix(flat, ROW_TWO, HID, C, lambda j, step, p: G["two"][pl.ds(j, 96, stride=4), :])
    lane = iota((96, 128), 1)
    columns = jnp.zeros((96, 128), F32)
    for at, name in enumerate(["gain1", "bias1", "gain2", "bias2"]):
        columns = jnp.where(lane == at, jnp.sum(G[name][...], axis=1, keepdims=True), columns)
    turned = jnp.concatenate([columns, jnp.zeros((32, 128), F32)], axis=0).T
    sources = [
        (turned[0:1], 3),
        (turned[1:2], 3),
        (G["q"][96:97, :], 3),
        (G["kv"][1, 96:97, :], 3),
        (G["proj"][96:97, :], 3),
        (turned[2:3], 3),
        (turned[3:4], 3),
        (G["one"][96:97, 0:128], 4),
        (G["one"][96:97, 128:256], 4),
        (G["one"][96:97, 256:384], 4),
        (G["two"][384:385, :], 3),
    ]
    pieces = [source for source, _ in sources]
    units = [(i, g) for i, (_, count) in enumerate(sources) for g in range(count)]
    tail = jnp.concatenate(
        [unit_copy(pieces, units[4 * o : 4 * o + 4]) for o in range(9)], axis=0
    )
    table = collapse_table(G["total"], spread, place, tiles, flat)
    flat[ROW_TABLE:ROW_TAIL, :] = table[0:102]
    none = jnp.zeros((1, 128), F32)
    moved = roll(jnp.concatenate([none, tail, none], axis=0), 126)
    lane = iota((10, 128), 1)
    mixed = jnp.where(lane >= 126, moved[1:11], moved[0:10])
    first = jnp.where(iota((1, 128), 1) >= 126, mixed[0:1], table[102:103])
    flat[ROW_TAIL:FLAT, :] = jnp.concatenate([first, mixed[1:10]], axis=0)


def round_up(value, to):
    return -(-value // to) * to


def take_grid(row_of, square, tall, grid, wrapped):
    for x in range(7):
        square[16 * x : 16 * x + 14, 0 : SZ * C] = row_of(x)
    for i in range(11):
        tall[128 * i : 128 * i + 128, :] = square[:, 128 * i : 128 * i + 128].T
    for z in range(SZ + 3 if wrapped else SZ):
        grid[:, 128 * z : 128 * z + 128] = tall[C * (z % SZ) : C * (z % SZ) + C, :].astype(BF16)


def take_window(grid, select, s, wy, wz):
    rows = grid[:, pl.ds(pl.multiple_of(896 * wz + 384 * s, 128), 896)]
    return nn(rows, select[s, :, pl.ds(pl.multiple_of(QLANE * wy, 128), QLANE)])


def give_grid(windows, select, s, put):
    for wz in range(2):
        both = jnp.concatenate([windows[wz], windows[2 + wz]], axis=1).astype(BF16)
        cells = nt(both, select[s])
        for r in range(7):
            put((r + 7 * wz + SHIFT * s) % SZ, cells[:, 128 * r : 128 * r + 128])


def give_rows(tall, square):
    for i in range(11):
        square[:, 128 * i : 128 * i + 128] = tall[128 * i : 128 * i + 128, :].T


def crop_bars(crop, ints, first, total):
    ids = [crop[0, lax.rem(first + a, total)] for a in range(7)]
    at = ints[5:6, :]
    own = jnp.zeros((1, QLANE), jnp.int32)
    for a in range(7):
        own = jnp.where(at == a, ids[a], own)
    row = iota((32, QLANE), 0)
    key = jnp.full((32, QLANE), -1, jnp.int32)
    for a in range(7):
        key = jnp.where(row == a, ids[a], key)
    return jnp.where((row < 7) & (key != own), -BIG, 0.0)


def shift_bars(marks, wy, wz):
    row = iota((32, QLANE), 0)
    factor = jnp.where(row < 14, wy, wz).astype(F32) * -BIG
    return marks[32:64, :].astype(F32) * factor


def step_kernel(n_win, n_fsdp, names, *refs):
    R = dict(zip(names, refs))
    W = {k: R["w_" + k] for k in WEIGHT_SHAPES}
    S = {k: R["s_" + k] for k in SAVED_SHAPES}
    G = {k: R["g_" + k] for k in GRAD_SHAPES}
    tokens, cotangent, crop = R["tokens"], R["cotangent"], R["crop"]
    ints, marks = R["ints"], R["marks"]
    select, place, spread = R["select"], R["place"], R["spread"]
    flat, wide, tiles = R["flat"], R["wide"], R["tiles"]
    square, tall = R["square"], R["tall"]
    send, recv = R["send"], R["recv"]
    shard = FLAT // n_fsdp
    extent = tokens.shape[0]
    total = n_win * extent
    me_win, me_fsdp = lax.axis_index("win"), lax.axis_index("fsdp")
    left, right = lax.rem(me_win + n_win - 1, n_win), lax.rem(me_win + 1, n_win)
    used = [0]

    def remote(src, dst, axis, to):
        slot = used[0]
        used[0] += 1
        copy = pltpu.make_async_remote_copy(
            src_ref=src,
            dst_ref=dst,
            send_sem=send.at[slot],
            recv_sem=recv.at[slot],
            device_id={axis: to},
            device_id_type=pl.DeviceIdType.MESH,
        )
        copy.start()
        return copy

    def to_all(axis, me, count, src_of, dst):
        copies = []
        for k in range(1, count):
            to = lax.rem(me + k, count)
            copies.append(remote(src_of(to), dst, axis, to))
        return copies

    def neighbour(src, dst, to):
        if n_win > 1:
            return [remote(src, dst, "win", to)]
        dst[...] = src[...]
        return []

    def wait(copies):
        for copy in copies:
            copy.wait()

    if n_win * n_fsdp > 1:
        barrier = pltpu.get_barrier_semaphore()
        for axis, me, count in (("fsdp", me_fsdp, n_fsdp), ("win", me_win, n_win)):
            for k in range(1, count):
                pl.semaphore_signal(
                    barrier,
                    inc=1,
                    device_id={axis: lax.rem(me + k, count)},
                    device_id_type=pl.DeviceIdType.MESH,
                )
        pl.semaphore_wait(barrier, n_win + n_fsdp - 2)

    gathered = R["gathered"]
    weights_in = []
    for b in range(2):
        gathered[me_fsdp, b, 0:shard, :] = R["params"][pl.ds(b, shard, stride=2), :].astype(BF16)
        mine = gathered.at[me_fsdp, b]
        weights_in.append(to_all("fsdp", me_fsdp, n_fsdp, lambda to: mine, mine))
    R["edge"][...] = cotangent[0:SHIFT]
    halo_in = neighbour(R["edge"], R["edge_in"], left)

    build_selectors(ints, select, place, spread)
    square[...] = jnp.zeros(square.shape, F32)
    take_grid(lambda x: tokens[x].astype(F32), square, tall, R["grid"], False)

    def spread_weights(b):
        wait(weights_in[b])
        for f in range(n_fsdp):
            flat[shard * f : shard * f + shard, :] = gathered[f, b, 0:shard, :].astype(F32)
        prepare(flat, W, wide, spread, place, tiles)

    spread_weights(0)
    windows, deltas = R["windows"], R["deltas"]
    R["bars"][...] = crop_bars(crop, ints, me_win * extent, total)

    def first_forward(w, carry):
        x = take_window(R["grid"], select, 0, w // 2, lax.rem(w, 2))
        windows[w] = window_forward(x, W, S, w, marks, R["bars"][...].astype(BF16))
        return carry

    lax.fori_loop(0, 4, first_forward, 0)

    halo, halo_back = R["halo"], R["halo_back"]
    kept = R["kept"]
    lane = iota((C, 128), 1)

    def first_slices(z, value):
        kept[z] = value

    give_grid(windows, select, 0, first_slices)
    for i in range(7):
        pair = jnp.where(lane < 64, kept[2 * i], roll(kept[2 * i + 1], 64))
        halo[:, 128 * i : 128 * i + 128] = pair.astype(BF16)
    slab_in = neighbour(halo, R["halo_in"], left)
    first_weights = {}
    for k in ("cols", "q_n", "kv_n", "proj_n", "one_n", "two_n"):
        R["k_" + k][...] = W[k][...]
        first_weights[k] = R["k_" + k]
    spread_weights(1)
    wait(halo_in)

    def shifted_cotangent(x):
        return (cotangent[x + SHIFT] if x < 7 - SHIFT else R["edge_in"][x - 7 + SHIFT]).astype(F32)

    take_grid(shifted_cotangent, square, tall, R["grid_two"], True)
    wait(slab_in)
    for z in range(SZ + 3):
        pair = R["halo_in"][:, 128 * (z % SZ // 2) : 128 * (z % SZ // 2) + 128].astype(F32)
        if z % SZ % 2 == 0:
            pair = roll(pair, 64)
        joined = jnp.where(lane < 64, roll(kept[z % SZ], -48), pair)
        R["grid"][:, 128 * z : 128 * z + 128] = joined.astype(BF16)

    def clear(ref):
        ref[...] = jnp.zeros(ref.shape, ref.dtype)

    for ref in G.values():
        clear(ref)
    R["bars"][...] = crop_bars(crop, ints, me_win * extent + SHIFT, total)

    def second(w, carry):
        wy, wz = w // 2, lax.rem(w, 2)
        bars = (R["bars"][...] + shift_bars(marks, wy, wz)).astype(BF16)
        x = take_window(R["grid"], select, 1, wy, wz)
        windows[w] = window_forward(x, W, S, 4, marks, bars)
        grad = take_window(R["grid_two"], select, 1, wy, wz)
        deltas[w] = window_backward(grad, W, S, 4, G, marks, bars)
        return carry

    lax.fori_loop(0, 4, second, 0)

    def put_kept(z, value):
        kept[z] = value

    give_grid(deltas, select, 1, put_kept)
    for i in range(7):
        pair = jnp.where(lane < 64, roll(kept[2 * i], 64), kept[2 * i + 1])
        halo_back[:, 128 * i : 128 * i + 128] = pair.astype(BF16)
    slab_back = neighbour(halo_back, R["halo_back_in"], right)

    def put_tall(z, value):
        tall[C * z : C * z + C, :] = value

    give_grid(windows, select, 1, put_tall)
    give_rows(tall, square)
    for x in range(7 - SHIFT):
        R["block_out"][x + SHIFT] = square[16 * x : 16 * x + 14, 0 : SZ * C].astype(BF16)
    for x in range(SHIFT):
        at = 16 * (x + 7 - SHIFT)
        R["edge"][x] = square[at : at + 14, 0 : SZ * C].astype(BF16)
    out_back = neighbour(R["edge"], R["edge_back"], right)

    piece = R["sums"].shape[1] // n_win
    padded = R["sums"].shape[1]

    def scatter(b):
        finish_gradients(G, flat, wide, spread, place, tiles)
        for f in range(n_fsdp):
            R["outgoing"][b, f, 0:shard, :] = flat[shard * f : shard * f + shard, :].astype(BF16)
            if padded > shard:
                R["outgoing"][b, f, shard:padded, :] = jnp.zeros((padded - shard, 128), BF16)
        return to_all(
            "fsdp",
            me_fsdp,
            n_fsdp,
            lambda to: R["outgoing"].at[b, to],
            R["incoming"].at[b, me_fsdp],
        )

    def add_fsdp(b, copies):
        wait(copies)
        R["incoming"][b, me_fsdp] = R["outgoing"][b, me_fsdp]
        total_rows = R["incoming"][b, 0].astype(F32)
        for f in range(1, n_fsdp):
            total_rows += R["incoming"][b, f].astype(F32)
        R["sums"][b] = total_rows.astype(BF16)
        return to_all(
            "win",
            me_win,
            n_win,
            lambda to: R["sums"].at[b, pl.ds(pl.multiple_of(piece * to, 16), piece)],
            R["parts"].at[b, me_win],
        )

    def add_win(b, copies):
        wait(copies)
        own = pl.ds(pl.multiple_of(piece * me_win, 16), piece)
        R["parts"][b, me_win] = R["sums"][b, own, :]
        total_rows = R["parts"][b, 0].astype(F32)
        for w in range(1, n_win):
            total_rows += R["parts"][b, w].astype(F32)
        R["whole"][b, own, :] = total_rows.astype(BF16)
        mine = R["whole"].at[b, own]
        return to_all("win", me_win, n_win, lambda to: mine, mine)

    first_scatter = scatter(1)
    wait(slab_back)
    wait(out_back)
    R["block_out"][0:SHIFT] = R["edge_back"][...]
    for z in range(SZ):
        pair = R["halo_back_in"][:, 128 * (z // 2) : 128 * (z // 2) + 128].astype(F32)
        if z % 2 == 1:
            pair = roll(pair, 64)
        joined = jnp.where(lane < 48, pair, roll(kept[z], 48))
        R["grid"][:, 128 * z : 128 * z + 128] = joined.astype(BF16)
    for ref in G.values():
        clear(ref)
    W0 = {**W, **first_weights}

    def first_backward(w, carry):
        grad = take_window(R["grid"], select, 0, w // 2, lax.rem(w, 2))
        deltas[w] = window_backward(grad, W0, S, w, G, marks, R["bars"][...].astype(BF16))
        return carry

    lax.fori_loop(0, 4, first_backward, 0)
    second_scatter = scatter(0)
    give_grid(deltas, select, 0, put_tall)
    give_rows(tall, square)
    for x in range(7):
        R["input_grad"][x] = square[16 * x : 16 * x + 14, 0 : SZ * C].astype(BF16)
    first_sum = add_fsdp(1, first_scatter)
    second_sum = add_fsdp(0, second_scatter)
    first_whole = add_win(1, first_sum)
    second_whole = add_win(0, second_sum)
    wait(first_whole)
    wait(second_whole)

    squares = jnp.zeros((1, 1), F32)
    for b in range(2):
        rows = R["whole"][b, 0:shard, :].astype(F32)
        squares += jnp.sum(jnp.sum(rows * rows, axis=0, keepdims=True), axis=1, keepdims=True)
    R["norms"][me_fsdp] = jnp.broadcast_to(squares, (8, 128))
    mine = R["norms"].at[me_fsdp]
    wait(to_all("fsdp", me_fsdp, n_fsdp, lambda to: mine, mine))
    norm = R["norms"][0]
    for f in range(1, n_fsdp):
        norm += R["norms"][f]
    norm = jnp.sqrt(norm)
    R["grad_norm"][...] = norm
    factor = jnp.minimum(1.0, CLIP_LIMIT / (norm + 1e-06))[0:1]
    for b in range(2):
        at = pl.ds(b, shard, stride=2)
        clipped = R["whole"][b, 0:shard, :].astype(F32) * factor
        new_first = BETA_FIRST * R["first"][at, :] + (1.0 - BETA_FIRST) * clipped
        new_second = BETA_SECOND * R["second"][at, :] + (1.0 - BETA_SECOND) * clipped * clipped
        first_hat = new_first / (1.0 - BETA_FIRST**STEP)
        second_hat = new_second / (1.0 - BETA_SECOND**STEP)
        params = R["params"][at, :]
        R["new_params"][at, :] = params - LEARN_RATE * (
            first_hat / (jnp.sqrt(second_hat) + EPS_ADAM) + WEIGHT_DECAY * params
        )
        R["new_first"][at, :] = new_first
        R["new_second"][at, :] = new_second


def interleave(rows):
    return rows.reshape(2, -1, 128).transpose(1, 0, 2).reshape(-1, 128)


def separate(rows):
    return rows.reshape(-1, 2, 128).transpose(1, 0, 2).reshape(2, -1)


def per_device(n_win, n_fsdp, tokens, cotangent, crop_ids, params, first_moment, second_moment):
    ints, marks = constant_tables()
    extent = tokens.shape[1]
    shard = FLAT // n_fsdp
    held = round_up(shard, 16)
    padded = round_up(-(-shard // n_win), 16) * n_win
    rows = jax.ShapeDtypeStruct((2 * shard, 128), F32)
    cells = jax.ShapeDtypeStruct((extent, SY, SZ * C), BF16)
    inputs = dict(
        tokens=tokens[0],
        cotangent=cotangent[0],
        crop=crop_ids,
        ints=ints,
        marks=marks,
        params=interleave(params),
        first=interleave(first_moment),
        second=interleave(second_moment),
    )
    outputs = dict(
        block_out=cells,
        input_grad=cells,
        grad_norm=jax.ShapeDtypeStruct((8, 128), F32),
        new_params=rows,
        new_first=rows,
        new_second=rows,
    )
    V = pltpu.VMEM
    edge = V((SHIFT, SY, SZ * C), BF16)
    scratch = dict(
        gathered=V((n_fsdp, 2, held, 128), BF16),
        edge=edge,
        edge_in=edge,
        edge_back=edge,
        halo=V((C, 896), BF16),
        halo_in=V((C, 896), BF16),
        halo_back=V((C, 896), BF16),
        halo_back_in=V((C, 896), BF16),
        outgoing=V((2, n_fsdp, padded, 128), BF16),
        incoming=V((2, n_fsdp, padded, 128), BF16),
        sums=V((2, padded, 128), BF16),
        parts=V((2, n_win, padded // n_win, 128), BF16),
        whole=V((2, padded, 128), BF16),
        norms=V((n_fsdp, 8, 128), F32),
        select=V((2, 896, 2 * QLANE), BF16),
        place=V((896, QLANE), BF16),
        spread=V((176, 49 * 128), BF16),
        flat=V((FLAT + 8, 128), F32),
        wide=V((3, 384, 128), F32),
        tiles=V((80 * 56, 128), F32),
        square=V((128, 1408), F32),
        tall=V((1408, 128), F32),
        grid=V((C, 17 * 128), BF16),
        grid_two=V((C, 17 * 128), BF16),
        kept=V((SZ, C, 128), F32),
        windows=V((4, C, QLANE), F32),
        deltas=V((4, C, QLANE), F32),
        bars=V((32, QLANE), F32),
    )
    for k, (shape, kind) in WEIGHT_SHAPES.items():
        scratch["w_" + k] = V(shape, kind)
    for k in ("cols", "q_n", "kv_n", "proj_n", "one_n", "two_n"):
        scratch["k_" + k] = V(*WEIGHT_SHAPES[k])
    for k, (shape, kind) in SAVED_SHAPES.items():
        scratch["s_" + k] = V((5, *shape), kind)
    for k, (shape, kind) in GRAD_SHAPES.items():
        scratch["g_" + k] = V(shape, kind)
    copies = 5 * (n_fsdp - 1) + 4 * (n_win - 1) + 4
    scratch["send"] = pltpu.SemaphoreType.DMA((copies,))
    scratch["recv"] = pltpu.SemaphoreType.DMA((copies,))
    names = [*inputs, *outputs, *scratch]
    vmem = pl.BlockSpec(memory_space=pltpu.VMEM)
    results = pl.pallas_call(
        functools.partial(step_kernel, n_win, n_fsdp, names),
        out_shape=tuple(outputs.values()),
        in_specs=[
            pl.BlockSpec(memory_space=pltpu.SMEM) if k == "crop" else vmem for k in inputs
        ],
        out_specs=tuple(vmem for _ in outputs),
        scratch_shapes=list(scratch.values()),
        compiler_params=pltpu.CompilerParams(
            collective_id=0 if n_win * n_fsdp > 1 else None,
            has_side_effects=True,
            vmem_limit_bytes=66 * 1024 * 1024 - 2 * 1024 * 1024,
        ),
        name="layer_step",
    )(*inputs.values())
    block_out, input_grad, grad_norm, new_params, new_first, new_second = results
    new_params = separate(new_params)
    return (
        block_out[None],
        input_grad[None],
        grad_norm[0, 0],
        new_params,
        separate(new_first),
        separate(new_second),
        new_params.astype(BF16),
    )


def solution(mesh):
    data = P("fsdp", "win", None, None)
    state = P(None, "fsdp")
    return jax.shard_map(
        functools.partial(per_device, mesh.shape["win"], mesh.shape["fsdp"]),
        mesh=mesh,
        in_specs=(data, data, P("fsdp", None), state, state, state),
        out_specs=(data, data, P(), state, state, state, state),
        check_vma=False,
    )
```

time: 2840 us -> 126 us (0.04)
  other arithmetic: 1370 us -> 0.93 us
  local copies, waits for them, and re-layouts: 1200 us -> 10.2 us
  Pallas kernels: 0 us -> 114 us
  waiting for transfers between devices: 98 us -> 0 us
  matrix products: 95.9 us -> 0 us
    scatter-add x2 -> x0, other arithmetic: 1250 us -> none  [block_backward(): jax.ops.segment_sum(d_table_full.transpose(1, 2, 0).reshape(-1, HEADS), r...]
    gather x6 -> x0, local copies, waits for them, and re-layouts: 863 us -> none  [the longest x4 861 us: block_forward(): table_bias = jnp.take(bias_table, rel_index, axis=0).astype(jnp.float32)]
    pallas_call x0 -> x1, Pallas kernels: none -> 114 us  [per_device(): pl.pallas_call(functools.partial(step_kernel, n_win, n_fsdp, names), out_...]
    dot_general x52 -> x0, matrix products: 95.9 us -> none  [the longest x4 16 us: one_group(): jnp.einsum('wqhd,wkhd->whqk', block_grad, value_rows, preferred_element_t...]
    reshape x35 -> x7, local copies, waits for them, and re-layouts: 97.4 us -> 3.58 us  [the longest x4 2.03 us: separate(): return rows.reshape(-1, 2, 128).transpose(1, 0, 2).reshape(2, -1)]
    psum x1 -> x0, waiting for transfers between devices: 67.2 us -> none  [reduce_block(): summed = lax.psum(flat_grad.astype(jnp.bfloat16), 'win')]
    another operation x27 -> x0, local copies, waits for them, and re-layouts: 64.9 us -> none
    reduce_sum x33 -> x0, other arithmetic: 63.6 us -> none  [the longest x4 29.2 us: one_group(): jnp.sum(d_scores.astype(jnp.float32), axis=0)]
  transfers between devices with their start and end apart: 6 -> 0, of which waited for: 2 -> 0; matrix products, arithmetic and copies ran while one was open for 25% -> 0% of each run, Pallas kernels for 0% -> 0%
where the time goes in v2:
time: 126 us
  Pallas kernels  114 us (90%)
  local copies, waits for them, and re-layouts  10.2 us (8%)
    pallas_call x1, Pallas kernels, per_device(): pl.pallas_call(functools.partial(step_kernel, n_win, n_fsdp, names), out_...  114 us
    unnamed x14, local copies, waits for them, and re-layouts  2.98 us

profile of v2, /device:TPU:0, one launch (start us, length us, event | category | flops | bytes accessed | tf_op | source)
XLA Modules:
  0.0 125.8 jit_solution(12204680065849429037)
XLA Ops:
  0.6 1.1 reshape.50
  1.8 0.0 copy-start.2
  1.8 0.8 copy.21
  2.6 0.1 copy-done.2
  2.7 0.2 reshape.52
  2.9 0.0 copy-start.3
  2.9 0.8 copy.22
  3.8 0.1 copy-done.3
  3.9 0.2 reshape.54
  4.1 0.8 copy.23
  4.9 114.0 %layer_step.1 = (bf16[7,14,1344]{2,1,0:T(8,128)(2,1)}, bf16[7,14,1344]{2,1,0:T(8,128)(2,1)}, f32[8,128]{1,0:T(8,128)}, f32[488,128]{1,0:T(8,128)}, f32[488,128]{1,0:T(8,128)}, /*index=5*/f32[488,128]{1,0:T(8,128)}) custom-call(bf16[7,14,1344]{2,1,0:T(8,128)(2,1)} %bitcast.42, bf16[7,14,1344]{2,1,0:T(8,128)(2,1)} %bitcast.43, s32[1,56]{1,0:T(1,128)} %refs_2_.1, ...), custom_call_target="tpu_custom_call" | custom-call | tf_op jit(solution)/shard_map/layer_step/pallas_call | solution.py:903
  118.9 1.2 slice.3
  120.1 1.0 copy.39
  121.0 0.0 copy-start.5
  121.0 0.9 fusion
  122.0 0.0 copy-done.5
  122.0 0.0 copy-start.4
  122.0 0.9 copy-done.4
  123.0 0.0 copy-start.1
  123.0 1.0 copy_bitcast_fusion.3
  124.0 0.0 copy-done.1
  124.0 0.0 copy-start
  124.0 0.7 copy.42
  124.7 0.4 copy-done
  125.1 0.7 copy.43
  (2 shorter events, 0.0 us)
Async XLA Ops:
  1.8 0.9 copy-start.2
  2.9 0.9 copy-start.3
  121.0 0.9 copy-start.5
  122.0 0.9 copy-start.4
  123.0 1.0 copy-start.1
  124.0 1.1 copy-start

commit v3 on v2

--- a/solution.py
+++ b/solution.py
@@ -1,4 +1,5 @@
 import functools
+from types import SimpleNamespace as Names
 
 import jax
 import jax.numpy as jnp
@@ -180,14 +181,30 @@
     mixed = jnp.where((lane < 78) & (iota((176, 128), 0) < 169), mixed, 0.0)
     turned = jnp.concatenate([mixed, jnp.zeros((80, 128), F32)], axis=0).T
     cube = turned[:80, :176].astype(BF16)
-    for k in range(49):
-        tiles[pl.ds(k, 80, stride=56), :] = nn(cube, spread[:, 128 * k : 128 * k + 128])
-    for ck in range(7):
-        lhs = jnp.concatenate(
-            [tiles[336 * (cq - ck + 6) : 336 * (cq - ck + 7), :].astype(BF16) for cq in range(7)],
+    for k in range(0, 49, 2):
+        some = min(2, 49 - k)
+        block = nn(cube, spread[:, 128 * k : 128 * k + 128 * some])
+        for i in range(some):
+            tiles[pl.ds(k + i, 80, stride=56), :] = block[:, 128 * i : 128 * i + 128]
+
+    def gathered(ck, first, last):
+        return jnp.concatenate(
+            [
+                tiles[336 * (cq - ck + 6) : 336 * (cq - ck + 7), :].astype(BF16)
+                for cq in range(first, last)
+            ],
             axis=1,
         )
-        block = nn(lhs, place[...]) * LOG2E
+
+    for ck in range(7):
+        block = jnp.concatenate(
+            [
+                nn(gathered(ck, 0, 6), place[0:768, 0:256]),
+                nn(gathered(ck, 5, 7), place[640:896, 256:QLANE]),
+            ],
+            axis=1,
+        )
+        block = block * LOG2E
         for h in range(HEADS):
             table[h, 49 * ck : 49 * ck + 49, :] = block[56 * h : 56 * h + 49, :]
     for h in range(HEADS):
@@ -200,14 +217,16 @@
         lhs = jnp.concatenate(
             [total[h, 49 * ck : 49 * ck + 56, :] for h in range(HEADS)], axis=0
         ).astype(BF16)
-        for cq in range(7):
-            dc = cq - ck + 6
-            tiles[336 * dc : 336 * dc + 336, :] += nt(lhs, place[128 * cq : 128 * cq + 128, :])
-    cube = jnp.zeros((80, 176), F32)
-    for k in range(49):
-        cube += nt(
-            tiles[pl.ds(k, 80, stride=56), :].astype(BF16), spread[:, 128 * k : 128 * k + 128]
-        )
+        for cq, start, end in ((0, 0, 128), (2, 0, 256), (4, 128, 384), (6, 256, 384)):
+            some = min(2, 7 - cq)
+            block = nt(lhs[:, start:end], place[128 * cq : 128 * cq + 128 * some, start:end])
+            for i in range(some):
+                dc = cq + i - ck + 6
+                tiles[336 * dc : 336 * dc + 336, :] += block[:, 128 * i : 128 * i + 128]
+    lhs = jnp.concatenate(
+        [tiles[pl.ds(k, 80, stride=56), :].astype(BF16) for k in range(49)], axis=1
+    )
+    cube = nt(lhs, spread[...])
     wide = jnp.concatenate([cube, jnp.zeros((80, 80), F32)], axis=1)
     wide = jnp.concatenate([wide, jnp.zeros((48, 256), F32)], axis=0)
     mixed = wide.T[:176, :]
@@ -240,7 +259,7 @@
     tail = jnp.where(lane < 2, roll(rows[:9], 2), roll(rows[1:10], 2))
     turned = jnp.concatenate([tail, jnp.zeros((119, 128), F32)], axis=0).T
     for o in range(9):
-        W["cols"][128 * o : 128 * o + 128, :] = jnp.broadcast_to(turned[:, o : o + 1], (128, 128))
+        W.cols[128 * o : 128 * o + 128, :] = jnp.broadcast_to(turned[:, o : o + 1], (128, 128))
 
     def into(j, step, p, value):
         wide[p, pl.ds(j, value.shape[0], stride=step), :] = value
@@ -253,30 +272,30 @@
     finish(0, tail_vector(tail, V_BQ, C))
     finish(1, jnp.zeros((1, 128), F32))
     finish(2, tail_vector(tail, V_BV, C))
-    W["q_n"][...] = wide[0, 0:96, :].astype(BF16)
+    W.q_n[...] = wide[0, 0:96, :].astype(BF16)
     for p in range(1, 3):
-        W["kv_n"][:, 128 * p - 128 : 128 * p] = wide[p, 0:96, :].astype(BF16)
+        W.kv_n[:, 128 * p - 128 : 128 * p] = wide[p, 0:96, :].astype(BF16)
     for p in range(3):
-        W["qkv_t"][96 * p : 96 * p + 96, :] = wide[p, 0:128, :].T[:96].astype(BF16)
+        W.qkv_t[96 * p : 96 * p + 96, :] = wide[p, 0:128, :].T[:96].astype(BF16)
 
     read_matrix(flat, ROW_PROJ, C, C, into)
     finish(0, tail_vector(tail, V_BPROJ, C))
-    W["proj_n"][...] = wide[0, 0:96, :].astype(BF16)
-    W["proj_t"][...] = wide[0, 0:128, :].T[:96].astype(BF16)
+    W.proj_n[...] = wide[0, 0:96, :].astype(BF16)
+    W.proj_t[...] = wide[0, 0:128, :].T[:96].astype(BF16)
 
     read_matrix(flat, ROW_ONE, C, HID, into)
     for p in range(3):
         finish(p, tail_vector(tail, V_BHID + 128 * p, 128))
-        W["one_n"][:, 128 * p : 128 * p + 128] = wide[p, 0:96, :].astype(BF16)
-        W["one_t"][128 * p : 128 * p + 128, :] = wide[p, 0:128, :].T.astype(BF16)
+        W.one_n[:, 128 * p : 128 * p + 128] = wide[p, 0:96, :].astype(BF16)
+        W.one_t[128 * p : 128 * p + 128, :] = wide[p, 0:128, :].T.astype(BF16)
 
     read_matrix(flat, ROW_TWO, HID, C, into)
-    W["two_n"][...] = wide[0].astype(BF16)
+    W.two_n[...] = wide[0].astype(BF16)
     for p in range(3):
-        W["two_t"][:, 128 * p : 128 * p + 128] = wide[0, 128 * p : 128 * p + 128, :].T[:96].astype(
+        W.two_t[:, 128 * p : 128 * p + 128] = wide[0, 128 * p : 128 * p + 128, :].T[:96].astype(
             BF16
         )
-    build_table(flat, spread, place, tiles, W["table"])
+    build_table(flat, spread, place, tiles, W.table)
 
 
 WEIGHT_SHAPES = dict(
@@ -324,7 +343,7 @@
 
 
 def column(W, start, rows=96):
-    part = W["cols"][start : start + rows, :]
+    part = W.cols[start : start + rows, :]
     return jnp.concatenate([part, part, part], axis=1)
 
 
@@ -357,42 +376,52 @@
 
 def window_forward(x, W, S, s, marks, barred):
     hat, scale = standardize(x)
-    S["hat"][s] = hat
-    S["scale"][s, 0:1] = scale
+    S.hat[s] = hat
+    S.scale[s, 0:1] = scale
     normed = extended((hat * column(W, V_GAIN1) + column(W, V_BIAS1)).astype(BF16))
-    S["normed"][s] = normed
-    qkv = nn(W["qkv_t"][...], normed).astype(BF16)
-    S["qkv"][s] = qkv
+    S.normed[s] = normed
+    qkv = nn(W.qkv_t[...], normed).astype(BF16)
+    S.qkv[s] = qkv
     queries = scaled_queries(qkv)
     keys = jnp.concatenate([qkv[96:192], marks[0:32, :]], axis=0).T[:KROW]
     ones = jnp.ones((16, KROW), BF16)
+
+    def pair_scores(p):
+        sides = [at_head(h, queries[16 * h : 16 * h + 16], barred) for h in (2 * p, 2 * p + 1)]
+        return nn(keys, jnp.concatenate(sides, axis=1))
+
     parts = []
+    coming = pair_scores(0)
     for h in range(HEADS):
-        scores = nn(keys, at_head(h, queries[16 * h : 16 * h + 16], barred)) + W["table"][h]
+        if h % 2 == 0:
+            pair = coming
+            if h + 2 < HEADS:
+                coming = pair_scores(h // 2 + 1)
+        scores = pair[:, QLANE * (h % 2) : QLANE * (h % 2) + QLANE] + W.table[h]
         highest = jnp.max(scores, axis=0, keepdims=True)
         probs = jnp.exp2(scores - highest).astype(BF16)
-        S["probs"][s, h] = probs
+        S.probs[s, h] = probs
         values = jnp.concatenate([qkv[192 + 16 * h : 208 + 16 * h, :KROW], ones], axis=0)
         mixed = nn(values, probs)
         inverse = 1.0 / mixed[16:17]
-        S["inverse"][s, h : h + 1] = inverse
+        S.inverse[s, h : h + 1] = inverse
         parts.append((mixed[:16] * inverse).astype(BF16))
     attended = extended(jnp.concatenate(parts, axis=0))
-    S["attended"][s] = attended
-    branch = nn(W["proj_t"][...], attended).astype(BF16)
+    S.attended[s] = attended
+    branch = nn(W.proj_t[...], attended).astype(BF16)
     middle = x + branch.astype(F32)
     hat, scale = standardize(middle)
-    S["hat_two"][s] = hat
-    S["scale_two"][s, 0:1] = scale
+    S.hat_two[s] = hat
+    S.scale_two[s, 0:1] = scale
     normed_two = extended((hat * column(W, V_GAIN2) + column(W, V_BIAS2)).astype(BF16))
-    S["normed_two"][s] = normed_two
-    hidden = nn(W["one_t"][...], normed_two)
+    S.normed_two[s] = normed_two
+    hidden = nn(W.one_t[...], normed_two)
     share = 0.5 + 0.5 * lax.erf(hidden * (0.5**0.5))
     active = (hidden * share).astype(BF16)
-    S["active"][s] = active
+    S.active[s] = active
     slope = share + hidden * jnp.exp2(hidden * hidden * (-0.5 * LOG2E)) * 0.3989422804014327
-    S["slope"][s] = slope.astype(BF16)
-    return middle + nn(W["two_t"][...], active) + column(W, V_BOUT)
+    S.slope[s] = slope.astype(BF16)
+    return middle + nn(W.two_t[...], active) + column(W, V_BOUT)
 
 
 def fold(x):
@@ -408,96 +437,109 @@
 
 def window_backward(grad, W, S, s, G, marks, barred):
     result = extended(grad.astype(BF16))
-    active = S["active"][s]
-    G["two"][...] += nt(jnp.concatenate([active, jnp.ones((16, QLANE), BF16)], axis=0), result)
-    hidden = (nn(W["two_n"][...], result) * S["slope"][s].astype(F32)).astype(BF16)
-    G["one"][...] += nt(S["normed_two"][s, 0:112], hidden)
-    d_normed = nn(W["one_n"][...], hidden)
-    hat = S["hat_two"][s]
-    G["gain2"][...] += fold(d_normed * hat)
-    G["bias2"][...] += fold(d_normed)
-    d_middle = grad + norm_backward(d_normed, hat, S["scale_two"][s, 0:1], column(W, V_GAIN2))
+    active = S.active[s]
+    G.two[...] += nt(jnp.concatenate([active, jnp.ones((16, QLANE), BF16)], axis=0), result)
+    hidden = (nn(W.two_n[...], result) * S.slope[s].astype(F32)).astype(BF16)
+    G.one[...] += nt(S.normed_two[s, 0:112], hidden)
+    d_normed = nn(W.one_n[...], hidden)
+    hat = S.hat_two[s]
+    G.gain2[...] += fold(d_normed * hat)
+    G.bias2[...] += fold(d_normed)
+    d_middle = grad + norm_backward(d_normed, hat, S.scale_two[s, 0:1], column(W, V_GAIN2))
     d_branch = extended(d_middle.astype(BF16))
-    attended = S["attended"][s]
-    G["proj"][...] += nt(attended[0:112], d_branch)
-    d_attended = nn(W["proj_n"][...], d_branch).astype(BF16).astype(F32)
+    attended = S.attended[s]
+    G.proj[...] += nt(attended[0:112], d_branch)
+    d_attended = nn(W.proj_n[...], d_branch).astype(BF16).astype(F32)
     product = d_attended * attended[0:96].astype(F32)
-    qkv = S["qkv"][s]
+    qkv = S.qkv[s]
     queries = scaled_queries(qkv)
     values = extended(qkv[192:288]).T[:KROW]
-    d_keys = jnp.zeros((KROW, 128), F32)
-    d_values = jnp.zeros((KROW, 128), F32)
+    d_both = jnp.zeros((KROW, 256), F32)
+    none = jnp.zeros((32, QLANE), BF16)
+    blank = jnp.zeros((128, QLANE), BF16)
+    row = iota((32, QLANE), 0)
     parts = []
-    for h in range(HEADS):
-        inverse = S["inverse"][s, h : h + 1]
+
+    def head_gradient(h):
+        inverse = S.inverse[s, h : h + 1]
         inner = jnp.sum(product[16 * h : 16 * h + 16], axis=0, keepdims=True) * inverse
         high = inner.astype(BF16)
         low = (inner - high.astype(F32)).astype(BF16)
-        row = iota((32, QLANE), 0)
         less = jnp.where(row == 0, -high.astype(F32), jnp.where(row == 1, -low.astype(F32), 0.0))
-        d_out = at_head(
-            h, (d_attended[16 * h : 16 * h + 16] * inverse).astype(BF16), less.astype(BF16)
-        )
-        probs = S["probs"][s, h]
-        d_scores = probs * nn(values, d_out).astype(BF16)
-        G["total"][h] += d_scores.astype(F32)
-        d_values += nt(probs, d_out)
-        d_keys += nt(d_scores, at_head(h, queries[16 * h : 16 * h + 16], jnp.zeros_like(barred)))
-        parts.append(nn(qkv[96 + 16 * h : 112 + 16 * h, :KROW], d_scores))
+        rows = (d_attended[16 * h : 16 * h + 16] * inverse).astype(BF16)
+        return at_head(h, rows, less.astype(BF16))
+
+    for p in range(HEADS // 2):
+        d_outs = [head_gradient(h) for h in (2 * p, 2 * p + 1)]
+        d_pair = nn(values, jnp.concatenate(d_outs, axis=1)).astype(BF16)
+        for h in (2 * p, 2 * p + 1):
+            probs = S.probs[s, h]
+            d_scores = probs * d_pair[:, QLANE * (h % 2) : QLANE * (h % 2) + QLANE]
+            G.total[h] += d_scores.astype(F32)
+            sides = jnp.concatenate(
+                [
+                    jnp.concatenate(
+                        [at_head(h, queries[16 * h : 16 * h + 16], none), blank], axis=0
+                    ),
+                    jnp.concatenate([blank, d_outs[h % 2]], axis=0),
+                ],
+                axis=1,
+            )
+            d_both += nt(jnp.concatenate([d_scores, probs], axis=1), sides)
+            parts.append(nn(qkv[96 + 16 * h : 112 + 16 * h, :KROW], d_scores))
     d_queries = (jnp.concatenate(parts, axis=0) * HEAD**-0.5).astype(BF16)
-    live = iota((KROW, 128), 1) < 96
-    d_pair = jnp.concatenate(
-        [jnp.where(live, d_keys * LN2, 0.0), jnp.where(live, d_values, 0.0)], axis=1
-    ).astype(BF16)
-    normed = S["normed"][s, 0:112]
-    G["q"][:, 0:96] += nt(normed, d_queries)
+    lane = iota((KROW, 256), 1)
+    factor = jnp.where(lane < 96, LN2, jnp.where((lane >= 128) & (lane < 224), 1.0, 0.0))
+    d_pair = jnp.where(factor > 0, d_both * factor, 0.0).astype(BF16)
+    normed = S.normed[s, 0:112]
+    G.q[:, 0:96] += nt(normed, d_queries)
     both = nn(normed[:, :KROW], d_pair)
     for p in range(2):
-        G["kv"][p] += both[:, 128 * p : 128 * p + 128]
+        G.kv[p] += both[:, 128 * p : 128 * p + 128]
     d_pair = jnp.concatenate([d_pair, jnp.zeros((QLANE - KROW, 256), BF16)], axis=0)
-    d_normed = nn(W["q_n"][:, 0:96], d_queries) + nt(W["kv_n"][...], d_pair)
-    hat = S["hat"][s]
-    G["gain1"][...] += fold(d_normed * hat)
-    G["bias1"][...] += fold(d_normed)
-    return d_middle + norm_backward(d_normed, hat, S["scale"][s, 0:1], column(W, V_GAIN1))
+    d_normed = nn(W.q_n[:, 0:96], d_queries) + nt(W.kv_n[...], d_pair)
+    hat = S.hat[s]
+    G.gain1[...] += fold(d_normed * hat)
+    G.bias1[...] += fold(d_normed)
+    return d_middle + norm_backward(d_normed, hat, S.scale[s, 0:1], column(W, V_GAIN1))
 
 
 def finish_gradients(G, flat, wide, spread, place, tiles):
     def qkv_rows(j, step, p):
         if p == 0:
-            return G["q"][pl.ds(j, 24, stride=4), :]
-        return G["kv"][p - 1, pl.ds(j, 24, stride=4), :]
+            return G.q[pl.ds(j, 24, stride=4), :]
+        return G.kv[p - 1, pl.ds(j, 24, stride=4), :]
 
     write_matrix(flat, 0, C, 3 * C, qkv_rows)
-    write_matrix(flat, ROW_PROJ, C, C, lambda j, step, p: G["proj"][pl.ds(j, 24, stride=4), :])
+    write_matrix(flat, ROW_PROJ, C, C, lambda j, step, p: G.proj[pl.ds(j, 24, stride=4), :])
     write_matrix(
-        flat, ROW_ONE, C, HID, lambda j, step, p: G["one"][0:96, 128 * p : 128 * p + 128]
+        flat, ROW_ONE, C, HID, lambda j, step, p: G.one[0:96, 128 * p : 128 * p + 128]
     )
-    write_matrix(flat, ROW_TWO, HID, C, lambda j, step, p: G["two"][pl.ds(j, 96, stride=4), :])
+    write_matrix(flat, ROW_TWO, HID, C, lambda j, step, p: G.two[pl.ds(j, 96, stride=4), :])
     lane = iota((96, 128), 1)
     columns = jnp.zeros((96, 128), F32)
-    for at, name in enumerate(["gain1", "bias1", "gain2", "bias2"]):
-        columns = jnp.where(lane == at, jnp.sum(G[name][...], axis=1, keepdims=True), columns)
+    for at, ref in enumerate([G.gain1, G.bias1, G.gain2, G.bias2]):
+        columns = jnp.where(lane == at, jnp.sum(ref[...], axis=1, keepdims=True), columns)
     turned = jnp.concatenate([columns, jnp.zeros((32, 128), F32)], axis=0).T
     sources = [
         (turned[0:1], 3),
         (turned[1:2], 3),
-        (G["q"][96:97, :], 3),
-        (G["kv"][1, 96:97, :], 3),
-        (G["proj"][96:97, :], 3),
+        (G.q[96:97, :], 3),
+        (G.kv[1, 96:97, :], 3),
+        (G.proj[96:97, :], 3),
         (turned[2:3], 3),
         (turned[3:4], 3),
-        (G["one"][96:97, 0:128], 4),
-        (G["one"][96:97, 128:256], 4),
-        (G["one"][96:97, 256:384], 4),
-        (G["two"][384:385, :], 3),
+        (G.one[96:97, 0:128], 4),
+        (G.one[96:97, 128:256], 4),
+        (G.one[96:97, 256:384], 4),
+        (G.two[384:385, :], 3),
     ]
     pieces = [source for source, _ in sources]
     units = [(i, g) for i, (_, count) in enumerate(sources) for g in range(count)]
     tail = jnp.concatenate(
         [unit_copy(pieces, units[4 * o : 4 * o + 4]) for o in range(9)], axis=0
     )
-    table = collapse_table(G["total"], spread, place, tiles, flat)
+    table = collapse_table(G.total, spread, place, tiles, flat)
     flat[ROW_TABLE:ROW_TAIL, :] = table[0:102]
     none = jnp.zeros((1, 128), F32)
     moved = roll(jnp.concatenate([none, tail, none], axis=0), 126)
@@ -558,27 +600,27 @@
 
 
 def step_kernel(n_win, n_fsdp, names, *refs):
-    R = dict(zip(names, refs))
-    W = {k: R["w_" + k] for k in WEIGHT_SHAPES}
-    S = {k: R["s_" + k] for k in SAVED_SHAPES}
-    G = {k: R["g_" + k] for k in GRAD_SHAPES}
-    tokens, cotangent, crop = R["tokens"], R["cotangent"], R["crop"]
-    ints, marks = R["ints"], R["marks"]
-    select, place, spread = R["select"], R["place"], R["spread"]
-    flat, wide, tiles = R["flat"], R["wide"], R["tiles"]
-    square, tall = R["square"], R["tall"]
-    send, recv = R["send"], R["recv"]
+    held = dict(zip(names, refs))
+    R = Names(**held)
+    W = Names(**{k: held["w_" + k] for k in WEIGHT_SHAPES})
+    S = Names(**{k: held["s_" + k] for k in SAVED_SHAPES})
+    G = Names(**{k: held["g_" + k] for k in GRAD_SHAPES})
+    tokens, cotangent, crop = R.tokens, R.cotangent, R.crop
+    ints, marks = R.ints, R.marks
+    select, place, spread = R.select, R.place, R.spread
+    flat, wide, tiles = R.flat, R.wide, R.tiles
+    square, tall = R.square, R.tall
+    send, recv = R.send, R.recv
     shard = FLAT // n_fsdp
     extent = tokens.shape[0]
     total = n_win * extent
     me_win, me_fsdp = lax.axis_index("win"), lax.axis_index("fsdp")
     left, right = lax.rem(me_win + n_win - 1, n_win), lax.rem(me_win + 1, n_win)
-    used = [0]
-
-    def remote(src, dst, axis, to):
-        slot = used[0]
-        used[0] += 1
-        copy = pltpu.make_async_remote_copy(
+    slots = {}
+
+    def remote(name, src, dst, axis, to):
+        slot = slots.setdefault(name, len(slots))
+        return pltpu.make_async_remote_copy(
             src_ref=src,
             dst_ref=dst,
             send_sem=send.at[slot],
@@ -586,19 +628,22 @@
             device_id={axis: to},
             device_id_type=pl.DeviceIdType.MESH,
         )
-        copy.start()
-        return copy
-
-    def to_all(axis, me, count, src_of, dst):
+
+    def to_all(name, axis, me, count, src_of, dst):
         copies = []
         for k in range(1, count):
             to = lax.rem(me + k, count)
-            copies.append(remote(src_of(to), dst, axis, to))
+            copies.append(remote((name, k), src_of(to), dst, axis, to))
         return copies
 
-    def neighbour(src, dst, to):
+    def start(copies):
+        for copy in copies:
+            copy.start()
+        return copies
+
+    def neighbour(name, src, dst, to):
         if n_win > 1:
-            return [remote(src, dst, "win", to)]
+            return start([remote(name, src, dst, "win", to)])
         dst[...] = src[...]
         return []
 
@@ -616,20 +661,24 @@
                     device_id={axis: lax.rem(me + k, count)},
                     device_id_type=pl.DeviceIdType.MESH,
                 )
+    gathered = R.gathered
+    for b in range(2):
+        R.own[b] = R.params[b : b + 1, :].reshape(shard, 128)
+        gathered[me_fsdp, b, 0:shard, :] = R.own[b].astype(BF16)
+    R.edge[...] = cotangent[0:SHIFT]
+    build_selectors(ints, select, place, spread)
+    square[...] = jnp.zeros(square.shape, F32)
+    take_grid(lambda x: tokens[x].astype(F32), square, tall, R.grid, False)
+    if n_win * n_fsdp > 1:
         pl.semaphore_wait(barrier, n_win + n_fsdp - 2)
 
-    gathered = R["gathered"]
     weights_in = []
     for b in range(2):
-        gathered[me_fsdp, b, 0:shard, :] = R["params"][pl.ds(b, shard, stride=2), :].astype(BF16)
         mine = gathered.at[me_fsdp, b]
-        weights_in.append(to_all("fsdp", me_fsdp, n_fsdp, lambda to: mine, mine))
-    R["edge"][...] = cotangent[0:SHIFT]
-    halo_in = neighbour(R["edge"], R["edge_in"], left)
-
-    build_selectors(ints, select, place, spread)
-    square[...] = jnp.zeros(square.shape, F32)
-    take_grid(lambda x: tokens[x].astype(F32), square, tall, R["grid"], False)
+        weights_in.append(
+            start(to_all(("weights", b), "fsdp", me_fsdp, n_fsdp, lambda to: mine, mine))
+        )
+    halo_in = neighbour("halo", R.edge, R.edge_in, left)
 
     def spread_weights(b):
         wait(weights_in[b])
@@ -638,18 +687,18 @@
         prepare(flat, W, wide, spread, place, tiles)
 
     spread_weights(0)
-    windows, deltas = R["windows"], R["deltas"]
-    R["bars"][...] = crop_bars(crop, ints, me_win * extent, total)
+    windows, deltas = R.windows, R.deltas
+    R.bars[...] = crop_bars(crop, ints, me_win * extent, total)
 
     def first_forward(w, carry):
-        x = take_window(R["grid"], select, 0, w // 2, lax.rem(w, 2))
-        windows[w] = window_forward(x, W, S, w, marks, R["bars"][...].astype(BF16))
+        x = take_window(R.grid, select, 0, w // 2, lax.rem(w, 2))
+        windows[w] = window_forward(x, W, S, w, marks, R.bars[...].astype(BF16))
         return carry
 
     lax.fori_loop(0, 4, first_forward, 0)
 
-    halo, halo_back = R["halo"], R["halo_back"]
-    kept = R["kept"]
+    halo, halo_back = R.halo, R.halo_back
+    kept = R.kept
     lane = iota((C, 128), 1)
 
     def first_slices(z, value):
@@ -659,39 +708,39 @@
     for i in range(7):
         pair = jnp.where(lane < 64, kept[2 * i], roll(kept[2 * i + 1], 64))
         halo[:, 128 * i : 128 * i + 128] = pair.astype(BF16)
-    slab_in = neighbour(halo, R["halo_in"], left)
+    slab_in = neighbour("slab", halo, R.halo_in, left)
     first_weights = {}
     for k in ("cols", "q_n", "kv_n", "proj_n", "one_n", "two_n"):
-        R["k_" + k][...] = W[k][...]
-        first_weights[k] = R["k_" + k]
+        held["k_" + k][...] = held["w_" + k][...]
+        first_weights[k] = held["k_" + k]
     spread_weights(1)
     wait(halo_in)
 
     def shifted_cotangent(x):
-        return (cotangent[x + SHIFT] if x < 7 - SHIFT else R["edge_in"][x - 7 + SHIFT]).astype(F32)
-
-    take_grid(shifted_cotangent, square, tall, R["grid_two"], True)
+        return (cotangent[x + SHIFT] if x < 7 - SHIFT else R.edge_in[x - 7 + SHIFT]).astype(F32)
+
+    take_grid(shifted_cotangent, square, tall, R.grid_two, True)
     wait(slab_in)
     for z in range(SZ + 3):
-        pair = R["halo_in"][:, 128 * (z % SZ // 2) : 128 * (z % SZ // 2) + 128].astype(F32)
+        pair = R.halo_in[:, 128 * (z % SZ // 2) : 128 * (z % SZ // 2) + 128].astype(F32)
         if z % SZ % 2 == 0:
             pair = roll(pair, 64)
         joined = jnp.where(lane < 64, roll(kept[z % SZ], -48), pair)
-        R["grid"][:, 128 * z : 128 * z + 128] = joined.astype(BF16)
+        R.grid[:, 128 * z : 128 * z + 128] = joined.astype(BF16)
 
     def clear(ref):
         ref[...] = jnp.zeros(ref.shape, ref.dtype)
 
-    for ref in G.values():
+    for ref in vars(G).values():
         clear(ref)
-    R["bars"][...] = crop_bars(crop, ints, me_win * extent + SHIFT, total)
+    R.bars[...] = crop_bars(crop, ints, me_win * extent + SHIFT, total)
 
     def second(w, carry):
         wy, wz = w // 2, lax.rem(w, 2)
-        bars = (R["bars"][...] + shift_bars(marks, wy, wz)).astype(BF16)
-        x = take_window(R["grid"], select, 1, wy, wz)
+        bars = (R.bars[...] + shift_bars(marks, wy, wz)).astype(BF16)
+        x = take_window(R.grid, select, 1, wy, wz)
         windows[w] = window_forward(x, W, S, 4, marks, bars)
-        grad = take_window(R["grid_two"], select, 1, wy, wz)
+        grad = take_window(R.grid_two, select, 1, wy, wz)
         deltas[w] = window_backward(grad, W, S, 4, G, marks, bars)
         return carry
 
@@ -704,7 +753,7 @@
     for i in range(7):
         pair = jnp.where(lane < 64, roll(kept[2 * i], 64), kept[2 * i + 1])
         halo_back[:, 128 * i : 128 * i + 128] = pair.astype(BF16)
-    slab_back = neighbour(halo_back, R["halo_back_in"], right)
+    slab_back = neighbour("slab_back", halo_back, R.halo_back_in, right)
 
     def put_tall(z, value):
         tall[C * z : C * z + C, :] = value
@@ -712,130 +761,151 @@
     give_grid(windows, select, 1, put_tall)
     give_rows(tall, square)
     for x in range(7 - SHIFT):
-        R["block_out"][x + SHIFT] = square[16 * x : 16 * x + 14, 0 : SZ * C].astype(BF16)
+        R.block_out[x + SHIFT] = square[16 * x : 16 * x + 14, 0 : SZ * C].astype(BF16)
     for x in range(SHIFT):
         at = 16 * (x + 7 - SHIFT)
-        R["edge"][x] = square[at : at + 14, 0 : SZ * C].astype(BF16)
-    out_back = neighbour(R["edge"], R["edge_back"], right)
-
-    piece = R["sums"].shape[1] // n_win
-    padded = R["sums"].shape[1]
+        R.edge[x] = square[at : at + 14, 0 : SZ * C].astype(BF16)
+    out_back = neighbour("out_back", R.edge, R.edge_back, right)
+
+    piece = R.sums.shape[1] // n_win
+    padded = R.sums.shape[1]
 
     def scatter(b):
         finish_gradients(G, flat, wide, spread, place, tiles)
         for f in range(n_fsdp):
-            R["outgoing"][b, f, 0:shard, :] = flat[shard * f : shard * f + shard, :].astype(BF16)
+            R.outgoing[b, f, 0:shard, :] = flat[shard * f : shard * f + shard, :].astype(BF16)
             if padded > shard:
-                R["outgoing"][b, f, shard:padded, :] = jnp.zeros((padded - shard, 128), BF16)
+                R.outgoing[b, f, shard:padded, :] = jnp.zeros((padded - shard, 128), BF16)
+        start(fsdp_copies(b))
+
+    def fsdp_copies(b):
         return to_all(
+            ("scatter", b),
             "fsdp",
             me_fsdp,
             n_fsdp,
-            lambda to: R["outgoing"].at[b, to],
-            R["incoming"].at[b, me_fsdp],
+            lambda to: R.outgoing.at[b, to],
+            R.incoming.at[b, me_fsdp],
         )
 
-    def add_fsdp(b, copies):
-        wait(copies)
-        R["incoming"][b, me_fsdp] = R["outgoing"][b, me_fsdp]
-        total_rows = R["incoming"][b, 0].astype(F32)
-        for f in range(1, n_fsdp):
-            total_rows += R["incoming"][b, f].astype(F32)
-        R["sums"][b] = total_rows.astype(BF16)
+    def win_copies(b):
         return to_all(
+            ("sum", b),
             "win",
             me_win,
             n_win,
-            lambda to: R["sums"].at[b, pl.ds(pl.multiple_of(piece * to, 16), piece)],
-            R["parts"].at[b, me_win],
+            lambda to: R.sums.at[b, pl.ds(pl.multiple_of(piece * to, 16), piece)],
+            R.parts.at[b, me_win],
         )
 
-    def add_win(b, copies):
-        wait(copies)
-        own = pl.ds(pl.multiple_of(piece * me_win, 16), piece)
-        R["parts"][b, me_win] = R["sums"][b, own, :]
-        total_rows = R["parts"][b, 0].astype(F32)
+    own = pl.ds(pl.multiple_of(piece * me_win, 16), piece)
+
+    def whole_copies(b):
+        mine = R.whole.at[b, own]
+        return to_all(("whole", b), "win", me_win, n_win, lambda to: mine, mine)
+
+    def add_fsdp(b):
+        wait(fsdp_copies(b))
+        R.incoming[b, me_fsdp] = R.outgoing[b, me_fsdp]
+        total_rows = R.incoming[b, 0].astype(F32)
+        for f in range(1, n_fsdp):
+            total_rows += R.incoming[b, f].astype(F32)
+        R.sums[b] = total_rows.astype(BF16)
+        start(win_copies(b))
+
+    def add_win(b):
+        wait(win_copies(b))
+        R.parts[b, me_win] = R.sums[b, own, :]
+        total_rows = R.parts[b, 0].astype(F32)
         for w in range(1, n_win):
-            total_rows += R["parts"][b, w].astype(F32)
-        R["whole"][b, own, :] = total_rows.astype(BF16)
-        mine = R["whole"].at[b, own]
-        return to_all("win", me_win, n_win, lambda to: mine, mine)
-
-    first_scatter = scatter(1)
+            total_rows += R.parts[b, w].astype(F32)
+        R.whole[b, own, :] = total_rows.astype(BF16)
+        start(whole_copies(b))
+
+    scatter(1)
     wait(slab_back)
     wait(out_back)
-    R["block_out"][0:SHIFT] = R["edge_back"][...]
+    R.block_out[0:SHIFT] = R.edge_back[...]
     for z in range(SZ):
-        pair = R["halo_back_in"][:, 128 * (z // 2) : 128 * (z // 2) + 128].astype(F32)
+        pair = R.halo_back_in[:, 128 * (z // 2) : 128 * (z // 2) + 128].astype(F32)
         if z % 2 == 1:
             pair = roll(pair, 64)
         joined = jnp.where(lane < 48, pair, roll(kept[z], 48))
-        R["grid"][:, 128 * z : 128 * z + 128] = joined.astype(BF16)
-    for ref in G.values():
+        R.grid[:, 128 * z : 128 * z + 128] = joined.astype(BF16)
+    for ref in vars(G).values():
         clear(ref)
-    W0 = {**W, **first_weights}
+    W0 = Names(**{**vars(W), **first_weights})
 
     def first_backward(w, carry):
-        grad = take_window(R["grid"], select, 0, w // 2, lax.rem(w, 2))
-        deltas[w] = window_backward(grad, W0, S, w, G, marks, R["bars"][...].astype(BF16))
+        grad = take_window(R.grid, select, 0, w // 2, lax.rem(w, 2))
+        deltas[w] = window_backward(grad, W0, S, w, G, marks, R.bars[...].astype(BF16))
+
+        @pl.when(w == 1)
+        def _():
+            add_fsdp(1)
+
+        @pl.when(w == 2)
+        def _():
+            add_win(1)
+
         return carry
 
     lax.fori_loop(0, 4, first_backward, 0)
-    second_scatter = scatter(0)
+    scatter(0)
     give_grid(deltas, select, 0, put_tall)
     give_rows(tall, square)
     for x in range(7):
-        R["input_grad"][x] = square[16 * x : 16 * x + 14, 0 : SZ * C].astype(BF16)
-    first_sum = add_fsdp(1, first_scatter)
-    second_sum = add_fsdp(0, second_scatter)
-    first_whole = add_win(1, first_sum)
-    second_whole = add_win(0, second_sum)
-    wait(first_whole)
-    wait(second_whole)
+        R.input_grad[x] = square[16 * x : 16 * x + 14, 0 : SZ * C].astype(BF16)
+    for b in range(2):
+        R.first_held[b] = BETA_FIRST * R.first[b : b + 1, :].reshape(shard, 128)
+        R.second_held[b] = BETA_SECOND * R.second[b : b + 1, :].reshape(shard, 128)
+    wait(whole_copies(1))
+    add_fsdp(0)
+    add_win(0)
+    wait(whole_copies(0))
 
     squares = jnp.zeros((1, 1), F32)
     for b in range(2):
-        rows = R["whole"][b, 0:shard, :].astype(F32)
+        rows = R.whole[b, 0:shard, :].astype(F32)
         squares += jnp.sum(jnp.sum(rows * rows, axis=0, keepdims=True), axis=1, keepdims=True)
-    R["norms"][me_fsdp] = jnp.broadcast_to(squares, (8, 128))
-    mine = R["norms"].at[me_fsdp]
-    wait(to_all("fsdp", me_fsdp, n_fsdp, lambda to: mine, mine))
-    norm = R["norms"][0]
+    R.norms[me_fsdp] = jnp.broadcast_to(squares, (8, 128))
+    mine = R.norms.at[me_fsdp]
+    wait(start(to_all("norm", "fsdp", me_fsdp, n_fsdp, lambda to: mine, mine)))
+    norm = R.norms[0]
     for f in range(1, n_fsdp):
-        norm += R["norms"][f]
+        norm += R.norms[f]
     norm = jnp.sqrt(norm)
-    R["grad_norm"][...] = norm
+    R.grad_norm[0, 0] = norm[0, 0]
     factor = jnp.minimum(1.0, CLIP_LIMIT / (norm + 1e-06))[0:1]
     for b in range(2):
-        at = pl.ds(b, shard, stride=2)
-        clipped = R["whole"][b, 0:shard, :].astype(F32) * factor
-        new_first = BETA_FIRST * R["first"][at, :] + (1.0 - BETA_FIRST) * clipped
-        new_second = BETA_SECOND * R["second"][at, :] + (1.0 - BETA_SECOND) * clipped * clipped
+
+        def store(ref, rows):
+            ref[b : b + 1, :] = rows.reshape(1, shard * 128)
+
+        clipped = R.whole[b, 0:shard, :].astype(F32) * factor
+        new_first = R.first_held[b] + (1.0 - BETA_FIRST) * clipped
+        new_second = R.second_held[b] + (1.0 - BETA_SECOND) * clipped * clipped
         first_hat = new_first / (1.0 - BETA_FIRST**STEP)
         second_hat = new_second / (1.0 - BETA_SECOND**STEP)
-        params = R["params"][at, :]
-        R["new_params"][at, :] = params - LEARN_RATE * (
-            first_hat / (jnp.sqrt(second_hat) + EPS_ADAM) + WEIGHT_DECAY * params
+        params = R.own[b]
+        store(
+            R.new_params,
+            params
+            - LEARN_RATE
+            * (first_hat / (jnp.sqrt(second_hat) + EPS_ADAM) + WEIGHT_DECAY * params),
         )
-        R["new_first"][at, :] = new_first
-        R["new_second"][at, :] = new_second
-
-
-def interleave(rows):
-    return rows.reshape(2, -1, 128).transpose(1, 0, 2).reshape(-1, 128)
-
-
-def separate(rows):
-    return rows.reshape(-1, 2, 128).transpose(1, 0, 2).reshape(2, -1)
+        store(R.new_first, new_first)
+        store(R.new_second, new_second)
+    R.params_copy[...] = R.new_params[...].astype(BF16)
 
 
 def per_device(n_win, n_fsdp, tokens, cotangent, crop_ids, params, first_moment, second_moment):
     ints, marks = constant_tables()
     extent = tokens.shape[1]
-    shard = FLAT // n_fsdp
+    shard = params.shape[1] // 128
     held = round_up(shard, 16)
     padded = round_up(-(-shard // n_win), 16) * n_win
-    rows = jax.ShapeDtypeStruct((2 * shard, 128), F32)
+    rows = jax.ShapeDtypeStruct(params.shape, F32)
     cells = jax.ShapeDtypeStruct((extent, SY, SZ * C), BF16)
     inputs = dict(
         tokens=tokens[0],
@@ -843,21 +913,25 @@
         crop=crop_ids,
         ints=ints,
         marks=marks,
-        params=interleave(params),
-        first=interleave(first_moment),
-        second=interleave(second_moment),
+        params=params,
+        first=first_moment,
+        second=second_moment,
     )
     outputs = dict(
         block_out=cells,
         input_grad=cells,
-        grad_norm=jax.ShapeDtypeStruct((8, 128), F32),
+        grad_norm=jax.ShapeDtypeStruct((1, 1), F32),
         new_params=rows,
         new_first=rows,
         new_second=rows,
+        params_copy=jax.ShapeDtypeStruct(params.shape, BF16),
     )
     V = pltpu.VMEM
     edge = V((SHIFT, SY, SZ * C), BF16)
     scratch = dict(
+        own=V((2, shard, 128), F32),
+        first_held=V((2, shard, 128), F32),
+        second_held=V((2, shard, 128), F32),
         gathered=V((n_fsdp, 2, held, 128), BF16),
         edge=edge,
         edge_in=edge,
@@ -900,13 +974,12 @@
     scratch["recv"] = pltpu.SemaphoreType.DMA((copies,))
     names = [*inputs, *outputs, *scratch]
     vmem = pl.BlockSpec(memory_space=pltpu.VMEM)
+    smem = pl.BlockSpec(memory_space=pltpu.SMEM)
     results = pl.pallas_call(
         functools.partial(step_kernel, n_win, n_fsdp, names),
         out_shape=tuple(outputs.values()),
-        in_specs=[
-            pl.BlockSpec(memory_space=pltpu.SMEM) if k == "crop" else vmem for k in inputs
-        ],
-        out_specs=tuple(vmem for _ in outputs),
+        in_specs=[smem if k == "crop" else vmem for k in inputs],
+        out_specs=tuple(smem if k == "grad_norm" else vmem for k in outputs),
         scratch_shapes=list(scratch.values()),
         compiler_params=pltpu.CompilerParams(
             collective_id=0 if n_win * n_fsdp > 1 else None,
@@ -915,17 +988,8 @@
         ),
         name="layer_step",
     )(*inputs.values())
-    block_out, input_grad, grad_norm, new_params, new_first, new_second = results
-    new_params = separate(new_params)
-    return (
-        block_out[None],
-        input_grad[None],
-        grad_norm[0, 0],
-        new_params,
-        separate(new_first),
-        separate(new_second),
-        new_params.astype(BF16),
-    )
+    block_out, input_grad, grad_norm, *states = results
+    return (block_out[None], input_grad[None], grad_norm[0, 0], *states)
 
 
 def solution(mesh):

time: 126 us -> 112 us (0.89)
  Pallas kernels: 114 us -> 103 us
  local copies, waits for them, and re-layouts: 10.2 us -> 6.19 us
  between operations: 0.7 us -> 2.43 us
    pallas_call x1, Pallas kernels: 114 us -> 103 us  [per_device(): pl.pallas_call(functools.partial(step_kernel, n_win, n_fsdp, names), out_...]
    reshape x7 -> x0, local copies, waits for them, and re-layouts: 3.58 us -> none  [the longest x4 2.03 us: separate(): return rows.reshape(-1, 2, 128).transpose(1, 0, 2).reshape(2, -1)]
    unnamed x14 -> x16, local copies, waits for them, and re-layouts: 2.98 us -> 6.19 us
    transpose x3 -> x0, local copies, waits for them, and re-layouts: 2.47 us -> none  [interleave(): return rows.reshape(2, -1, 128).transpose(1, 0, 2).reshape(-1, 128)]
where the time goes in v3:
time: 112 us
  Pallas kernels  103 us (92%)
  local copies, waits for them, and re-layouts  6.19 us (6%)
  between operations  2.43 us (2%)
    pallas_call x1, Pallas kernels, per_device(): pl.pallas_call(functools.partial(step_kernel, n_win, n_fsdp, names), out_...  103 us
    unnamed x16, local copies, waits for them, and re-layouts  6.19 us

profile of v3, /device:TPU:0, one launch (start us, length us, event | category | flops | bytes accessed | tf_op | source)
XLA Modules:
  0.0 112.0 jit_solution(1131337741052739802)
XLA Ops:
  0.6 103.3 %layer_step.1 = (bf16[7,14,1344]{2,1,0:T(8,128)(2,1)}, bf16[7,14,1344]{2,1,0:T(8,128)(2,1)}, f32[1,1]{1,0:T(1,128)}, f32[2,31232]{1,0:T(2,128)}, f32[2,31232]{1,...) custom-call(bf16[7,14,1344]{2,1,0:T(8,128)(2,1)} %bitcast.5, bf16[7,14,1344]{2,1,0:T(8,128)(2,1)} %bitcast.6, ...), custom_call_target="tpu_custom_call" | custom-call | tf_op jit(solution)/shard_map/layer_step/pallas_call | solution.py:978
  104.0 0.0 copy-start
  104.0 1.8 %copy.22 = bf16[1,7,14,1344]{3,2,1,0:T(8,128)(2,1)} copy(bf16[1,7,14,1344]{3,2,1,0:T(8,128)(2,1)} %bitcast.8) | data formatting | bytes 526848
  105.8 0.0 copy-done
  105.8 0.0 copy-start.3
  105.8 0.7 copy.23
  107.1 0.0 copy-done.3
  107.1 0.0 copy-start.2
  107.1 0.7 copy.25
  107.8 0.3 copy-done.2
  108.2 0.0 copy-start.1
  108.2 0.7 copy.26
  108.8 0.3 copy-done.1
  109.2 0.0 copy-start.4
  109.2 0.7 copy.27
  109.9 0.3 copy-done.4
  110.2 0.6 copy.28
Async XLA Ops:
  104.0 1.8 %copy-start = (bf16[7,14,1344]{2,1,0:T(8,128)(2,1)S(1)}, bf16[7,14,1344]{2,1,0:T(8,128)(2,1)}, u32[]{:S(2)}) copy-start(bf16[7,14,1344]{2,1,0:T(8,128)(2,1)} %get-tuple-element.15) | copy-start | bytes 790276
  105.8 1.4 %copy-start.3 = (f32[2,31232]{1,0:T(2,128)S(1)}, f32[2,31232]{1,0:T(2,128)}, u32[]{:S(2)}) copy-start(f32[2,31232]{1,0:T(2,128)} %get-tuple-element.31) | copy-start | bytes 749572
  107.1 1.0 copy-start.2
  108.2 1.0 copy-start.1
  109.2 1.0 copy-start.4

commit v4 on v3

--- a/solution.py
+++ b/solution.py
@@ -374,10 +374,14 @@
     return (qkv[0:96].astype(F32) * (HEAD**-0.5 * LOG2E)).astype(BF16)
 
 
-def window_forward(x, W, S, s, marks, barred):
+def window_norm(x, S, s):
     hat, scale = standardize(x)
     S.hat[s] = hat
     S.scale[s, 0:1] = scale
+
+
+def window_forward(x, W, S, s, marks, barred):
+    hat = S.hat[s]
     normed = extended((hat * column(W, V_GAIN1) + column(W, V_BIAS1)).astype(BF16))
     S.normed[s] = normed
     qkv = nn(W.qkv_t[...], normed).astype(BF16)
@@ -567,12 +571,11 @@
     return nn(rows, select[s, :, pl.ds(pl.multiple_of(QLANE * wy, 128), QLANE)])
 
 
-def give_grid(windows, select, s, put):
-    for wz in range(2):
-        both = jnp.concatenate([windows[wz], windows[2 + wz]], axis=1).astype(BF16)
-        cells = nt(both, select[s])
-        for r in range(7):
-            put((r + 7 * wz + SHIFT * s) % SZ, cells[:, 128 * r : 128 * r + 128])
+def give_grid(windows, select, s, wz, put):
+    both = jnp.concatenate([windows[2 * wz], windows[2 * wz + 1]], axis=1).astype(BF16)
+    cells = nt(both, select[s])
+    for r in range(7):
+        put((r + 7 * wz + SHIFT * s) % SZ, cells[:, 128 * r : 128 * r + 128])
 
 
 def give_rows(tall, square):
@@ -597,6 +600,19 @@
     row = iota((32, QLANE), 0)
     factor = jnp.where(row < 14, wy, wz).astype(F32) * -BIG
     return marks[32:64, :].astype(F32) * factor
+
+
+STAGED = ("params", "tokens", "cotangent", "first_moment", "second_moment")
+RESULTS = (
+    "block_out", "input_grad", "new_params", "new_first", "new_second", "params_copy",
+)
+
+
+def near_extent(n_win):
+    n_x = 1
+    while 4 * n_x * n_x <= n_win:
+        n_x *= 2
+    return n_x
 
 
 def step_kernel(n_win, n_fsdp, names, *refs):
@@ -616,25 +632,28 @@
     total = n_win * extent
     me_win, me_fsdp = lax.axis_index("win"), lax.axis_index("fsdp")
     left, right = lax.rem(me_win + n_win - 1, n_win), lax.rem(me_win + 1, n_win)
+    n_x = near_extent(n_win)
+    n_z = n_win // n_x
+    me_x, me_z = lax.rem(me_win, n_x), me_win // n_x
+    me_near = me_fsdp * n_x + me_x
+    near = []
+    for k in range(1, n_fsdp * n_x):
+        f, x = lax.rem(me_fsdp + k // n_x, n_fsdp), lax.rem(me_x + k % n_x, n_x)
+        near.append((k, f, x, {"win": me_z * n_x + x, "fsdp": f}))
+    far = [(k, {"win": lax.rem(me_z + k, n_z) * n_x + me_x}) for k in range(1, n_z)]
+    sides = [{"win": left}, {"win": right}] if n_win > 1 else []
     slots = {}
 
-    def remote(name, src, dst, axis, to):
+    def remote(name, src, dst, to):
         slot = slots.setdefault(name, len(slots))
         return pltpu.make_async_remote_copy(
             src_ref=src,
             dst_ref=dst,
             send_sem=send.at[slot],
             recv_sem=recv.at[slot],
-            device_id={axis: to},
+            device_id=to,
             device_id_type=pl.DeviceIdType.MESH,
         )
-
-    def to_all(name, axis, me, count, src_of, dst):
-        copies = []
-        for k in range(1, count):
-            to = lax.rem(me + k, count)
-            copies.append(remote((name, k), src_of(to), dst, axis, to))
-        return copies
 
     def start(copies):
         for copy in copies:
@@ -643,42 +662,74 @@
 
     def neighbour(name, src, dst, to):
         if n_win > 1:
-            return start([remote(name, src, dst, "win", to)])
+            return start([remote(name, src, dst, {"win": to})])
         dst[...] = src[...]
         return []
+
+    def fetch(k):
+        at = STAGED.index(k)
+        return pltpu.make_async_copy(held["hbm_" + k], held[k], R.local.at[at])
+
+    def flush(k):
+        at = len(STAGED) + RESULTS.index(k)
+        return pltpu.make_async_copy(held[k], held["hbm_" + k], R.local.at[at])
 
     def wait(copies):
         for copy in copies:
             copy.wait()
 
+    start([fetch(k) for k in STAGED])
     if n_win * n_fsdp > 1:
         barrier = pltpu.get_barrier_semaphore()
-        for axis, me, count in (("fsdp", me_fsdp, n_fsdp), ("win", me_win, n_win)):
-            for k in range(1, count):
-                pl.semaphore_signal(
-                    barrier,
-                    inc=1,
-                    device_id={axis: lax.rem(me + k, count)},
-                    device_id_type=pl.DeviceIdType.MESH,
-                )
+        peers = [peer[-1] for peer in near + far] + sides
+        for peer in peers:
+            pl.semaphore_signal(
+                barrier, inc=1, device_id=peer, device_id_type=pl.DeviceIdType.MESH
+            )
     gathered = R.gathered
+    fetch("params").wait()
     for b in range(2):
         R.own[b] = R.params[b : b + 1, :].reshape(shard, 128)
         gathered[me_fsdp, b, 0:shard, :] = R.own[b].astype(BF16)
+    fetch("cotangent").wait()
     R.edge[...] = cotangent[0:SHIFT]
     build_selectors(ints, select, place, spread)
     square[...] = jnp.zeros(square.shape, F32)
+    fetch("tokens").wait()
     take_grid(lambda x: tokens[x].astype(F32), square, tall, R.grid, False)
+    windows, deltas = R.windows, R.deltas
+
+    def first_window(w, carry):
+        x = take_window(R.grid, select, 0, lax.rem(w, 2), w // 2)
+        windows[w] = x
+        window_norm(x, S, w)
+        return carry
+
+    lax.fori_loop(0, 4, first_window, 0)
     if n_win * n_fsdp > 1:
-        pl.semaphore_wait(barrier, n_win + n_fsdp - 2)
+        pl.semaphore_wait(barrier, len(peers))
 
     weights_in = []
     for b in range(2):
         mine = gathered.at[me_fsdp, b]
-        weights_in.append(
-            start(to_all(("weights", b), "fsdp", me_fsdp, n_fsdp, lambda to: mine, mine))
-        )
+        copies = []
+        for k in range(1, n_fsdp):
+            to = {"fsdp": lax.rem(me_fsdp + k, n_fsdp)}
+            copies.append(remote(("weights", b, k), mine, mine, to))
+        weights_in.append(start(copies))
     halo_in = neighbour("halo", R.edge, R.edge_in, left)
+
+    def clear(ref):
+        ref[...] = jnp.zeros(ref.shape, ref.dtype)
+
+    for ref in vars(G).values():
+        clear(ref)
+    wait(halo_in)
+
+    def shifted_cotangent(x):
+        return (cotangent[x + SHIFT] if x < 7 - SHIFT else R.edge_in[x - 7 + SHIFT]).astype(F32)
+
+    take_grid(shifted_cotangent, square, tall, R.grid_two, True)
 
     def spread_weights(b):
         wait(weights_in[b])
@@ -687,78 +738,98 @@
         prepare(flat, W, wide, spread, place, tiles)
 
     spread_weights(0)
-    windows, deltas = R.windows, R.deltas
     R.bars[...] = crop_bars(crop, ints, me_win * extent, total)
-
-    def first_forward(w, carry):
-        x = take_window(R.grid, select, 0, w // 2, lax.rem(w, 2))
-        windows[w] = window_forward(x, W, S, w, marks, R.bars[...].astype(BF16))
-        return carry
-
-    lax.fori_loop(0, 4, first_forward, 0)
 
     halo, halo_back = R.halo, R.halo_back
     kept = R.kept
     lane = iota((C, 128), 1)
-
-    def first_slices(z, value):
+    slab_parts = [(0, 3), (3, 7)]
+
+    def slab_copy(wz, name, src, dst, to):
+        start, end = slab_parts[wz]
+        part = pl.ds(start, end - start)
+        return remote((name, wz), src.at[part], dst.at[part], {"win": to})
+
+    def pass_slab(wz, name, src, dst, to):
+        if n_win > 1:
+            slab_copy(wz, name, src, dst, to).start()
+        else:
+            start, end = slab_parts[wz]
+            dst[start:end] = src[start:end]
+
+    def wait_slab(name, src, dst, to):
+        if n_win > 1:
+            wait([slab_copy(wz, name, src, dst, to) for wz in range(2)])
+
+    def put_kept(z, value):
         kept[z] = value
 
-    give_grid(windows, select, 0, first_slices)
-    for i in range(7):
-        pair = jnp.where(lane < 64, kept[2 * i], roll(kept[2 * i + 1], 64))
-        halo[:, 128 * i : 128 * i + 128] = pair.astype(BF16)
-    slab_in = neighbour("slab", halo, R.halo_in, left)
+    def give_slices(wz):
+        give_grid(windows, select, 0, wz, put_kept)
+        for i in range(*slab_parts[wz]):
+            pair = jnp.where(lane < 64, kept[2 * i], roll(kept[2 * i + 1], 64))
+            halo[i] = pair.astype(BF16)
+        pass_slab(wz, "slab", halo, R.halo_in, left)
+
+    def first_forward(w, carry):
+        windows[w] = window_forward(windows[w], W, S, w, marks, R.bars[...].astype(BF16))
+
+        @pl.when(w == 1)
+        def _():
+            give_slices(0)
+
+        return carry
+
+    lax.fori_loop(0, 4, first_forward, 0)
+
+    give_slices(1)
     first_weights = {}
     for k in ("cols", "q_n", "kv_n", "proj_n", "one_n", "two_n"):
         held["k_" + k][...] = held["w_" + k][...]
         first_weights[k] = held["k_" + k]
     spread_weights(1)
-    wait(halo_in)
-
-    def shifted_cotangent(x):
-        return (cotangent[x + SHIFT] if x < 7 - SHIFT else R.edge_in[x - 7 + SHIFT]).astype(F32)
-
-    take_grid(shifted_cotangent, square, tall, R.grid_two, True)
-    wait(slab_in)
+    wait_slab("slab", halo, R.halo_in, left)
     for z in range(SZ + 3):
-        pair = R.halo_in[:, 128 * (z % SZ // 2) : 128 * (z % SZ // 2) + 128].astype(F32)
+        pair = R.halo_in[z % SZ // 2].astype(F32)
         if z % SZ % 2 == 0:
             pair = roll(pair, 64)
         joined = jnp.where(lane < 64, roll(kept[z % SZ], -48), pair)
         R.grid[:, 128 * z : 128 * z + 128] = joined.astype(BF16)
 
-    def clear(ref):
-        ref[...] = jnp.zeros(ref.shape, ref.dtype)
-
-    for ref in vars(G).values():
-        clear(ref)
     R.bars[...] = crop_bars(crop, ints, me_win * extent + SHIFT, total)
 
+    def give_back(wz):
+        give_grid(deltas, select, 1, wz, put_kept)
+        for at in range(*slab_parts[wz]):
+            i = (at + 2) % 7
+            pair = jnp.where(lane < 64, roll(kept[2 * i], 64), kept[2 * i + 1])
+            halo_back[at] = pair.astype(BF16)
+        pass_slab(wz, "slab_back", halo_back, R.halo_back_in, right)
+
     def second(w, carry):
-        wy, wz = w // 2, lax.rem(w, 2)
+        wy, wz = lax.rem(w, 2), w // 2
         bars = (R.bars[...] + shift_bars(marks, wy, wz)).astype(BF16)
         x = take_window(R.grid, select, 1, wy, wz)
+        window_norm(x, S, 4)
         windows[w] = window_forward(x, W, S, 4, marks, bars)
         grad = take_window(R.grid_two, select, 1, wy, wz)
         deltas[w] = window_backward(grad, W, S, 4, G, marks, bars)
+
+        @pl.when(w == 1)
+        def _():
+            give_back(0)
+
         return carry
 
     lax.fori_loop(0, 4, second, 0)
 
-    def put_kept(z, value):
-        kept[z] = value
-
-    give_grid(deltas, select, 1, put_kept)
-    for i in range(7):
-        pair = jnp.where(lane < 64, roll(kept[2 * i], 64), kept[2 * i + 1])
-        halo_back[:, 128 * i : 128 * i + 128] = pair.astype(BF16)
-    slab_back = neighbour("slab_back", halo_back, R.halo_back_in, right)
+    give_back(1)
 
     def put_tall(z, value):
         tall[C * z : C * z + C, :] = value
 
-    give_grid(windows, select, 1, put_tall)
+    for wz in range(2):
+        give_grid(windows, select, 1, wz, put_tall)
     give_rows(tall, square)
     for x in range(7 - SHIFT):
         R.block_out[x + SHIFT] = square[16 * x : 16 * x + 14, 0 : SZ * C].astype(BF16)
@@ -767,8 +838,8 @@
         R.edge[x] = square[at : at + 14, 0 : SZ * C].astype(BF16)
     out_back = neighbour("out_back", R.edge, R.edge_back, right)
 
-    piece = R.sums.shape[1] // n_win
-    padded = R.sums.shape[1]
+    padded = R.outgoing.shape[2]
+    piece = padded // n_x
 
     def scatter(b):
         finish_gradients(G, flat, wide, spread, place, tiles)
@@ -776,58 +847,60 @@
             R.outgoing[b, f, 0:shard, :] = flat[shard * f : shard * f + shard, :].astype(BF16)
             if padded > shard:
                 R.outgoing[b, f, shard:padded, :] = jnp.zeros((padded - shard, 128), BF16)
-        start(fsdp_copies(b))
-
-    def fsdp_copies(b):
-        return to_all(
-            ("scatter", b),
-            "fsdp",
-            me_fsdp,
-            n_fsdp,
-            lambda to: R.outgoing.at[b, to],
-            R.incoming.at[b, me_fsdp],
-        )
-
-    def win_copies(b):
-        return to_all(
-            ("sum", b),
-            "win",
-            me_win,
-            n_win,
-            lambda to: R.sums.at[b, pl.ds(pl.multiple_of(piece * to, 16), piece)],
-            R.parts.at[b, me_win],
-        )
-
-    own = pl.ds(pl.multiple_of(piece * me_win, 16), piece)
+        start(near_copies(b))
+
+    def rows_of(x):
+        return pl.ds(pl.multiple_of(piece * x, 16), piece)
+
+    own = rows_of(me_x)
+
+    def near_copies(b):
+        return [
+            remote(
+                ("near", b, k), R.outgoing.at[b, f, rows_of(x)], R.incoming.at[b, me_near], to
+            )
+            for k, f, x, to in near
+        ]
+
+    def far_copies(b):
+        mine = R.parts.at[b, me_z]
+        return [remote(("far", b, k), mine, mine, to) for k, to in far]
 
     def whole_copies(b):
         mine = R.whole.at[b, own]
-        return to_all(("whole", b), "win", me_win, n_win, lambda to: mine, mine)
-
-    def add_fsdp(b):
-        wait(fsdp_copies(b))
-        R.incoming[b, me_fsdp] = R.outgoing[b, me_fsdp]
+        return [remote(("whole", b, k), mine, mine, to) for k, f, x, to in near if k < n_x]
+
+    def norm_copies():
+        mine = R.norms.at[me_near]
+        return [remote(("norm", k), mine, mine, to) for k, f, x, to in near]
+
+    def add_near(b):
+        wait(near_copies(b))
+        R.incoming[b, me_near] = R.outgoing[b, me_fsdp, own, :]
         total_rows = R.incoming[b, 0].astype(F32)
-        for f in range(1, n_fsdp):
-            total_rows += R.incoming[b, f].astype(F32)
-        R.sums[b] = total_rows.astype(BF16)
-        start(win_copies(b))
-
-    def add_win(b):
-        wait(win_copies(b))
-        R.parts[b, me_win] = R.sums[b, own, :]
+        for i in range(1, n_fsdp * n_x):
+            total_rows += R.incoming[b, i].astype(F32)
+        R.parts[b, me_z] = total_rows.astype(BF16)
+        start(far_copies(b))
+
+    def add_far(b):
+        wait(far_copies(b))
         total_rows = R.parts[b, 0].astype(F32)
-        for w in range(1, n_win):
-            total_rows += R.parts[b, w].astype(F32)
+        for i in range(1, n_z):
+            total_rows += R.parts[b, i].astype(F32)
         R.whole[b, own, :] = total_rows.astype(BF16)
         start(whole_copies(b))
+        squares = jnp.sum((total_rows * total_rows).reshape(piece // 8, 8, 128), axis=0)
+        if b == 1:
+            R.norms[me_near] = squares
+        else:
+            R.norms[me_near] += squares
+            start(norm_copies())
 
     scatter(1)
-    wait(slab_back)
-    wait(out_back)
-    R.block_out[0:SHIFT] = R.edge_back[...]
+    wait_slab("slab_back", halo_back, R.halo_back_in, right)
     for z in range(SZ):
-        pair = R.halo_back_in[:, 128 * (z // 2) : 128 * (z // 2) + 128].astype(F32)
+        pair = R.halo_back_in[(z // 2 + 5) % 7].astype(F32)
         if z % 2 == 1:
             pair = roll(pair, 64)
         joined = jnp.where(lane < 48, pair, roll(kept[z], 48))
@@ -837,66 +910,92 @@
     W0 = Names(**{**vars(W), **first_weights})
 
     def first_backward(w, carry):
-        grad = take_window(R.grid, select, 0, w // 2, lax.rem(w, 2))
+        grad = take_window(R.grid, select, 0, lax.rem(w, 2), w // 2)
         deltas[w] = window_backward(grad, W0, S, w, G, marks, R.bars[...].astype(BF16))
 
         @pl.when(w == 1)
         def _():
-            add_fsdp(1)
+            add_near(1)
 
         @pl.when(w == 2)
         def _():
-            add_win(1)
+            add_far(1)
 
         return carry
 
     lax.fori_loop(0, 4, first_backward, 0)
     scatter(0)
-    give_grid(deltas, select, 0, put_tall)
+    for wz in range(2):
+        give_grid(deltas, select, 0, wz, put_tall)
     give_rows(tall, square)
     for x in range(7):
         R.input_grad[x] = square[16 * x : 16 * x + 14, 0 : SZ * C].astype(BF16)
+    flush("input_grad").start()
+    wait(out_back)
+    R.block_out[0:SHIFT] = R.edge_back[...]
+    flush("block_out").start()
+    add_near(0)
+    fetch("first_moment").wait()
+    fetch("second_moment").wait()
     for b in range(2):
-        R.first_held[b] = BETA_FIRST * R.first[b : b + 1, :].reshape(shard, 128)
-        R.second_held[b] = BETA_SECOND * R.second[b : b + 1, :].reshape(shard, 128)
+        R.first_held[b] = BETA_FIRST * R.first_moment[b : b + 1, :].reshape(shard, 128)
+        R.second_held[b] = BETA_SECOND * R.second_moment[b : b + 1, :].reshape(shard, 128)
     wait(whole_copies(1))
-    add_fsdp(0)
-    add_win(0)
+    add_far(0)
     wait(whole_copies(0))
-
-    squares = jnp.zeros((1, 1), F32)
-    for b in range(2):
-        rows = R.whole[b, 0:shard, :].astype(F32)
-        squares += jnp.sum(jnp.sum(rows * rows, axis=0, keepdims=True), axis=1, keepdims=True)
-    R.norms[me_fsdp] = jnp.broadcast_to(squares, (8, 128))
-    mine = R.norms.at[me_fsdp]
-    wait(start(to_all("norm", "fsdp", me_fsdp, n_fsdp, lambda to: mine, mine)))
+    wait(norm_copies())
     norm = R.norms[0]
-    for f in range(1, n_fsdp):
-        norm += R.norms[f]
-    norm = jnp.sqrt(norm)
+    for i in range(1, n_fsdp * n_x):
+        norm += R.norms[i]
+    norm = jnp.sum(jnp.sum(norm, axis=0, keepdims=True), axis=1, keepdims=True)
+    norm = jnp.broadcast_to(jnp.sqrt(norm), (1, 128))
     R.grad_norm[0, 0] = norm[0, 0]
     factor = jnp.minimum(1.0, CLIP_LIMIT / (norm + 1e-06))[0:1]
+    states = []
     for b in range(2):
-
-        def store(ref, rows):
-            ref[b : b + 1, :] = rows.reshape(1, shard * 128)
-
         clipped = R.whole[b, 0:shard, :].astype(F32) * factor
         new_first = R.first_held[b] + (1.0 - BETA_FIRST) * clipped
         new_second = R.second_held[b] + (1.0 - BETA_SECOND) * clipped * clipped
         first_hat = new_first / (1.0 - BETA_FIRST**STEP)
         second_hat = new_second / (1.0 - BETA_SECOND**STEP)
         params = R.own[b]
-        store(
-            R.new_params,
-            params
-            - LEARN_RATE
-            * (first_hat / (jnp.sqrt(second_hat) + EPS_ADAM) + WEIGHT_DECAY * params),
+        new_params = params - LEARN_RATE * (
+            first_hat / (jnp.sqrt(second_hat) + EPS_ADAM) + WEIGHT_DECAY * params
         )
-        store(R.new_first, new_first)
-        store(R.new_second, new_second)
+        states.append((new_first, new_second, new_params))
+
+    def store(ref, at):
+        for b in range(2):
+            ref[b : b + 1, :] = states[b][at].reshape(1, shard * 128)
+
+    store(R.new_first, 0)
+    flush("new_first").start()
+    store(R.new_second, 1)
+    flush("new_second").start()
+    store(R.new_params, 2)
+    flush("new_params").start()
     R.params_copy[...] = R.new_params[...].astype(BF16)
+    flush("params_copy").start()
+    wait([flush(k) for k in RESULTS])
+
+
+def deliver(*refs):
+    count = (len(refs) - 1) // 3 + 1
+    sources, targets, held, sems = refs[:count], refs[count : 2 * count], refs[2 * count : -1], refs[-1]
+    moves = []
+    for source, target in zip(sources, targets):
+        if source.shape == (1, 1):
+            target[0, 0] = source[0, 0]
+            continue
+        at = len(moves)
+        into = pltpu.make_async_copy(source, held[at], sems.at[0, at])
+        moves.append((into, pltpu.make_async_copy(held[at], target, sems.at[1, at])))
+        into.start()
+    for into, out in moves:
+        into.wait()
+        out.start()
+    for into, out in moves:
+        out.wait()
 
 
 def per_device(n_win, n_fsdp, tokens, cotangent, crop_ids, params, first_moment, second_moment):
@@ -904,7 +1003,10 @@
     extent = tokens.shape[1]
     shard = params.shape[1] // 128
     held = round_up(shard, 16)
-    padded = round_up(-(-shard // n_win), 16) * n_win
+    n_x = near_extent(n_win)
+    n_near, n_z = n_fsdp * n_x, n_win // n_x
+    piece = round_up(-(-shard // n_x), 16)
+    padded = piece * n_x
     rows = jax.ShapeDtypeStruct(params.shape, F32)
     cells = jax.ShapeDtypeStruct((extent, SY, SZ * C), BF16)
     inputs = dict(
@@ -914,8 +1016,8 @@
         ints=ints,
         marks=marks,
         params=params,
-        first=first_moment,
-        second=second_moment,
+        first_moment=first_moment,
+        second_moment=second_moment,
     )
     outputs = dict(
         block_out=cells,
@@ -936,16 +1038,15 @@
         edge=edge,
         edge_in=edge,
         edge_back=edge,
-        halo=V((C, 896), BF16),
-        halo_in=V((C, 896), BF16),
-        halo_back=V((C, 896), BF16),
-        halo_back_in=V((C, 896), BF16),
+        halo=V((7, C, 128), BF16),
+        halo_in=V((7, C, 128), BF16),
+        halo_back=V((7, C, 128), BF16),
+        halo_back_in=V((7, C, 128), BF16),
         outgoing=V((2, n_fsdp, padded, 128), BF16),
-        incoming=V((2, n_fsdp, padded, 128), BF16),
-        sums=V((2, padded, 128), BF16),
-        parts=V((2, n_win, padded // n_win, 128), BF16),
+        incoming=V((2, n_near, piece, 128), BF16),
+        parts=V((2, n_z, piece, 128), BF16),
         whole=V((2, padded, 128), BF16),
-        norms=V((n_fsdp, 8, 128), F32),
+        norms=V((n_near, 8, 128), F32),
         select=V((2, 896, 2 * QLANE), BF16),
         place=V((896, QLANE), BF16),
         spread=V((176, 49 * 128), BF16),
@@ -969,17 +1070,24 @@
         scratch["s_" + k] = V((5, *shape), kind)
     for k, (shape, kind) in GRAD_SHAPES.items():
         scratch["g_" + k] = V(shape, kind)
-    copies = 5 * (n_fsdp - 1) + 4 * (n_win - 1) + 4
+    copies = 2 * (n_fsdp - 1) + 3 * (n_near - 1) + 2 * (n_z - 1) + 2 * (n_x - 1) + 6
+    for k in STAGED:
+        scratch[k] = V(inputs[k].shape, inputs[k].dtype)
+    for k in RESULTS:
+        scratch[k] = V(outputs[k].shape, outputs[k].dtype)
+    scratch["local"] = pltpu.SemaphoreType.DMA((len(STAGED) + len(RESULTS),))
     scratch["send"] = pltpu.SemaphoreType.DMA((copies,))
     scratch["recv"] = pltpu.SemaphoreType.DMA((copies,))
-    names = [*inputs, *outputs, *scratch]
+    outside = {k: "hbm_" + k if k in STAGED + RESULTS else k for k in [*inputs, *outputs]}
+    names = [*outside.values(), *scratch]
     vmem = pl.BlockSpec(memory_space=pltpu.VMEM)
+    hbm = pl.BlockSpec(memory_space=pltpu.HBM)
     smem = pl.BlockSpec(memory_space=pltpu.SMEM)
     results = pl.pallas_call(
         functools.partial(step_kernel, n_win, n_fsdp, names),
         out_shape=tuple(outputs.values()),
-        in_specs=[smem if k == "crop" else vmem for k in inputs],
-        out_specs=tuple(smem if k == "grad_norm" else vmem for k in outputs),
+        in_specs=[smem if k == "crop" else hbm if k in STAGED else vmem for k in inputs],
+        out_specs=tuple(smem if k == "grad_norm" else hbm for k in outputs),
         scratch_shapes=list(scratch.values()),
         compiler_params=pltpu.CompilerParams(
             collective_id=0 if n_win * n_fsdp > 1 else None,
@@ -988,6 +1096,17 @@
         ),
         name="layer_step",
     )(*inputs.values())
+    results = pl.pallas_call(
+        deliver,
+        out_shape=tuple(outputs.values()),
+        in_specs=[smem if k == "grad_norm" else hbm for k in outputs],
+        out_specs=tuple(smem if k == "grad_norm" else hbm for k in outputs),
+        scratch_shapes=[
+            *(V(outputs[k].shape, outputs[k].dtype) for k in RESULTS),
+            pltpu.SemaphoreType.DMA((2, len(RESULTS))),
+        ],
+        name="deliver",
+    )(*results)
     block_out, input_grad, grad_norm, *states = results
     return (block_out[None], input_grad[None], grad_norm[0, 0], *states)
 

time: 112 us -> 98.8 us (0.88)
  local copies, waits for them, and re-layouts: 6.19 us -> 0 us
  Pallas kernels: 103 us -> 97.7 us
  between operations: 2.43 us -> 0.82 us
    pallas_call x1, Pallas kernels: 103 us -> 94.4 us  [per_device(): pl.pallas_call(functools.partial(step_kernel, n_win, n_fsdp, names), out_...]
    unnamed x16 -> x0, local copies, waits for them, and re-layouts: 6.19 us -> none
    pallas_call x0 -> x1, Pallas kernels: none -> 3.33 us  [per_device(): pl.pallas_call(deliver, out_shape=tuple(outputs.values()), in_specs=[smem...]
where the time goes in v4:
time: 98.8 us; the launch traced here: 98.5 us
  Pallas kernels  97.7 us (99%)
    pallas_call x1, Pallas kernels, per_device(): pl.pallas_call(functools.partial(step_kernel, n_win, n_fsdp, names), out_...  94.4 us
    pallas_call x1, Pallas kernels, per_device(): pl.pallas_call(deliver, out_shape=tuple(outputs.values()), in_specs=[smem...  3.33 us

profile of v4, /device:TPU:0, one launch (start us, length us, event | category | flops | bytes accessed | tf_op | source)
XLA Modules:
  0.0 98.5 jit_solution(15605666874817352056)
XLA Ops:
  0.6 94.4 %layer_step.1 = (bf16[7,14,1344]{2,1,0:T(8,128)(2,1)}, bf16[7,14,1344]{2,1,0:T(8,128)(2,1)}, f32[1,1]{1,0:T(1,128)}, f32[2,31232]{1,0:T(2,128)}, f32[2,31232]{1,...) custom-call(bf16[7,14,1344]{2,1,0:T(8,128)(2,1)} %bitcast.5, bf16[7,14,1344]{2,1,0:T(8,128)(2,1)} %bitcast.6, ...), custom_call_target="tpu_custom_call" | custom-call | tf_op jit(solution)/shard_map/layer_step/pallas_call | solution.py:1086
  95.0 3.3 %deliver.1 = (bf16[7,14,1344]{2,1,0:T(8,128)(2,1)}, bf16[7,14,1344]{2,1,0:T(8,128)(2,1)}, f32[1,1]{1,0:T(1,128)}, f32[2,31232]{1,0:T(2,128)}, f32[2,31232]{1,0:T...) custom-call(bf16[7,14,1344]{2,1,0:T(8,128)(2,1)} %get-tuple-element.21.refs_0_, ...), custom_call_target="tpu_custom_call" | custom-call | tf_op jit(solution)/shard_map/deliver/pallas_call | solution.py:1099

commit v5 on v4

--- a/solution.py
+++ b/solution.py
@@ -211,11 +211,13 @@
         table[h, CELLS:KROW, :] = jnp.full((KROW - CELLS, QLANE), -BIG, F32)
 
 
-def collapse_table(total, spread, place, tiles, flat):
+def collapse_table(total, wide_total, spread, place, tiles, flat):
     tiles[...] = jnp.zeros(tiles.shape, F32)
+    for h in range(HEADS):
+        wide_total[h] = total[h].astype(F32)
     for ck in range(7):
         lhs = jnp.concatenate(
-            [total[h, 49 * ck : 49 * ck + 56, :] for h in range(HEADS)], axis=0
+            [wide_total[h, 49 * ck : 49 * ck + 56, :] for h in range(HEADS)], axis=0
         ).astype(BF16)
         for cq, start, end in ((0, 0, 128), (2, 0, 256), (4, 128, 384), (6, 256, 384)):
             some = min(2, 7 - cq)
@@ -338,7 +340,7 @@
     bias1=((96, 128), F32),
     gain2=((96, 128), F32),
     bias2=((96, 128), F32),
-    total=((HEADS, KROW, QLANE), F32),
+    total=((HEADS, KROW, QLANE), BF16),
 )
 
 
@@ -458,11 +460,8 @@
     qkv = S.qkv[s]
     queries = scaled_queries(qkv)
     values = extended(qkv[192:288]).T[:KROW]
-    d_both = jnp.zeros((KROW, 256), F32)
-    none = jnp.zeros((32, QLANE), BF16)
-    blank = jnp.zeros((128, QLANE), BF16)
     row = iota((32, QLANE), 0)
-    parts = []
+    parts, d_keys, d_values = [], [], []
 
     def head_gradient(h):
         inverse = S.inverse[s, h : h + 1]
@@ -471,44 +470,55 @@
         low = (inner - high.astype(F32)).astype(BF16)
         less = jnp.where(row == 0, -high.astype(F32), jnp.where(row == 1, -low.astype(F32), 0.0))
         rows = (d_attended[16 * h : 16 * h + 16] * inverse).astype(BF16)
-        return at_head(h, rows, less.astype(BF16))
-
+        return rows, at_head(h, rows, less.astype(BF16))
+
+    def pair_gradient(p):
+        d_outs = [head_gradient(h) for h in (2 * p, 2 * p + 1)]
+        product = nn(values, jnp.concatenate([d_out for _, d_out in d_outs], axis=1))
+        return d_outs, product.astype(BF16)
+
+    def head_products(h, d_scores, rows, probs):
+        d_keys.append(nt(queries[16 * h : 16 * h + 16], d_scores))
+        d_values.append(nt(rows, probs))
+        parts.append(nn(qkv[96 + 16 * h : 112 + 16 * h, :KROW], d_scores))
+
+    late = []
+    coming = pair_gradient(0)
     for p in range(HEADS // 2):
-        d_outs = [head_gradient(h) for h in (2 * p, 2 * p + 1)]
-        d_pair = nn(values, jnp.concatenate(d_outs, axis=1)).astype(BF16)
+        d_outs, d_pair = coming
+        if p + 1 < HEADS // 2:
+            coming = pair_gradient(p + 1)
         for h in (2 * p, 2 * p + 1):
             probs = S.probs[s, h]
             d_scores = probs * d_pair[:, QLANE * (h % 2) : QLANE * (h % 2) + QLANE]
-            G.total[h] += d_scores.astype(F32)
-            sides = jnp.concatenate(
-                [
-                    jnp.concatenate(
-                        [at_head(h, queries[16 * h : 16 * h + 16], none), blank], axis=0
-                    ),
-                    jnp.concatenate([blank, d_outs[h % 2]], axis=0),
-                ],
-                axis=1,
-            )
-            d_both += nt(jnp.concatenate([d_scores, probs], axis=1), sides)
-            parts.append(nn(qkv[96 + 16 * h : 112 + 16 * h, :KROW], d_scores))
+            G.total[h] += d_scores
+            late.append((h, d_scores, d_outs[h % 2][0], probs))
+            if len(late) > 6:
+                head_products(*late.pop(0))
+    for held in late:
+        head_products(*held)
     d_queries = (jnp.concatenate(parts, axis=0) * HEAD**-0.5).astype(BF16)
-    lane = iota((KROW, 256), 1)
-    factor = jnp.where(lane < 96, LN2, jnp.where((lane >= 128) & (lane < 224), 1.0, 0.0))
-    d_pair = jnp.where(factor > 0, d_both * factor, 0.0).astype(BF16)
+    gap = jnp.zeros((32, QLANE), BF16)
+    tokens_gap = jnp.zeros((96, QLANE - KROW), F32)
+
+    def side(rows, factor):
+        rows = jnp.concatenate(rows, axis=0) * factor
+        return jnp.concatenate([rows, tokens_gap], axis=1).astype(BF16)
+
+    d_pair = jnp.concatenate([side(d_keys, LN2), gap, side(d_values, 1.0), gap], axis=0)
     normed = S.normed[s, 0:112]
     G.q[:, 0:96] += nt(normed, d_queries)
-    both = nn(normed[:, :KROW], d_pair)
+    both = nt(normed, d_pair)
     for p in range(2):
         G.kv[p] += both[:, 128 * p : 128 * p + 128]
-    d_pair = jnp.concatenate([d_pair, jnp.zeros((QLANE - KROW, 256), BF16)], axis=0)
-    d_normed = nn(W.q_n[:, 0:96], d_queries) + nt(W.kv_n[...], d_pair)
+    d_normed = nn(W.q_n[:, 0:96], d_queries) + nn(W.kv_n[...], d_pair)
     hat = S.hat[s]
     G.gain1[...] += fold(d_normed * hat)
     G.bias1[...] += fold(d_normed)
     return d_middle + norm_backward(d_normed, hat, S.scale[s, 0:1], column(W, V_GAIN1))
 
 
-def finish_gradients(G, flat, wide, spread, place, tiles):
+def finish_gradients(G, wide_total, flat, wide, spread, place, tiles):
     def qkv_rows(j, step, p):
         if p == 0:
             return G.q[pl.ds(j, 24, stride=4), :]
@@ -543,7 +553,7 @@
     tail = jnp.concatenate(
         [unit_copy(pieces, units[4 * o : 4 * o + 4]) for o in range(9)], axis=0
     )
-    table = collapse_table(G.total, spread, place, tiles, flat)
+    table = collapse_table(G.total, wide_total, spread, place, tiles, flat)
     flat[ROW_TABLE:ROW_TAIL, :] = table[0:102]
     none = jnp.zeros((1, 128), F32)
     moved = roll(jnp.concatenate([none, tail, none], axis=0), 126)
@@ -746,16 +756,16 @@
     slab_parts = [(0, 3), (3, 7)]
 
     def slab_copy(wz, name, src, dst, to):
-        start, end = slab_parts[wz]
-        part = pl.ds(start, end - start)
+        begin, end = slab_parts[wz]
+        part = pl.ds(begin, end - begin)
         return remote((name, wz), src.at[part], dst.at[part], {"win": to})
 
     def pass_slab(wz, name, src, dst, to):
         if n_win > 1:
-            slab_copy(wz, name, src, dst, to).start()
+            start([slab_copy(wz, name, src, dst, to)])
         else:
-            start, end = slab_parts[wz]
-            dst[start:end] = src[start:end]
+            begin, end = slab_parts[wz]
+            dst[begin:end] = src[begin:end]
 
     def wait_slab(name, src, dst, to):
         if n_win > 1:
@@ -842,7 +852,7 @@
     piece = padded // n_x
 
     def scatter(b):
-        finish_gradients(G, flat, wide, spread, place, tiles)
+        finish_gradients(G, R.wide_total, flat, wide, spread, place, tiles)
         for f in range(n_fsdp):
             R.outgoing[b, f, 0:shard, :] = flat[shard * f : shard * f + shard, :].astype(BF16)
             if padded > shard:
@@ -1061,6 +1071,7 @@
         windows=V((4, C, QLANE), F32),
         deltas=V((4, C, QLANE), F32),
         bars=V((32, QLANE), F32),
+        wide_total=V((HEADS, KROW, QLANE), F32),
     )
     for k, (shape, kind) in WEIGHT_SHAPES.items():
         scratch["w_" + k] = V(shape, kind)

time: 98.8 us -> 95.3 us (0.965)
  Pallas kernels: 97.7 us -> 94.2 us
    pallas_call x1, Pallas kernels: 94.4 us -> 90.9 us  [per_device(): pl.pallas_call(functools.partial(step_kernel, n_win, n_fsdp, names), out_...]
where the time goes in v5:
time: 95.3 us; the launch traced here: 95 us
  Pallas kernels  94.2 us (99%)
    pallas_call x1, Pallas kernels, per_device(): pl.pallas_call(functools.partial(step_kernel, n_win, n_fsdp, names), out_...  90.9 us
    pallas_call x1, Pallas kernels, per_device(): pl.pallas_call(deliver, out_shape=tuple(outputs.values()), in_specs=[smem...  3.33 us

profile of v5, /device:TPU:0, one launch (start us, length us, event | category | flops | bytes accessed | tf_op | source)
XLA Modules:
  0.0 95.0 jit_solution(16561596619211813041)
XLA Ops:
  0.6 90.9 %layer_step.1 = (bf16[7,14,1344]{2,1,0:T(8,128)(2,1)}, bf16[7,14,1344]{2,1,0:T(8,128)(2,1)}, f32[1,1]{1,0:T(1,128)}, f32[2,31232]{1,0:T(2,128)}, f32[2,31232]{1,...) custom-call(bf16[7,14,1344]{2,1,0:T(8,128)(2,1)} %bitcast.5, bf16[7,14,1344]{2,1,0:T(8,128)(2,1)} %bitcast.6, ...), custom_call_target="tpu_custom_call" | custom-call | tf_op jit(solution)/shard_map/layer_step/pallas_call | solution.py:1097
  91.5 3.3 %deliver.1 = (bf16[7,14,1344]{2,1,0:T(8,128)(2,1)}, bf16[7,14,1344]{2,1,0:T(8,128)(2,1)}, f32[1,1]{1,0:T(1,128)}, f32[2,31232]{1,0:T(2,128)}, f32[2,31232]{1,0:T...) custom-call(bf16[7,14,1344]{2,1,0:T(8,128)(2,1)} %get-tuple-element.21.refs_0_, ...), custom_call_target="tpu_custom_call" | custom-call | tf_op jit(solution)/shard_map/deliver/pallas_call | solution.py:1110

commit v6 on v5

--- a/solution.py
+++ b/solution.py
@@ -518,7 +518,7 @@
     return d_middle + norm_backward(d_normed, hat, S.scale[s, 0:1], column(W, V_GAIN1))
 
 
-def finish_gradients(G, wide_total, flat, wide, spread, place, tiles):
+def finish_gradients(G, matrices_done, wide_total, flat, wide, spread, place, tiles):
     def qkv_rows(j, step, p):
         if p == 0:
             return G.q[pl.ds(j, 24, stride=4), :]
@@ -530,6 +530,7 @@
         flat, ROW_ONE, C, HID, lambda j, step, p: G.one[0:96, 128 * p : 128 * p + 128]
     )
     write_matrix(flat, ROW_TWO, HID, C, lambda j, step, p: G.two[pl.ds(j, 96, stride=4), :])
+    matrices_done()
     lane = iota((96, 128), 1)
     columns = jnp.zeros((96, 128), F32)
     for at, ref in enumerate([G.gain1, G.bias1, G.gain2, G.bias2]):
@@ -612,10 +613,10 @@
     return marks[32:64, :].astype(F32) * factor
 
 
-STAGED = ("params", "tokens", "cotangent", "first_moment", "second_moment")
-RESULTS = (
-    "block_out", "input_grad", "new_params", "new_first", "new_second", "params_copy",
-)
+STAGED = ("params", "tokens", "cotangent")
+RESULTS = ("block_out", "input_grad", "grads")
+TAKEN = ("block_out", "input_grad", "grads", "params", "first_moment", "second_moment")
+GIVEN = ("block_out", "input_grad", "new_params", "new_first", "new_second", "params_copy")
 
 
 def near_extent(n_win):
@@ -699,8 +700,8 @@
     gathered = R.gathered
     fetch("params").wait()
     for b in range(2):
-        R.own[b] = R.params[b : b + 1, :].reshape(shard, 128)
-        gathered[me_fsdp, b, 0:shard, :] = R.own[b].astype(BF16)
+        rows = R.params[b : b + 1, :].reshape(shard, 128)
+        gathered[me_fsdp, b, 0:shard, :] = rows.astype(BF16)
     fetch("cotangent").wait()
     R.edge[...] = cotangent[0:SHIFT]
     build_selectors(ints, select, place, spread)
@@ -852,12 +853,20 @@
     piece = padded // n_x
 
     def scatter(b):
-        finish_gradients(G, R.wide_total, flat, wide, spread, place, tiles)
-        for f in range(n_fsdp):
-            R.outgoing[b, f, 0:shard, :] = flat[shard * f : shard * f + shard, :].astype(BF16)
-            if padded > shard:
-                R.outgoing[b, f, shard:padded, :] = jnp.zeros((padded - shard, 128), BF16)
-        start(near_copies(b))
+        early = ROW_TABLE // shard
+
+        def send(first, last):
+            for f in range(first, last):
+                R.outgoing[b, f, 0:shard, :] = flat[shard * f : shard * f + shard, :].astype(BF16)
+                if padded > shard:
+                    R.outgoing[b, f, shard:padded, :] = jnp.zeros((padded - shard, 128), BF16)
+            for (k, f, x, to), copy in zip(near, near_copies(b)):
+                pl.when((f >= first) & (f < last))(copy.start)
+
+        finish_gradients(
+            G, lambda: send(0, early), R.wide_total, flat, wide, spread, place, tiles
+        )
+        send(early, n_fsdp)
 
     def rows_of(x):
         return pl.ds(pl.multiple_of(piece * x, 16), piece)
@@ -877,7 +886,7 @@
         return [remote(("far", b, k), mine, mine, to) for k, to in far]
 
     def whole_copies(b):
-        mine = R.whole.at[b, own]
+        mine = R.grads.at[b, own]
         return [remote(("whole", b, k), mine, mine, to) for k, f, x, to in near if k < n_x]
 
     def norm_copies():
@@ -898,7 +907,7 @@
         total_rows = R.parts[b, 0].astype(F32)
         for i in range(1, n_z):
             total_rows += R.parts[b, i].astype(F32)
-        R.whole[b, own, :] = total_rows.astype(BF16)
+        R.grads[b, own, :] = total_rows.astype(BF16)
         start(whole_copies(b))
         squares = jnp.sum((total_rows * total_rows).reshape(piece // 8, 8, 128), axis=0)
         if b == 1:
@@ -945,11 +954,6 @@
     R.block_out[0:SHIFT] = R.edge_back[...]
     flush("block_out").start()
     add_near(0)
-    fetch("first_moment").wait()
-    fetch("second_moment").wait()
-    for b in range(2):
-        R.first_held[b] = BETA_FIRST * R.first_moment[b : b + 1, :].reshape(shard, 128)
-        R.second_held[b] = BETA_SECOND * R.second_moment[b : b + 1, :].reshape(shard, 128)
     wait(whole_copies(1))
     add_far(0)
     wait(whole_copies(0))
@@ -960,52 +964,57 @@
     norm = jnp.sum(jnp.sum(norm, axis=0, keepdims=True), axis=1, keepdims=True)
     norm = jnp.broadcast_to(jnp.sqrt(norm), (1, 128))
     R.grad_norm[0, 0] = norm[0, 0]
-    factor = jnp.minimum(1.0, CLIP_LIMIT / (norm + 1e-06))[0:1]
+    flush("grads").start()
+    wait([flush(k) for k in RESULTS])
+
+
+def optimizer_kernel(names, *refs):
+    R = Names(**dict(zip(names, refs)))
+    held = vars(R)
+    n = R.params.shape[1]
+
+    def move(i, k, out):
+        ends = (held[k], held["out_" + k]) if out else (held["in_" + k], held[k])
+        return pltpu.make_async_copy(*ends, R.local.at[i])
+
+    coming = {k: move(i, k, False) for i, k in enumerate(TAKEN)}
+    going = {k: move(len(TAKEN) + i, k, True) for i, k in enumerate(GIVEN)}
+    for copy in coming.values():
+        copy.start()
+    for k in ("block_out", "input_grad"):
+        coming[k].wait()
+        going[k].start()
+    for k in TAKEN[2:]:
+        coming[k].wait()
+    R.out_grad_norm[0, 0] = R.grad_norm[0, 0]
+    norm = jnp.full((1, 128), R.grad_norm[0, 0], F32)
+    factor = jnp.minimum(1.0, CLIP_LIMIT / (norm + 1e-06))
     states = []
     for b in range(2):
-        clipped = R.whole[b, 0:shard, :].astype(F32) * factor
-        new_first = R.first_held[b] + (1.0 - BETA_FIRST) * clipped
-        new_second = R.second_held[b] + (1.0 - BETA_SECOND) * clipped * clipped
+
+        def rows(ref):
+            return ref[b : b + 1, :].reshape(n // 128, 128)
+
+        params = rows(R.params)
+        clipped = R.grads[b, 0 : n // 128, :].astype(F32) * factor
+        new_first = BETA_FIRST * rows(R.first_moment) + (1.0 - BETA_FIRST) * clipped
+        new_second = (
+            BETA_SECOND * rows(R.second_moment) + (1.0 - BETA_SECOND) * clipped * clipped
+        )
         first_hat = new_first / (1.0 - BETA_FIRST**STEP)
         second_hat = new_second / (1.0 - BETA_SECOND**STEP)
-        params = R.own[b]
         new_params = params - LEARN_RATE * (
             first_hat / (jnp.sqrt(second_hat) + EPS_ADAM) + WEIGHT_DECAY * params
         )
-        states.append((new_first, new_second, new_params))
-
-    def store(ref, at):
+        states.append((new_params, new_first, new_second))
+    for at, k in enumerate(GIVEN[2:5]):
         for b in range(2):
-            ref[b : b + 1, :] = states[b][at].reshape(1, shard * 128)
-
-    store(R.new_first, 0)
-    flush("new_first").start()
-    store(R.new_second, 1)
-    flush("new_second").start()
-    store(R.new_params, 2)
-    flush("new_params").start()
+            held[k][b : b + 1, :] = states[b][at].reshape(1, n)
+        going[k].start()
     R.params_copy[...] = R.new_params[...].astype(BF16)
-    flush("params_copy").start()
-    wait([flush(k) for k in RESULTS])
-
-
-def deliver(*refs):
-    count = (len(refs) - 1) // 3 + 1
-    sources, targets, held, sems = refs[:count], refs[count : 2 * count], refs[2 * count : -1], refs[-1]
-    moves = []
-    for source, target in zip(sources, targets):
-        if source.shape == (1, 1):
-            target[0, 0] = source[0, 0]
-            continue
-        at = len(moves)
-        into = pltpu.make_async_copy(source, held[at], sems.at[0, at])
-        moves.append((into, pltpu.make_async_copy(held[at], target, sems.at[1, at])))
-        into.start()
-    for into, out in moves:
-        into.wait()
-        out.start()
-    for into, out in moves:
-        out.wait()
+    going["params_copy"].start()
+    for copy in going.values():
+        copy.wait()
 
 
 def per_device(n_win, n_fsdp, tokens, cotangent, crop_ids, params, first_moment, second_moment):
@@ -1026,24 +1035,16 @@
         ints=ints,
         marks=marks,
         params=params,
-        first_moment=first_moment,
-        second_moment=second_moment,
     )
     outputs = dict(
         block_out=cells,
         input_grad=cells,
         grad_norm=jax.ShapeDtypeStruct((1, 1), F32),
-        new_params=rows,
-        new_first=rows,
-        new_second=rows,
-        params_copy=jax.ShapeDtypeStruct(params.shape, BF16),
+        grads=jax.ShapeDtypeStruct((2, padded, 128), BF16),
     )
     V = pltpu.VMEM
     edge = V((SHIFT, SY, SZ * C), BF16)
     scratch = dict(
-        own=V((2, shard, 128), F32),
-        first_held=V((2, shard, 128), F32),
-        second_held=V((2, shard, 128), F32),
         gathered=V((n_fsdp, 2, held, 128), BF16),
         edge=edge,
         edge_in=edge,
@@ -1055,7 +1056,6 @@
         outgoing=V((2, n_fsdp, padded, 128), BF16),
         incoming=V((2, n_near, piece, 128), BF16),
         parts=V((2, n_z, piece, 128), BF16),
-        whole=V((2, padded, 128), BF16),
         norms=V((n_near, 8, 128), F32),
         select=V((2, 896, 2 * QLANE), BF16),
         place=V((896, QLANE), BF16),
@@ -1107,17 +1107,30 @@
         ),
         name="layer_step",
     )(*inputs.values())
+    taken = dict(zip(outputs, results))
+    taken.update(params=params, first_moment=first_moment, second_moment=second_moment)
+    given = dict(
+        block_out=cells,
+        input_grad=cells,
+        grad_norm=outputs["grad_norm"],
+        new_params=rows,
+        new_first=rows,
+        new_second=rows,
+        params_copy=jax.ShapeDtypeStruct(params.shape, BF16),
+    )
+    inside = {k: V(taken[k].shape, taken[k].dtype) for k in TAKEN}
+    inside.update({k: V(given[k].shape, given[k].dtype) for k in GIVEN})
+    inside["local"] = pltpu.SemaphoreType.DMA((len(TAKEN) + len(GIVEN),))
+    names = [k if k == "grad_norm" else "in_" + k for k in taken]
+    names += ["out_" + k for k in given] + [*inside]
     results = pl.pallas_call(
-        deliver,
-        out_shape=tuple(outputs.values()),
-        in_specs=[smem if k == "grad_norm" else hbm for k in outputs],
-        out_specs=tuple(smem if k == "grad_norm" else hbm for k in outputs),
-        scratch_shapes=[
-            *(V(outputs[k].shape, outputs[k].dtype) for k in RESULTS),
-            pltpu.SemaphoreType.DMA((2, len(RESULTS))),
-        ],
-        name="deliver",
-    )(*results)
+        functools.partial(optimizer_kernel, names),
+        out_shape=tuple(given.values()),
+        in_specs=[smem if k == "grad_norm" else hbm for k in taken],
+        out_specs=tuple(smem if k == "grad_norm" else hbm for k in given),
+        scratch_shapes=list(inside.values()),
+        name="optimizer",
+    )(*taken.values())
     block_out, input_grad, grad_norm, *states = results
     return (block_out[None], input_grad[None], grad_norm[0, 0], *states)
 

time: 95.3 us -> 92.2 us (0.967)
  Pallas kernels: 94.2 us -> 91.2 us
    pallas_call x1, Pallas kernels: 90.9 us -> 87.4 us  [per_device(): pl.pallas_call(functools.partial(step_kernel, n_win, n_fsdp, names), out_...]
where the time goes in v6:
time: 92.2 us; the launch traced here: 92 us
  Pallas kernels  91.2 us (99%)
    pallas_call x1, Pallas kernels, per_device(): pl.pallas_call(functools.partial(step_kernel, n_win, n_fsdp, names), out_...  87.4 us
    pallas_call x1, Pallas kernels, per_device(): pl.pallas_call(functools.partial(optimizer_kernel, names), out_shape=tupl...  3.82 us

profile of v6, /device:TPU:0, one launch (start us, length us, event | category | flops | bytes accessed | tf_op | source)
XLA Modules:
  0.0 92.0 jit_solution(7184402784901547663)
XLA Ops:
  0.6 87.4 %layer_step.1 = (bf16[7,14,1344]{2,1,0:T(8,128)(2,1)}, bf16[7,14,1344]{2,1,0:T(8,128)(2,1)}, f32[1,1]{1,0:T(1,128)}, bf16[2,256,128]{2,1,0:T(8,128)(2,1)}) custom-call(bf16[7,14,1344]{2,1,0:T(8,128)(2,1)} %bitcast.5, bf16[7,14,1344]{2,1,0:T(8,128)(2,1)} %bitcast.6, s32[1,56]{1,0:T(1,128)} %refs_2_.1, s32[8,384]{1,0:T(8,128)} %constant.4.clone.refs_3_, ...), custom_call_target="tpu_custom_call" | custom-call | tf_op jit(solution)/shard_map/layer_step/pallas_call | solution.py:1097
  88.0 3.8 %optimizer.1 = (bf16[7,14,1344]{2,1,0:T(8,128)(2,1)}, bf16[7,14,1344]{2,1,0:T(8,128)(2,1)}, f32[1,1]{1,0:T(1,128)}, f32[2,31232]{1,0:T(2,128)}, f32[2,31232]{1,0...) custom-call(bf16[7,14,1344]{2,1,0:T(8,128)(2,1)} %get-tuple-element.18.refs_0_, ...), custom_call_target="tpu_custom_call" | custom-call | tf_op jit(solution)/shard_map/optimizer/pallas_call | solution.py:1126

commit v7 on v6

--- a/solution.py
+++ b/solution.py
@@ -396,7 +396,15 @@
         sides = [at_head(h, queries[16 * h : 16 * h + 16], barred) for h in (2 * p, 2 * p + 1)]
         return nn(keys, jnp.concatenate(sides, axis=1))
 
-    parts = []
+    parts, late = [], []
+
+    def head_values(h, probs):
+        values = jnp.concatenate([qkv[192 + 16 * h : 208 + 16 * h, :KROW], ones], axis=0)
+        mixed = nn(values, probs)
+        inverse = 1.0 / mixed[16:17]
+        S.inverse[s, h : h + 1] = inverse
+        parts.append((mixed[:16] * inverse).astype(BF16))
+
     coming = pair_scores(0)
     for h in range(HEADS):
         if h % 2 == 0:
@@ -407,11 +415,10 @@
         highest = jnp.max(scores, axis=0, keepdims=True)
         probs = jnp.exp2(scores - highest).astype(BF16)
         S.probs[s, h] = probs
-        values = jnp.concatenate([qkv[192 + 16 * h : 208 + 16 * h, :KROW], ones], axis=0)
-        mixed = nn(values, probs)
-        inverse = 1.0 / mixed[16:17]
-        S.inverse[s, h : h + 1] = inverse
-        parts.append((mixed[:16] * inverse).astype(BF16))
+        late.append((h, probs))
+        if len(late) > 1:
+            head_values(*late.pop(0))
+    head_values(*late.pop(0))
     attended = extended(jnp.concatenate(parts, axis=0))
     S.attended[s] = attended
     branch = nn(W.proj_t[...], attended).astype(BF16)
@@ -705,18 +712,6 @@
     fetch("cotangent").wait()
     R.edge[...] = cotangent[0:SHIFT]
     build_selectors(ints, select, place, spread)
-    square[...] = jnp.zeros(square.shape, F32)
-    fetch("tokens").wait()
-    take_grid(lambda x: tokens[x].astype(F32), square, tall, R.grid, False)
-    windows, deltas = R.windows, R.deltas
-
-    def first_window(w, carry):
-        x = take_window(R.grid, select, 0, lax.rem(w, 2), w // 2)
-        windows[w] = x
-        window_norm(x, S, w)
-        return carry
-
-    lax.fori_loop(0, 4, first_window, 0)
     if n_win * n_fsdp > 1:
         pl.semaphore_wait(barrier, len(peers))
 
@@ -729,6 +724,18 @@
             copies.append(remote(("weights", b, k), mine, mine, to))
         weights_in.append(start(copies))
     halo_in = neighbour("halo", R.edge, R.edge_in, left)
+    square[...] = jnp.zeros(square.shape, F32)
+    fetch("tokens").wait()
+    take_grid(lambda x: tokens[x].astype(F32), square, tall, R.grid, False)
+    windows, deltas = R.windows, R.deltas
+
+    def first_window(w, carry):
+        x = take_window(R.grid, select, 0, lax.rem(w, 2), w // 2)
+        windows[w] = x
+        window_norm(x, S, w)
+        return carry
+
+    lax.fori_loop(0, 4, first_window, 0)
 
     def clear(ref):
         ref[...] = jnp.zeros(ref.shape, ref.dtype)

time: 92.2 us -> 91.9 us (level)
  no operation moved by 1% of the time
where the time goes in v7:
time: 91.9 us; the launch traced here: 91.7 us
  Pallas kernels  90.9 us (99%)
    pallas_call x1, Pallas kernels, per_device(): pl.pallas_call(functools.partial(step_kernel, n_win, n_fsdp, names), out_...  87.1 us
    pallas_call x1, Pallas kernels, per_device(): pl.pallas_call(functools.partial(optimizer_kernel, names), out_shape=tupl...  3.82 us

profile of v7, /device:TPU:0, one launch (start us, length us, event | category | flops | bytes accessed | tf_op | source)
XLA Modules:
  0.0 91.7 jit_solution(17583596925979424605)
XLA Ops:
  0.6 87.1 %layer_step.1 = (bf16[7,14,1344]{2,1,0:T(8,128)(2,1)}, bf16[7,14,1344]{2,1,0:T(8,128)(2,1)}, f32[1,1]{1,0:T(1,128)}, bf16[2,256,128]{2,1,0:T(8,128)(2,1)}) custom-call(bf16[7,14,1344]{2,1,0:T(8,128)(2,1)} %bitcast.5, bf16[7,14,1344]{2,1,0:T(8,128)(2,1)} %bitcast.6, s32[1,56]{1,0:T(1,128)} %refs_2_.1, s32[8,384]{1,0:T(8,128)} %constant.4.clone.refs_3_, ...), custom_call_target="tpu_custom_call" | custom-call | tf_op jit(solution)/shard_map/layer_step/pallas_call | solution.py:1104
  87.7 3.8 %optimizer.1 = (bf16[7,14,1344]{2,1,0:T(8,128)(2,1)}, bf16[7,14,1344]{2,1,0:T(8,128)(2,1)}, f32[1,1]{1,0:T(1,128)}, f32[2,31232]{1,0:T(2,128)}, f32[2,31232]{1,0...) custom-call(bf16[7,14,1344]{2,1,0:T(8,128)(2,1)} %get-tuple-element.18.refs_0_, ...), custom_call_target="tpu_custom_call" | custom-call | tf_op jit(solution)/shard_map/optimizer/pallas_call | solution.py:1133
